TPU v7x, 512 devices: a whole 4x4x16 slice. The times are simulated.
512 devices in a mesh: lat: 16 (over x_hi, y, core), lon: 32 (over z, x_lo).
Axes of the slice: x: 4 (x_hi: 2, x_lo: 2; x = x_hi * 2 + x_lo), y: 4, z: 16, core: 2. Of those that a mesh axis runs over, the one named last changes fastest.
Arguments:
- sample_field: float32 [32, 128, 64, 256], P('lat', 'lon'), may hold values from -6 to 6
- langevin_noise: bfloat16 [2, 32, 128, 64, 256], P(None, 'lat', 'lon'), may hold values from -6 to 6
- precision: bfloat16 [32, 128, 9, 64, 64], P('lat', 'lon'), as said below
- pattern: int32 [32, 128, 9], P('lat', 'lon'), may hold values from 0 to 8, as said below
- foot_weight: bfloat16 [32, 128, 64, 4, 64], P('lat', 'lon'), may hold values from -0.375 to 0.375
- foot_columns: int32 [32, 128, 64, 4], P('lat', 'lon'), may hold values from 0 to 8, as said below
- foot_count: int32 [32, 128, 64], P('lat', 'lon'), may hold values from 0 to 4, as said below
- observed: float32 [32, 128, 64], P('lat', 'lon'), may hold values from -6 to 6
- inverse_var: float32 [32, 128, 64], P('lat', 'lon'), may hold values from 0.5 to 4
Outputs:
- new_field: float32 [32, 128, 64, 256], P('lat', 'lon')
Inputs may be any that keep to these rules, and one draw needn't show every extreme that they name: `pattern`: each block's nine slots name the nine offset codes, each once. `foot_columns`: the 4 codes of one footprint are distinct. `foot_count`: in every block the slots with nonzero count come first, and all blocks of one device have the same number of them, between 8 and 64; some device has all 64 in every block. Each block row's precision block in the slot of code 4 has a large diagonal.
All inputs are finite; a program needn't handle non-finite values.
Results may differ from a plain program's by a relative error of at most 0.0023.
Values may be sent and summed in bfloat16 or wider, within the bound.
No kernel may reach another device: no remote copies, remote signals or barrier semaphores. Data moves between devices by JAX's collectives and lax.ppermute only.
A program may use at most 64 MiB of HBM per device.

v0:
```python
import math

import jax
import jax.numpy as jnp
from jax import lax
from jax.sharding import PartitionSpec as P

STEPS = 2


step_size = 0.2


def padded(block, sides, width, periodic):
    for axis, dim in sides:
        count = lax.axis_size(axis)
        forward = [(i, i + 1) for i in range(count - 1)]
        if periodic:
            forward.append((count - 1, 0))
        backward = [(target, source) for source, target in forward]
        low = lax.ppermute(
            lax.slice_in_dim(block, block.shape[dim] - width, None, axis=dim), axis, forward
        )
        high = lax.ppermute(lax.slice_in_dim(block, 0, width, axis=dim), axis, backward)
        block = jnp.concatenate([low, block, high], axis=dim)
    return block


def passed_along(block, axis, distance):
    devices = range(lax.axis_size(axis))
    route = [((i - distance) % len(devices), i) for i in devices]
    return lax.ppermute(block, axis, route)


def shifted_2(shard, axis, by):
    count = lax.axis_size(axis)
    pairs = [(i, i + by) for i in range(count) if 0 <= i + by < count]
    return lax.ppermute(shard, axis, pairs)


def local(
    sample_field,
    langevin_noise,
    precision,
    pattern,
    foot_weight,
    foot_columns,
    foot_count,
    observed,
    inverse_var,
):
    band_height = sample_field.shape[0]
    band_width = sample_field.shape[1]
    block_cells = sample_field.shape[2]
    chains = sample_field.shape[3]
    select = (pattern[..., None] == jnp.arange(9, dtype=jnp.int32)).astype(jnp.bfloat16)
    ordered = jnp.einsum(
        "abko,abkcd->abocd", select, precision, preferred_element_type=jnp.float32
    ).astype(jnp.bfloat16)
    active = jnp.arange(foot_weight.shape[3], dtype=jnp.int32) < foot_count[..., None]
    masked = jnp.where(active[..., None], foot_weight, jnp.zeros_like(foot_weight))
    code_hot = (foot_columns[..., None] == jnp.arange(9, dtype=jnp.int32)).astype(jnp.bfloat16)
    foot_matrix = jnp.einsum(
        "abfjo,abfjc->abfoc", code_hot, masked, preferred_element_type=jnp.float32
    ).astype(jnp.bfloat16)
    target = observed[..., None]
    scale = inverse_var[..., None]
    sample = sample_field
    for update in range(STEPS):
        compact = sample.astype(jnp.bfloat16)
        widened = padded(compact, (("lon", 1),), 1, True)
        window = padded(widened, (("lat", 0),), 1, False)
        shifted = jnp.stack(
            [
                window[
                    offset // 3 : offset // 3 + band_height, offset % 3 : offset % 3 + band_width
                ]
                for offset in range(9)
            ]
        )
        prior_term = jnp.einsum(
            "abocd,oabds->abcs", ordered, shifted, preferred_element_type=jnp.float32
        )
        forward = jnp.einsum(
            "abfoc,oabcs->abfs", foot_matrix, shifted, preferred_element_type=jnp.float32
        )
        residual = (scale * (forward - target)).astype(jnp.bfloat16)
        spread = jnp.einsum(
            "abfoc,abfs->oabcs", foot_matrix, residual, preferred_element_type=jnp.float32
        )
        partial_grid = jnp.zeros(
            (band_height + 2, band_width + 2, block_cells, chains), jnp.float32
        )
        for offset in range(9):
            partial_grid = partial_grid.at[
                offset // 3 : offset // 3 + band_height, offset % 3 : offset % 3 + band_width
            ].add(spread[offset])
        from_east = passed_along(partial_grid[:, 0], "lon", -1)
        from_west = passed_along(partial_grid[:, -1], "lon", 1)
        middle = partial_grid[:, 1:-1]
        middle = middle.at[:, -1].add(from_east).at[:, 0].add(from_west)
        from_north = shifted_2(middle[0], "lat", -1)
        from_south = shifted_2(middle[-1], "lat", 1)
        interior = middle[1:-1]
        interior = interior.at[-1].add(from_north).at[0].add(from_south)
        gradient = prior_term + interior
        sample = (
            sample
            - step_size * gradient
            + math.sqrt(2.0 * step_size) * langevin_noise[update].astype(jnp.float32)
        )
    return sample


def solution(mesh):
    placed = (
        P("lat", "lon", None, None),
        P(None, "lat", "lon", None, None),
        P("lat", "lon", None, None, None),
        P("lat", "lon", None),
        P("lat", "lon", None, None, None),
        P("lat", "lon", None, None),
        P("lat", "lon", None),
        P("lat", "lon", None),
        P("lat", "lon", None),
    )
    return jax.shard_map(
        local, mesh=mesh, in_specs=placed, out_specs=P("lat", "lon", None, None), check_vma=False
    )
```

profile of v0, /device:TPU:4, one launch (start us, length us, event | category | flops | bytes accessed | tf_op | source)
XLA Modules:
  0.0 166.0 jit_solution(1337017106451108804)
XLA Ops:
  0.0 1.2 convert_element_type.29
  1.2 12.0 %collective-permute-start.1 = (bf16[2,1,64,256]{3,2,1,0:T(8,128)(2,1)S(1)}, bf16[2,1,64,256]{3,2,1,0:T(8,128)(2,1)S(1)}, u32[]{:S(2)}, u32[]{:S(2)}) collective-permute-start(bf16[2,1,64,256]{3,2,1,0:T(8,128)(2,1)S(1)} %get-tuple-element.336), channel_id=1, source_target_pairs={{1,0},{2,1},{3,2},{4,3},{5,4},{6,5},{7,6},{8,7},{9,8},{10,9},{11,1... | collective-permute-start | bytes 196616 | tf_op jit(solution)/shard_map/ppermute | solution.py:24
  13.2 1.9 %collective-permute-start = (bf16[2,1,64,256]{3,2,1,0:T(8,128)(2,1)S(1)}, bf16[2,1,64,256]{3,2,1,0:T(8,128)(2,1)S(1)}, u32[]{:S(2)}, u32[]{:S(2)}) collective-permute-start(bf16[2,1,64,256]{3,2,1,0:T(8,128)(2,1)S(1)} %get-tuple-element.335), channel_id=1, source_target_pairs={{0,1},{1,2},{2,3},{3,4},{4,5},{5,6},{6,7},{7,8},{8,9},{9,10},{10,1... | collective-permute-start | bytes 196616 | tf_op jit(solution)/shard_map/ppermute | solution.py:21
  15.2 0.9 copy.42
  16.0 0.8 iota_compare_fusion.2
  16.9 4.6 %convolution_convert_fusion = bf16[2,4,64,9,64]{4,3,2,1,0:T(8,128)(2,1)} fusion(bf16[2,4,64,4,64]{4,3,2,1,0:T(4,128)(2,1)} %param.65, s32[2,4,64,4]{3,2,1,0:T(8,128)S(1)} %copy.42, pred[2,4,64,4]{3,2,1,0:T(8,128)(4,1)S(1)} %iota_compare_fusion.2), kind=kOutput, calls=%fused_computation.9 | convolution fusion | flops 2803712 | bytes 862208 | tf_op jit(solution)/shard_map/abfjo,abfjc->abfoc/dot_general | solution.py:63
  21.4 3.1 %copy.43 = bf16[2,4,64,9,64]{2,4,3,1,0:T(8,128)(2,1)S(1)} copy(bf16[2,4,64,9,64]{4,3,2,1,0:T(8,128)(2,1)} %convolution_convert_fusion) | data formatting | bytes 1179648 | tf_op jit(solution)/shard_map/convert_element_type | solution.py:65
  24.5 0.6 fusion.121
  25.2 4.5 %collective-permute-start.3 = (bf16[1,6,64,256]{3,2,1,0:T(8,128)(2,1)S(1)}, bf16[1,6,64,256]{3,2,1,0:T(8,128)(2,1)S(1)}, u32[]{:S(2)}, u32[]{:S(2)}) collective-permute-start(bf16[1,6,64,256]{3,2,1,0:T(8,128)(2,1)S(1)} %get-tuple-element.331), channel_id=1, source_target_pairs={{32,0},{64,32},{96,64},{128,96},{160,128},{192,160},{224,192},{256... | collective-permute-start | bytes 589832 | tf_op jit(solution)/shard_map/ppermute | solution.py:24
  29.7 1.9 %collective-permute-start.2 = (bf16[1,6,64,256]{3,2,1,0:T(8,128)(2,1)S(1)}, bf16[1,6,64,256]{3,2,1,0:T(8,128)(2,1)S(1)}, u32[]{:S(2)}, u32[]{:S(2)}) collective-permute-start(bf16[1,6,64,256]{3,2,1,0:T(8,128)(2,1)S(1)} %get-tuple-element.332), channel_id=1, source_target_pairs={{0,32},{32,64},{64,96},{96,128},{128,160},{160,192},{192,224},{224... | collective-permute-start | bytes 589832 | tf_op jit(solution)/shard_map/ppermute | solution.py:21
  31.6 0.6 fusion.120
  32.2 0.7 and_reduce_fusion
  33.0 7.3 %collective-permute-done.2 = bf16[1,6,64,256]{3,2,1,0:T(8,128)(2,1)S(1)} collective-permute-done((bf16[1,6,64,256]{3,2,1,0:T(8,128)(2,1)S(1)}, bf16[1,6,64,256]{3,2,1,0:T(8,128)(2,1)S(1)}, u32[]{:S(2)}, u32[]{:S(2)}) %collective-permute-start.2) | collective-permute-done | bytes 196640 | tf_op jit(solution)/shard_map/ppermute | solution.py:21
  40.4 0.8 fusion.106
  41.2 0.8 fusion.105
  41.9 0.7 fusion.104
  42.7 0.7 fusion.103
  43.4 0.8 bitcast_dynamic-update-slice_fusion
  44.2 0.8 fusion.101
  44.9 0.8 fusion.99
  45.7 0.7 fusion.98
  46.4 0.8 fusion.97
  47.2 5.1 %fusion.40 = f32[2,4,256,576]{2,3,1,0} fusion(bf16[2,4,64,576]{2,3,1,0:T(8,128)(2,1)S(1)} %bitcast.299, bf16[2,4,64,9,64]{2,4,3,1,0:T(8,128)(2,1)S(1)} %copy.43, bf16[9,2,4,64,256]{4,3,0,2,1:T(8,128)(2,1)} %fusion.97, f32[2,4,64]{2,1,0:T(4,128)S(1)} %copy-done.6, f32[2,4,64]{2,1,0:T(4,128)S(1)} %copy-done.7), kind=kOutput, calls=%fused_computation.28 | convolution fusion | flops 302383104 | bytes 8261632
  52.2 2.9 %copy.97 = f32[2,4,256,9,64]{2,4,0,1,3:T(8,128)S(1)} copy(f32[2,4,256,9,64]{2,4,3,1,0:T(8,128)} %bitcast.320) | data formatting | bytes 9437184 | tf_op jit(solution)/shard_map/abfoc,abfs->oabcs/dot_general | solution.py:88
  55.4 1.3 fusion.73
  56.7 1.9 %fusion.44 = f32[4,6,64,256]{3,2,0,1:T(8,128)S(1)} fusion(f32[4,6,64,256]{3,2,0,1:T(8,128)S(1)} %fusion.73, s32[]{:T(128)} %bitcast.30, s32[]{:T(128)} %bitcast.31, f32[9,2,4,64,256]{4,3,1,2,0:T(8,128)S(1)} %bitcast.312, pred[]{:T(512)} %and_reduce_fusion), kind=kLoop, calls=%fused_computation.37 | loop fusion | flops 262144 | bytes 1572873 | tf_op jit(solution)/shard_map/scatter-add | solution.py:97
  59.4 6.4 %collective-permute-start.4 = (f32[4,64,256]{2,1,0:T(8,128)S(1)}, f32[4,64,256]{2,1,0:T(8,128)S(1)}, u32[]{:S(2)}, u32[]{:S(2)}) collective-permute-start(f32[4,64,256]{2,1,0:T(8,128)S(1)} %get-tuple-element.320), channel_id=1, source_target_pairs={{1,0},{2,1},{3,2},{4,3},{5,4},{6,5},{7,6},{8,7},{9,8},{10,9},{11,1... | collective-permute-start | bytes 786440 | tf_op jit(solution)/shard_map/ppermute | solution.py:32
  65.8 1.9 %collective-permute-start.5 = (f32[4,64,256]{2,1,0:T(8,128)S(1)}, f32[4,64,256]{2,1,0:T(8,128)S(1)}, u32[]{:S(2)}, u32[]{:S(2)}) collective-permute-start(f32[4,64,256]{2,1,0:T(8,128)S(1)} %get-tuple-element.319), channel_id=1, source_target_pairs={{31,0},{0,1},{1,2},{2,3},{3,4},{4,5},{5,6},{6,7},{7,8},{8,9},{9,10... | collective-permute-start | bytes 786440 | tf_op jit(solution)/shard_map/ppermute | solution.py:32
  67.9 2.7 %collective-permute-done.4 = f32[4,64,256]{2,1,0:T(8,128)S(1)} collective-permute-done((f32[4,64,256]{2,1,0:T(8,128)S(1)}, f32[4,64,256]{2,1,0:T(8,128)S(1)}, u32[]{:S(2)}, u32[]{:S(2)}) %collective-permute-start.4) | collective-permute-done | bytes 262176 | tf_op jit(solution)/shard_map/ppermute | solution.py:32
  70.6 5.6 %collective-permute-done.5 = f32[4,64,256]{2,1,0:T(8,128)S(1)} collective-permute-done((f32[4,64,256]{2,1,0:T(8,128)S(1)}, f32[4,64,256]{2,1,0:T(8,128)S(1)}, u32[]{:S(2)}, u32[]{:S(2)}) %collective-permute-start.5) | collective-permute-done | bytes 262176 | tf_op jit(solution)/shard_map/ppermute | solution.py:32
  76.3 1.9 %collective-permute-start.6 = (f32[4,64,256]{2,1,0:T(8,128)S(1)}, f32[4,64,256]{2,1,0:T(8,128)S(1)}, u32[]{:S(2)}, u32[]{:S(2)}) collective-permute-start(f32[4,64,256]{2,1,0:T(8,128)S(1)} %get-tuple-element.324), channel_id=1, source_target_pairs={{32,0},{64,32},{96,64},{128,96},{160,128},{192,160},{224,192},{256... | collective-permute-start | bytes 786440 | tf_op jit(solution)/shard_map/ppermute | solution.py:38
  78.2 2.4 %collective-permute-start.7 = (f32[4,64,256]{2,1,0:T(8,128)S(1)}, f32[4,64,256]{2,1,0:T(8,128)S(1)}, u32[]{:S(2)}, u32[]{:S(2)}) collective-permute-start(f32[4,64,256]{2,1,0:T(8,128)S(1)} %get-tuple-element.323), channel_id=1, source_target_pairs={{0,32},{32,64},{64,96},{96,128},{128,160},{160,192},{192,224},{224... | collective-permute-start | bytes 786440 | tf_op jit(solution)/shard_map/ppermute | solution.py:38
  80.7 1.0 fusion
  82.1 8.1 %collective-permute-done.7 = f32[4,64,256]{2,1,0:T(8,128)S(1)} collective-permute-done((f32[4,64,256]{2,1,0:T(8,128)S(1)}, f32[4,64,256]{2,1,0:T(8,128)S(1)}, u32[]{:S(2)}, u32[]{:S(2)}) %collective-permute-start.7) | collective-permute-done | bytes 262176 | tf_op jit(solution)/shard_map/ppermute | solution.py:38
  90.3 2.4 %fusion.122 = (bf16[2,4,64,256]{3,2,1,0:T(8,128)(2,1)S(1)}, f32[2,4,64,256]{3,2,1,0:T(8,128)S(1)}) fusion(bf16[2,2,4,64,256]{4,3,2,1,0:T(8,128)(2,1)S(1)} %copy-done.4, f32[2,4,64,256]{3,2,1,0:T(8,128)S(1)} %copy-done.3, f32[2,4,64,256]{3,2,1,0:T(8,128)S(1)} %fusion.92, bf16[9,2,4,64,256]{4,3,0,2,1:T(8,128)(2,1)} %fusion.97, ...), kind=kOutput, calls=%fused_computation.172 | convolution fusion | flops 151912448 | bytes 5046272 | tf_op jit(solution)/shard_map/abocd,oabds->abcs/dot_general | solution.py:81
  92.8 4.5 %collective-permute-start.9 = (bf16[2,1,64,256]{3,2,1,0:T(8,128)(2,1)S(1)}, bf16[2,1,64,256]{3,2,1,0:T(8,128)(2,1)S(1)}, u32[]{:S(2)}, u32[]{:S(2)}) collective-permute-start(bf16[2,1,64,256]{3,2,1,0:T(8,128)(2,1)S(1)} %get-tuple-element.334), channel_id=1, source_target_pairs={{1,0},{2,1},{3,2},{4,3},{5,4},{6,5},{7,6},{8,7},{9,8},{10,9},{11,1... | collective-permute-start | bytes 196616 | tf_op jit(solution)/shard_map/ppermute | solution.py:24
  97.3 1.9 %collective-permute-start.8 = (bf16[2,1,64,256]{3,2,1,0:T(8,128)(2,1)S(1)}, bf16[2,1,64,256]{3,2,1,0:T(8,128)(2,1)S(1)}, u32[]{:S(2)}, u32[]{:S(2)}) collective-permute-start(bf16[2,1,64,256]{3,2,1,0:T(8,128)(2,1)S(1)} %get-tuple-element.333), channel_id=1, source_target_pairs={{0,1},{1,2},{2,3},{3,4},{4,5},{5,6},{6,7},{7,8},{8,9},{9,10},{10,1... | collective-permute-start | bytes 196616 | tf_op jit(solution)/shard_map/ppermute | solution.py:21
  99.2 6.3 %collective-permute-done.8 = bf16[2,1,64,256]{3,2,1,0:T(8,128)(2,1)S(1)} collective-permute-done((bf16[2,1,64,256]{3,2,1,0:T(8,128)(2,1)S(1)}, bf16[2,1,64,256]{3,2,1,0:T(8,128)(2,1)S(1)}, u32[]{:S(2)}, u32[]{:S(2)}) %collective-permute-start.8) | collective-permute-done | bytes 65568 | tf_op jit(solution)/shard_map/ppermute | solution.py:21
  105.6 1.9 %collective-permute-start.11 = (bf16[1,6,64,256]{3,2,1,0:T(8,128)(2,1)S(1)}, bf16[1,6,64,256]{3,2,1,0:T(8,128)(2,1)S(1)}, u32[]{:S(2)}, u32[]{:S(2)}) collective-permute-start(bf16[1,6,64,256]{3,2,1,0:T(8,128)(2,1)S(1)} %get-tuple-element.327), channel_id=1, source_target_pairs={{32,0},{64,32},{96,64},{128,96},{160,128},{192,160},{224,192},{256... | collective-permute-start | bytes 589832 | tf_op jit(solution)/shard_map/ppermute | solution.py:24
  107.6 2.4 %collective-permute-start.10 = (bf16[1,6,64,256]{3,2,1,0:T(8,128)(2,1)S(1)}, bf16[1,6,64,256]{3,2,1,0:T(8,128)(2,1)S(1)}, u32[]{:S(2)}, u32[]{:S(2)}) collective-permute-start(bf16[1,6,64,256]{3,2,1,0:T(8,128)(2,1)S(1)} %get-tuple-element.328), channel_id=1, source_target_pairs={{0,32},{32,64},{64,96},{96,128},{128,160},{160,192},{192,224},{224... | collective-permute-start | bytes 589832 | tf_op jit(solution)/shard_map/ppermute | solution.py:21
  110.0 0.8 collective-permute-done.11
  110.7 7.4 %collective-permute-done.10 = bf16[1,6,64,256]{3,2,1,0:T(8,128)(2,1)S(1)} collective-permute-done((bf16[1,6,64,256]{3,2,1,0:T(8,128)(2,1)S(1)}, bf16[1,6,64,256]{3,2,1,0:T(8,128)(2,1)S(1)}, u32[]{:S(2)}, u32[]{:S(2)}) %collective-permute-start.10) | collective-permute-done | bytes 196640 | tf_op jit(solution)/shard_map/ppermute | solution.py:21
  118.3 0.7 fusion.91
  119.0 0.7 fusion.90
  119.7 0.7 fusion.89
  120.5 0.7 fusion.88
  121.2 0.7 bitcast_dynamic-update-slice_fusion.1
  121.9 0.7 fusion.86
  122.6 0.7 fusion.84
  123.4 0.7 fusion.83
  124.1 0.7 fusion.82
  124.8 5.1 %fusion.42 = f32[2,4,256,576]{2,3,1,0} fusion(bf16[2,4,64,576]{2,3,1,0:T(8,128)(2,1)S(1)} %bitcast.300, bf16[2,4,64,9,64]{2,4,3,1,0:T(8,128)(2,1)S(1)} %copy.43, bf16[9,2,4,64,256]{4,3,2,1,0:T(8,128)(2,1)} %fusion.82, f32[2,4,64]{2,1,0:T(4,128)S(1)} %copy-done.6, f32[2,4,64]{2,1,0:T(4,128)S(1)} %copy-done.7), kind=kOutput, calls=%fused_computation.29 | convolution fusion | flops 302383104 | bytes 8261632
  129.9 2.9 %copy.96 = f32[2,4,256,9,64]{2,4,0,1,3:T(8,128)S(1)} copy(f32[2,4,256,9,64]{2,4,3,1,0:T(8,128)} %bitcast.319) | data formatting | bytes 9437184 | tf_op jit(solution)/shard_map/abfoc,abfs->oabcs/dot_general | solution.py:88
  133.0 1.3 fusion.59
  134.3 1.9 %fusion.45 = f32[4,6,64,256]{3,2,0,1:T(8,128)S(1)} fusion(f32[4,6,64,256]{3,2,0,1:T(8,128)S(1)} %fusion.59, s32[]{:T(128)} %bitcast.30, s32[]{:T(128)} %bitcast.31, f32[9,2,4,64,256]{4,3,1,2,0:T(8,128)S(1)} %bitcast.303, pred[]{:T(512)} %and_reduce_fusion), kind=kLoop, calls=%fused_computation.38 | loop fusion | flops 262144 | bytes 1572873 | tf_op jit(solution)/shard_map/scatter-add | solution.py:97
  137.1 1.9 %collective-permute-start.12 = (f32[4,64,256]{2,1,0:T(8,128)S(1)}, f32[4,64,256]{2,1,0:T(8,128)S(1)}, u32[]{:S(2)}, u32[]{:S(2)}) collective-permute-start(f32[4,64,256]{2,1,0:T(8,128)S(1)} %get-tuple-element.318), channel_id=1, source_target_pairs={{1,0},{2,1},{3,2},{4,3},{5,4},{6,5},{7,6},{8,7},{9,8},{10,9},{11,1... | collective-permute-start | bytes 786440 | tf_op jit(solution)/shard_map/ppermute | solution.py:32
  139.0 3.9 %collective-permute-start.13 = (f32[4,64,256]{2,1,0:T(8,128)S(1)}, f32[4,64,256]{2,1,0:T(8,128)S(1)}, u32[]{:S(2)}, u32[]{:S(2)}) collective-permute-start(f32[4,64,256]{2,1,0:T(8,128)S(1)} %get-tuple-element.317), channel_id=1, source_target_pairs={{31,0},{0,1},{1,2},{2,3},{3,4},{4,5},{5,6},{6,7},{7,8},{8,9},{9,10... | collective-permute-start | bytes 786440 | tf_op jit(solution)/shard_map/ppermute | solution.py:32
  143.1 2.6 %collective-permute-done.12 = f32[4,64,256]{2,1,0:T(8,128)S(1)} collective-permute-done((f32[4,64,256]{2,1,0:T(8,128)S(1)}, f32[4,64,256]{2,1,0:T(8,128)S(1)}, u32[]{:S(2)}, u32[]{:S(2)}) %collective-permute-start.12) | collective-permute-done | bytes 262176 | tf_op jit(solution)/shard_map/ppermute | solution.py:32
  145.8 3.6 %collective-permute-done.13 = f32[4,64,256]{2,1,0:T(8,128)S(1)} collective-permute-done((f32[4,64,256]{2,1,0:T(8,128)S(1)}, f32[4,64,256]{2,1,0:T(8,128)S(1)}, u32[]{:S(2)}, u32[]{:S(2)}) %collective-permute-start.13) | collective-permute-done | bytes 262176 | tf_op jit(solution)/shard_map/ppermute | solution.py:32
  149.5 1.9 %collective-permute-start.14 = (f32[4,64,256]{2,1,0:T(8,128)S(1)}, f32[4,64,256]{2,1,0:T(8,128)S(1)}, u32[]{:S(2)}, u32[]{:S(2)}) collective-permute-start(f32[4,64,256]{2,1,0:T(8,128)S(1)} %get-tuple-element.322), channel_id=1, source_target_pairs={{32,0},{64,32},{96,64},{128,96},{160,128},{192,160},{224,192},{256... | collective-permute-start | bytes 786440 | tf_op jit(solution)/shard_map/ppermute | solution.py:38
  151.4 2.4 %collective-permute-start.15 = (f32[4,64,256]{2,1,0:T(8,128)S(1)}, f32[4,64,256]{2,1,0:T(8,128)S(1)}, u32[]{:S(2)}, u32[]{:S(2)}) collective-permute-start(f32[4,64,256]{2,1,0:T(8,128)S(1)} %get-tuple-element.321), channel_id=1, source_target_pairs={{0,32},{32,64},{64,96},{96,128},{128,160},{160,192},{192,224},{224... | collective-permute-start | bytes 786440 | tf_op jit(solution)/shard_map/ppermute | solution.py:38
  153.9 1.4 collective-permute-done.14
  155.3 7.4 %collective-permute-done.15 = f32[4,64,256]{2,1,0:T(8,128)S(1)} collective-permute-done((f32[4,64,256]{2,1,0:T(8,128)S(1)}, f32[4,64,256]{2,1,0:T(8,128)S(1)}, u32[]{:S(2)}, u32[]{:S(2)}) %collective-permute-start.15) | collective-permute-done | bytes 262176 | tf_op jit(solution)/shard_map/ppermute | solution.py:38
  162.8 3.2 %fusion.29 = f32[2,4,64,256]{3,2,1,0:T(8,128)} fusion(f32[2,4,64,256]{3,2,1,0:T(8,128)S(1)} %get-tuple-element.342, f32[2,4,64,256]{3,2,1,0:T(8,128)S(1)} %fusion.77, bf16[9,2,4,64,256]{4,3,2,1,0:T(8,128)(2,1)} %fusion.82, bf16[2,2,4,64,256]{4,3,2,1,0:T(8,128)(2,1)S(1)} %copy-done.5, bf16[2,4,9,64,64]{4,2,3,1,0:T(8,128)(2,1)S(1)} %copy-done.2), kind=kOutput, calls=%fused_computation.21 | convolution fusion | flops 151781376 | bytes 4784128 | tf_op jit(solution)/shard_map/abocd,oabds->abcs/dot_general | solution.py:81
  (69 shorter events, 3.7 us)
Async XLA Ops:
  0.0 80.7 %copy-start = (bf16[2,4,9,64,64]{4,3,2,1,0:T(8,128)(2,1)S(1)}, bf16[2,4,9,64,64]{4,3,2,1,0:T(8,128)(2,1)}, u32[]{:S(2)}) copy-start(bf16[2,4,9,64,64]{4,3,2,1,0:T(8,128)(2,1)} %param.63) | copy-start | bytes 1769476
  1.2 23.9 %collective-permute-start.1 = (bf16[2,1,64,256]{3,2,1,0:T(8,128)(2,1)S(1)}, bf16[2,1,64,256]{3,2,1,0:T(8,128)(2,1)S(1)}, u32[]{:S(2)}, u32[]{:S(2)}) collective-permute-start(bf16[2,1,64,256]{3,2,1,0:T(8,128)(2,1)S(1)} %get-tuple-element.336), channel_id=1, source_target_pairs={{1,0},{2,1},{3,2},{4,3},{5,4},{6,5},{7,6},{8,7},{9,8},{10,9},{11,1... | collective-permute-start | bytes 196616 | tf_op jit(solution)/shard_map/ppermute | solution.py:24
  13.2 11.9 %collective-permute-start = (bf16[2,1,64,256]{3,2,1,0:T(8,128)(2,1)S(1)}, bf16[2,1,64,256]{3,2,1,0:T(8,128)(2,1)S(1)}, u32[]{:S(2)}, u32[]{:S(2)}) collective-permute-start(bf16[2,1,64,256]{3,2,1,0:T(8,128)(2,1)S(1)} %get-tuple-element.335), channel_id=1, source_target_pairs={{0,1},{1,2},{2,3},{3,4},{4,5},{5,6},{6,7},{7,8},{8,9},{9,10},{10,1... | collective-permute-start | bytes 196616 | tf_op jit(solution)/shard_map/ppermute | solution.py:21
  21.4 10.8 %copy-start.9 = (s32[4]{0:T(128)S(1)}, s32[4]{0:T(128)}, u32[]{:S(2)}) copy-start(s32[4]{0:T(128)} %constant.642.clone.1) | copy-start | bytes 52
  25.2 18.2 %copy-start.3 = (f32[2,4,64,256]{3,2,1,0:T(8,128)S(1)}, f32[2,4,64,256]{3,2,1,0:T(8,128)}, u32[]{:S(2)}) copy-start(f32[2,4,64,256]{3,2,1,0:T(8,128)} %param.61) | copy-start | bytes 1572868
  25.2 7.7 %collective-permute-start.3 = (bf16[1,6,64,256]{3,2,1,0:T(8,128)(2,1)S(1)}, bf16[1,6,64,256]{3,2,1,0:T(8,128)(2,1)S(1)}, u32[]{:S(2)}, u32[]{:S(2)}) collective-permute-start(bf16[1,6,64,256]{3,2,1,0:T(8,128)(2,1)S(1)} %get-tuple-element.331), channel_id=1, source_target_pairs={{32,0},{64,32},{96,64},{128,96},{160,128},{192,160},{224,192},{256... | collective-permute-start | bytes 589832 | tf_op jit(solution)/shard_map/ppermute | solution.py:24
  29.7 10.6 %collective-permute-start.2 = (bf16[1,6,64,256]{3,2,1,0:T(8,128)(2,1)S(1)}, bf16[1,6,64,256]{3,2,1,0:T(8,128)(2,1)S(1)}, u32[]{:S(2)}, u32[]{:S(2)}) collective-permute-start(bf16[1,6,64,256]{3,2,1,0:T(8,128)(2,1)S(1)} %get-tuple-element.332), channel_id=1, source_target_pairs={{0,32},{32,64},{64,96},{96,128},{128,160},{160,192},{192,224},{224... | collective-permute-start | bytes 589832 | tf_op jit(solution)/shard_map/ppermute | solution.py:21
  41.2 6.0 %copy-start.6 = (f32[2,4,64]{2,1,0:T(4,128)S(1)}, f32[2,4,64]{2,1,0:T(4,128)}, u32[]{:S(2)}) copy-start(f32[2,4,64]{2,1,0:T(4,128)} %param.68) | copy-start | bytes 6148
  41.2 6.0 %copy-start.7 = (f32[2,4,64]{2,1,0:T(4,128)S(1)}, f32[2,4,64]{2,1,0:T(4,128)}, u32[]{:S(2)}) copy-start(f32[2,4,64]{2,1,0:T(4,128)} %param.69) | copy-start | bytes 6148
  59.4 11.1 %collective-permute-start.4 = (f32[4,64,256]{2,1,0:T(8,128)S(1)}, f32[4,64,256]{2,1,0:T(8,128)S(1)}, u32[]{:S(2)}, u32[]{:S(2)}) collective-permute-start(f32[4,64,256]{2,1,0:T(8,128)S(1)} %get-tuple-element.320), channel_id=1, source_target_pairs={{1,0},{2,1},{3,2},{4,3},{5,4},{6,5},{7,6},{8,7},{9,8},{10,9},{11,1... | collective-permute-start | bytes 786440 | tf_op jit(solution)/shard_map/ppermute | solution.py:32
  65.8 14.9 %copy-start.8 = (s32[2,4,9]{2,1,0:T(4,128)S(1)}, s32[2,4,9]{2,1,0:T(4,128)}, u32[]{:S(2)}) copy-start(s32[2,4,9]{2,1,0:T(4,128)} %param.64) | copy-start | bytes 868
  65.8 10.4 %collective-permute-start.5 = (f32[4,64,256]{2,1,0:T(8,128)S(1)}, f32[4,64,256]{2,1,0:T(8,128)S(1)}, u32[]{:S(2)}, u32[]{:S(2)}) collective-permute-start(f32[4,64,256]{2,1,0:T(8,128)S(1)} %get-tuple-element.319), channel_id=1, source_target_pairs={{31,0},{0,1},{1,2},{2,3},{3,4},{4,5},{5,6},{6,7},{7,8},{8,9},{9,10... | collective-permute-start | bytes 786440 | tf_op jit(solution)/shard_map/ppermute | solution.py:32
  76.3 5.8 %collective-permute-start.6 = (f32[4,64,256]{2,1,0:T(8,128)S(1)}, f32[4,64,256]{2,1,0:T(8,128)S(1)}, u32[]{:S(2)}, u32[]{:S(2)}) collective-permute-start(f32[4,64,256]{2,1,0:T(8,128)S(1)} %get-tuple-element.324), channel_id=1, source_target_pairs={{32,0},{64,32},{96,64},{128,96},{160,128},{192,160},{224,192},{256... | collective-permute-start | bytes 786440 | tf_op jit(solution)/shard_map/ppermute | solution.py:38
  78.2 12.0 %collective-permute-start.7 = (f32[4,64,256]{2,1,0:T(8,128)S(1)}, f32[4,64,256]{2,1,0:T(8,128)S(1)}, u32[]{:S(2)}, u32[]{:S(2)}) collective-permute-start(f32[4,64,256]{2,1,0:T(8,128)S(1)} %get-tuple-element.323), channel_id=1, source_target_pairs={{0,32},{32,64},{64,96},{96,128},{128,160},{160,192},{192,224},{224... | collective-permute-start | bytes 786440 | tf_op jit(solution)/shard_map/ppermute | solution.py:38
  81.6 11.1 %copy-start.1 = (bf16[2,4,9,64,64]{4,2,3,1,0:T(8,128)(2,1)}, bf16[2,4,9,64,64]{4,2,3,1,0:T(8,128)(2,1)S(1)}, u32[]{:S(2)}) copy-start(bf16[2,4,9,64,64]{4,2,3,1,0:T(8,128)(2,1)S(1)} %fusion) | copy-start | bytes 1769476
  81.7 8.7 %copy-start.4 = (bf16[2,2,4,64,256]{4,3,2,1,0:T(8,128)(2,1)S(1)}, bf16[2,2,4,64,256]{4,3,2,1,0:T(8,128)(2,1)}, u32[]{:S(2)}) copy-start(bf16[2,2,4,64,256]{4,3,2,1,0:T(8,128)(2,1)} %param.62) | copy-start | bytes 1572868
  92.8 6.4 %collective-permute-start.9 = (bf16[2,1,64,256]{3,2,1,0:T(8,128)(2,1)S(1)}, bf16[2,1,64,256]{3,2,1,0:T(8,128)(2,1)S(1)}, u32[]{:S(2)}, u32[]{:S(2)}) collective-permute-start(bf16[2,1,64,256]{3,2,1,0:T(8,128)(2,1)S(1)} %get-tuple-element.334), channel_id=1, source_target_pairs={{1,0},{2,1},{3,2},{4,3},{5,4},{6,5},{7,6},{8,7},{9,8},{10,9},{11,1... | collective-permute-start | bytes 196616 | tf_op jit(solution)/shard_map/ppermute | solution.py:24
  97.3 8.3 %collective-permute-start.8 = (bf16[2,1,64,256]{3,2,1,0:T(8,128)(2,1)S(1)}, bf16[2,1,64,256]{3,2,1,0:T(8,128)(2,1)S(1)}, u32[]{:S(2)}, u32[]{:S(2)}) collective-permute-start(bf16[2,1,64,256]{3,2,1,0:T(8,128)(2,1)S(1)} %get-tuple-element.333), channel_id=1, source_target_pairs={{0,1},{1,2},{2,3},{3,4},{4,5},{5,6},{6,7},{7,8},{8,9},{9,10},{10,1... | collective-permute-start | bytes 196616 | tf_op jit(solution)/shard_map/ppermute | solution.py:21
  105.6 5.1 %collective-permute-start.11 = (bf16[1,6,64,256]{3,2,1,0:T(8,128)(2,1)S(1)}, bf16[1,6,64,256]{3,2,1,0:T(8,128)(2,1)S(1)}, u32[]{:S(2)}, u32[]{:S(2)}) collective-permute-start(bf16[1,6,64,256]{3,2,1,0:T(8,128)(2,1)S(1)} %get-tuple-element.327), channel_id=1, source_target_pairs={{32,0},{64,32},{96,64},{128,96},{160,128},{192,160},{224,192},{256... | collective-permute-start | bytes 589832 | tf_op jit(solution)/shard_map/ppermute | solution.py:24
  107.6 10.6 %collective-permute-start.10 = (bf16[1,6,64,256]{3,2,1,0:T(8,128)(2,1)S(1)}, bf16[1,6,64,256]{3,2,1,0:T(8,128)(2,1)S(1)}, u32[]{:S(2)}, u32[]{:S(2)}) collective-permute-start(bf16[1,6,64,256]{3,2,1,0:T(8,128)(2,1)S(1)} %get-tuple-element.328), channel_id=1, source_target_pairs={{0,32},{32,64},{64,96},{96,128},{128,160},{160,192},{192,224},{224... | collective-permute-start | bytes 589832 | tf_op jit(solution)/shard_map/ppermute | solution.py:21
  137.1 8.6 %collective-permute-start.12 = (f32[4,64,256]{2,1,0:T(8,128)S(1)}, f32[4,64,256]{2,1,0:T(8,128)S(1)}, u32[]{:S(2)}, u32[]{:S(2)}) collective-permute-start(f32[4,64,256]{2,1,0:T(8,128)S(1)} %get-tuple-element.318), channel_id=1, source_target_pairs={{1,0},{2,1},{3,2},{4,3},{5,4},{6,5},{7,6},{8,7},{9,8},{10,9},{11,1... | collective-permute-start | bytes 786440 | tf_op jit(solution)/shard_map/ppermute | solution.py:32
  139.0 10.4 %collective-permute-start.13 = (f32[4,64,256]{2,1,0:T(8,128)S(1)}, f32[4,64,256]{2,1,0:T(8,128)S(1)}, u32[]{:S(2)}, u32[]{:S(2)}) collective-permute-start(f32[4,64,256]{2,1,0:T(8,128)S(1)} %get-tuple-element.317), channel_id=1, source_target_pairs={{31,0},{0,1},{1,2},{2,3},{3,4},{4,5},{5,6},{6,7},{7,8},{8,9},{9,10... | collective-permute-start | bytes 786440 | tf_op jit(solution)/shard_map/ppermute | solution.py:32
  145.8 17.0 %copy-start.2 = (bf16[2,4,9,64,64]{4,2,3,1,0:T(8,128)(2,1)S(1)}, bf16[2,4,9,64,64]{4,2,3,1,0:T(8,128)(2,1)}, u32[]{:S(2)}) copy-start(bf16[2,4,9,64,64]{4,2,3,1,0:T(8,128)(2,1)} %copy-done.1) | copy-start | bytes 1769476
  145.8 17.0 %copy-start.5 = (bf16[2,2,4,64,256]{4,3,2,1,0:T(8,128)(2,1)S(1)}, bf16[2,2,4,64,256]{4,3,2,1,0:T(8,128)(2,1)}, u32[]{:S(2)}) copy-start(bf16[2,2,4,64,256]{4,3,2,1,0:T(8,128)(2,1)} %param.62) | copy-start | bytes 1572868
  149.5 5.8 %collective-permute-start.14 = (f32[4,64,256]{2,1,0:T(8,128)S(1)}, f32[4,64,256]{2,1,0:T(8,128)S(1)}, u32[]{:S(2)}, u32[]{:S(2)}) collective-permute-start(f32[4,64,256]{2,1,0:T(8,128)S(1)} %get-tuple-element.322), channel_id=1, source_target_pairs={{32,0},{64,32},{96,64},{128,96},{160,128},{192,160},{224,192},{256... | collective-permute-start | bytes 786440 | tf_op jit(solution)/shard_map/ppermute | solution.py:38
  151.4 11.3 %collective-permute-start.15 = (f32[4,64,256]{2,1,0:T(8,128)S(1)}, f32[4,64,256]{2,1,0:T(8,128)S(1)}, u32[]{:S(2)}, u32[]{:S(2)}) collective-permute-start(f32[4,64,256]{2,1,0:T(8,128)S(1)} %get-tuple-element.321), channel_id=1, source_target_pairs={{0,32},{32,64},{64,96},{96,128},{128,160},{160,192},{192,224},{224... | collective-permute-start | bytes 786440 | tf_op jit(solution)/shard_map/ppermute | solution.py:38
where the time goes:
time: 167 us; the launch traced here: 166 us
  starting transfers between devices  53.8 us (32%)
  waiting for transfers between devices  53.6 us (32%)
  local copies, waits for them, and re-layouts  21.5 us (13%)
  matrix products  21.3 us (13%)
  other arithmetic  15.1 us (9%)
    ppermute x4, starting transfers between devices, padded(): lax.ppermute(lax.slice_in_dim(block, 0, width, axis=dim), axis, backward)  22.9 us
    ppermute x4, waiting for transfers between devices, padded(): lax.ppermute(lax.slice_in_dim(block, block.shape[dim] - width, None, axis...  21.1 us
    ppermute x4, waiting for transfers between devices, shifted_2(): return lax.ppermute(shard, axis, pairs)  17.3 us
    ppermute x4, waiting for transfers between devices, passed_along(): return lax.ppermute(block, axis, route)  14.5 us
    ppermute x4, starting transfers between devices, passed_along(): return lax.ppermute(block, axis, route)  14.1 us
    unnamed x2, matrix products  10.1 us
    unnamed x33, local copies, waits for them, and re-layouts  9.01 us
    ppermute x4, starting transfers between devices, shifted_2(): return lax.ppermute(shard, axis, pairs)  8.65 us
  transfers between devices with their start and end apart: 16, of which 12 were waited for; matrix products, arithmetic and copies ran while one was open for 8% of the time, Pallas kernels for 0%

commit v1 on v0

v1 whole, which is shorter than its diff:
```python
import math

import jax
import jax.numpy as jnp
from jax import lax
from jax.experimental import pallas as pl
from jax.experimental.pallas import tpu as pltpu
from jax.sharding import PartitionSpec as P

STEPS = 2
step_size = 0.2
BF = jnp.bfloat16
F32 = jnp.float32
VM = pltpu.VMEM


def shift_lon(block, by):
    count = lax.axis_size("lon")
    return lax.ppermute(block, "lon", [(i, (i + by) % count) for i in range(count)])


def shift_lat(block, by):
    count = lax.axis_size("lat")
    return lax.ppermute(
        block, "lat", [(i, i + by) for i in range(count) if 0 <= i + by < count]
    )


def pieces(x):
    high = lax.reduce_precision(x, 8, 7)
    rest = x - high
    middle = lax.reduce_precision(rest, 8, 7)
    return [high, middle, rest - middle]


def prior_matrix_kernel(pattern_ref, precision_ref, lp_ref, slot_ref):
    for b in range(2):
        for j in range(4):
            for k in range(9):
                slot_ref[(b * 4 + j) * 9 + pattern_ref[b, j, k]] = k
    blank = jnp.zeros((64, 64), BF)
    for b in range(2):
        for p in range(2):
            for dr in range(3):
                for t in range(2):
                    j = 2 * p + t
                    parts = [
                        precision_ref[b, j, slot_ref[(b * 4 + j) * 9 + dr * 3 + o]]
                        for o in range(3)
                    ]
                    parts = [blank] * t + parts + [blank] * (1 - t)
                    lp_ref[b, p, dr, t * 64 : (t + 1) * 64, :] = jnp.concatenate(parts, axis=1)


def foot_matrix_kernel(fw_ref, mt_ref, lf_ref, la_ref, ov_ref):
    rowblock = lax.broadcasted_iota(jnp.int32, (256, 256), 0) // 64
    laneblock = lax.broadcasted_iota(jnp.int32, (256, 256), 1) // 64
    lane_owner = lax.broadcasted_iota(jnp.int32, (16, 256), 1) // 64
    for i in range(4):
        meta = mt_ref[i].astype(F32)
        columns = jnp.transpose(meta, (1, 0))
        obs = columns[:, 4:5] + columns[:, 5:6] + columns[:, 6:7]
        ivar = columns[:, 7:8] + columns[:, 8:9] + columns[:, 9:10]
        ov_ref[0, i] = jnp.broadcast_to(obs, (384, 128))
        ov_ref[1, i] = jnp.broadcast_to(ivar, (384, 128))
        weights = fw_ref[i]
        for q in range(2):
            rows = slice(q * 128, q * 128 + 256)
            for dr in range(3):
                col = laneblock - rowblock + 2 * q
                need = jnp.where((col >= 0) & (col <= 2), col + 3 * dr, 99).astype(F32)
                total = jnp.zeros((256, 256), F32)
                for j in range(4):
                    one = weights[rows, j * 64 : (j + 1) * 64].astype(F32)
                    four = jnp.concatenate([one] * 4, axis=1)
                    total = total + jnp.where(columns[rows, j : j + 1] == need, four, 0.0)
                lf_ref[i, q, dr] = total.astype(BF)
        turned = jnp.transpose(weights.astype(F32), (1, 0))
        for b in range(2):
            if not 0 <= b - i + 2 <= 2:
                continue
            for p in range(2):
                lanes = slice(p * 128, p * 128 + 256)
                for t in range(2):
                    col = t - lane_owner[0:1] + 2
                    need = jnp.where((col >= 0) & (col <= 2), col + 3 * (b - i + 2), 99)
                    need = need.astype(F32)
                    total = jnp.zeros((64, 256), F32)
                    for j in range(4):
                        hit = (meta[j : j + 1, lanes] == need).astype(F32)
                        total = total + turned[j * 64 : (j + 1) * 64, lanes] * hit
                    la_ref[b, p, i - b, t * 64 : (t + 1) * 64, :] = total.astype(BF)


def dot(a, b):
    return jnp.dot(a, b, preferred_element_type=F32)


def step_kernel(last, x_ref, lf_ref, la_ref, lp_ref, ov_ref, sample_ref, noise_ref, *refs):
    out_ref = refs[0]
    res_ref = refs[-1]
    for i in range(4):
        half = []
        for q in range(2):
            acc = dot(lf_ref[i, q, 0], x_ref[i, q * 256 : (q + 1) * 256, :])
            for dr in (1, 2):
                acc = acc + dot(lf_ref[i, q, dr], x_ref[i + dr, q * 256 : (q + 1) * 256, :])
            half.append(acc)
        for part in range(3):
            rows = slice(part * 128, (part + 1) * 128)
            if part == 0:
                fwd = half[0][:128]
            elif part == 1:
                fwd = half[0][128:] + half[1][:128]
            else:
                fwd = half[1][128:]
            obs = ov_ref[0, i, rows, :]
            ivar = ov_ref[1, i, rows, :]
            for h in range(2):
                lanes = slice(h * 128, (h + 1) * 128)
                res_ref[i, rows, lanes] = (ivar * (fwd[:, lanes] - obs)).astype(BF)
    for b in range(2):
        for p in range(2):
            acc = None
            for dr in range(3):
                term = dot(lp_ref[b, p, dr], x_ref[b + 1 + dr, (1 + 2 * p) * 64 : (5 + 2 * p) * 64, :])
                acc = term if acc is None else acc + term
                acc = acc + dot(la_ref[b, p, dr], res_ref[b + dr, p * 128 : p * 128 + 256, :])
            rows = slice(p * 128, (p + 1) * 128)
            value = (
                sample_ref[b, rows, :]
                - step_size * acc
                + math.sqrt(2.0 * step_size) * noise_ref[b, rows, :].astype(F32)
            )
            out_ref[b, rows, :] = value
            if not last:
                refs[1][b, rows, :] = value.astype(BF)


def whole(n):
    return [pl.BlockSpec(memory_space=VM)] * n


PARAMS = pltpu.CompilerParams(vmem_limit_bytes=48 * 1024 * 1024)


def prior_matrix(pattern, precision):
    return pl.pallas_call(
        prior_matrix_kernel,
        out_shape=jax.ShapeDtypeStruct((2, 2, 3, 128, 256), BF),
        in_specs=[pl.BlockSpec(memory_space=pltpu.SMEM)] + whole(1),
        out_specs=whole(1)[0],
        scratch_shapes=[pltpu.SMEM((72,), jnp.int32)],
        compiler_params=PARAMS,
        cost_estimate=pl.CostEstimate(flops=2000000, bytes_accessed=3000000, transcendentals=0),
    )(pattern, precision)


def foot_matrix(fw, mt):
    return pl.pallas_call(
        foot_matrix_kernel,
        out_shape=(
            jax.ShapeDtypeStruct((4, 2, 3, 256, 256), BF),
            jax.ShapeDtypeStruct((2, 2, 3, 128, 256), BF),
            jax.ShapeDtypeStruct((2, 4, 384, 128), F32),
        ),
        in_specs=whole(2),
        out_specs=tuple(whole(3)),
        compiler_params=PARAMS,
        cost_estimate=pl.CostEstimate(flops=20000000, bytes_accessed=6000000, transcendentals=0),
    )(fw, mt)


def step(window, lf, la, lp, ov, sample, noise, last):
    shapes = [jax.ShapeDtypeStruct((2, 256, 256), F32)]
    if not last:
        shapes.append(jax.ShapeDtypeStruct((2, 256, 256), BF))
    return pl.pallas_call(
        lambda *refs: step_kernel(last, *refs),
        name="langevin_last" if last else "langevin_first",
        out_shape=tuple(shapes),
        in_specs=whole(7),
        out_specs=tuple(whole(len(shapes))),
        scratch_shapes=[pltpu.VMEM((4, 384, 256), BF)],
        compiler_params=PARAMS,
        cost_estimate=pl.CostEstimate(flops=1200000000, bytes_accessed=9000000, transcendentals=0),
    )(window, lf, la, lp, ov, sample, noise)


def local(
    sample_field,
    langevin_noise,
    precision,
    pattern,
    foot_weight,
    foot_columns,
    foot_count,
    observed,
    inverse_var,
):
    sample = sample_field.reshape(2, 256, 256)
    noise = langevin_noise.reshape(STEPS, 2, 256, 256)
    compact = sample.astype(BF)
    active = jnp.arange(4, dtype=jnp.int32) < foot_count[..., None]
    fw = jnp.where(active[..., None], foot_weight, jnp.zeros_like(foot_weight))
    fw = fw.reshape(2, 256, 256)
    rows = [foot_columns.transpose(0, 3, 1, 2).reshape(2, 4, 256).astype(F32)]
    rows += [part.reshape(2, 1, 256) for part in pieces(observed) + pieces(inverse_var)]
    rows.append(jnp.zeros((2, 6, 256), F32))
    mt = jnp.concatenate(rows, axis=1).astype(BF)

    def edge(cells, col):
        meta = jnp.pad(mt[:, :, col * 64 : (col + 1) * 64], ((0, 0), (0, 0), (0, 192)))
        return jnp.concatenate([compact[:, cells], fw[:, col * 64 : (col + 1) * 64], meta], axis=1)

    lp = prior_matrix(pattern, precision)
    west = shift_lon(edge(slice(128, 256), 3), 1)
    east = shift_lon(edge(slice(0, 128), 0), -1)
    middle = jnp.concatenate([west[:, :128], compact, east[:, :128]], axis=1)
    fw = jnp.concatenate([west[:, 128:192], fw, east[:, 128:192]], axis=1)
    mt = jnp.concatenate([west[:, 192:, :64], mt, east[:, 192:, :64]], axis=2)
    flat = middle.reshape(1024, 256)

    def band(row):
        meta = jnp.pad(mt[row], ((0, 0), (0, 128)))
        return jnp.concatenate([flat, fw[row], meta[:, :256], meta[:, 256:]], axis=0)

    north = shift_lat(band(1), 1)
    south = shift_lat(band(0), -1)

    def unband(got):
        meta = jnp.concatenate([got[1408:1424], got[1424:1440, :128]], axis=1)
        return got[:1024].reshape(2, 512, 256), got[1024:1408][None], meta[None]

    (xn, fn, mn), (xs, fs, ms) = unband(north), unband(south)
    window = jnp.concatenate([xn, middle, xs], axis=0)
    fw = jnp.concatenate([fn, fw, fs], axis=0)
    mt = jnp.concatenate([mn, mt, ms], axis=0)
    lf, la, ov = foot_matrix(fw, mt)
    sample, compact = step(window, lf, la, lp, ov, sample, noise[0], False)

    west = shift_lon(compact[:, 128:], 1)
    east = shift_lon(compact[:, :128], -1)
    middle = jnp.concatenate([west, compact, east], axis=1)
    window = jnp.concatenate([shift_lat(middle, 1), middle, shift_lat(middle, -1)], axis=0)
    (sample,) = step(window, lf, la, lp, ov, sample, noise[1], True)
    return sample.reshape(sample_field.shape)


def solution(mesh):
    placed = (
        P("lat", "lon", None, None),
        P(None, "lat", "lon", None, None),
        P("lat", "lon", None, None, None),
        P("lat", "lon", None),
        P("lat", "lon", None, None, None),
        P("lat", "lon", None, None),
        P("lat", "lon", None),
        P("lat", "lon", None),
        P("lat", "lon", None),
    )
    return jax.shard_map(
        local, mesh=mesh, in_specs=placed, out_specs=P("lat", "lon", None, None), check_vma=False
    )
```

time: 167 us -> 95.3 us (0.57)
  waiting for transfers between devices: 53.6 us -> 31.4 us
  matrix products: 21.3 us -> 0 us
  local copies, waits for them, and re-layouts: 21.5 us -> 2.6 us
  Pallas kernels: 0 us -> 15.3 us
  starting transfers between devices: 53.8 us -> 39.6 us
  other arithmetic: 15.1 us -> 5.49 us
    ppermute x16 -> x8, waiting for transfers between devices: 53.6 us -> 31.4 us  [the longest x4 20.2 us: shift_lat(): lax.ppermute(block, 'lat', [(i, i + by) for i in range(count) if 0 <= i +...]
    pallas_call x0 -> x4, Pallas kernels: none -> 15.3 us  [the longest x2 7.86 us: step(): pl.pallas_call(lambda *refs: step_kernel(last, *refs), name='langevin_las...]
    ppermute x16 -> x8, starting transfers between devices: 53.8 us -> 39.6 us  [the longest x4 21.9 us: shift_lon(): lax.ppermute(block, 'lon', [(i, (i + by) % count) for i in range(count)])]
    dot_general x4 -> x0, matrix products: 11.2 us -> none  [the longest x2 5.62 us: local(): jnp.einsum('abocd,oabds->abcs', ordered, shifted, preferred_element_type=...]
    unnamed x2 -> x0, matrix products: 10.1 us -> none
    scatter-add x24 -> x0, other arithmetic: 8.33 us -> none  [the longest x16 7.97 us: local(): partial_grid = partial_grid.at[offset // 3:offset // 3 + band_height, off...]
    unnamed x33 -> x18, local copies, waits for them, and re-layouts: 9.01 us -> 1.24 us
    dot_general x2 -> x0, local copies, waits for them, and re-layouts: 5.81 us -> none  [local(): jnp.einsum('abfoc,abfs->oabcs', foot_matrix, residual, preferred_element_...]
  transfers between devices with their start and end apart: 16 -> 8, of which waited for: 12 -> 8; matrix products, arithmetic and copies ran while one was open for 8% -> 0% of each run, Pallas kernels for 0% -> 1%
where the time goes in v1:
time: 95.3 us; the launch traced here: 94.7 us
  starting transfers between devices  39.6 us (42%)
  waiting for transfers between devices  31.4 us (33%)
  Pallas kernels  15.3 us (16%)
  other arithmetic  5.49 us (6%)
  local copies, waits for them, and re-layouts  2.6 us (3%)
    ppermute x4, starting transfers between devices, shift_lon(): lax.ppermute(block, 'lon', [(i, (i + by) % count) for i in range(count)])  21.9 us
    ppermute x4, waiting for transfers between devices, shift_lat(): lax.ppermute(block, 'lat', [(i, i + by) for i in range(count) if 0 <= i +...  20.2 us
    ppermute x4, starting transfers between devices, shift_lat(): lax.ppermute(block, 'lat', [(i, i + by) for i in range(count) if 0 <= i +...  17.7 us
    ppermute x4, waiting for transfers between devices, shift_lon(): lax.ppermute(block, 'lon', [(i, (i + by) % count) for i in range(count)])  11.2 us
    pallas_call x2, Pallas kernels, step(): pl.pallas_call(lambda *refs: step_kernel(last, *refs), name='langevin_las...  7.86 us
    pallas_call x1, Pallas kernels, foot_matrix(): pl.pallas_call(foot_matrix_kernel, out_shape=(jax.ShapeDtypeStruct((4, 2,...  6.49 us
  transfers between devices with their start and end apart: 8, of which 8 were waited for; matrix products, arithmetic and copies ran while one was open for 0% of the time, Pallas kernels for 1%

profile of v1, /device:TPU:4, one launch (start us, length us, event | category | flops | bytes accessed | tf_op | source)
XLA Modules:
  0.0 94.7 jit_solution(16827809090621718858)
XLA Ops:
  0.0 0.0 copy-start.5
  0.0 0.8 fusion.7
  0.8 0.1 reshape.68
  0.8 0.1 reshape.67
  0.9 0.1 reshape.66
  1.0 0.7 fusion.8
  1.7 0.1 reshape.71
  1.8 0.1 reshape.70
  1.9 0.1 reshape.69
  2.0 0.7 fusion.6
  2.7 0.1 convert_element_type.22
  2.8 0.8 iota_compare_fusion.1
  3.6 0.0 copy-start.7
  3.6 1.1 %bitcast_convert_fusion = bf16[2,256,256]{2,1,0:T(8,128)(2,1)S(1)} fusion(f32[2,4,64,256]{3,2,1,0:T(8,128)} %param.9), kind=kLoop, calls=%fused_computation.45 | loop fusion | flops 131072 | bytes 786432 | tf_op jit(solution)/shard_map/convert_element_type | solution.py:203
  4.7 0.0 copy-done.5
  4.7 0.7 broadcast_select_fusion
  5.5 0.3 reshape.55
  5.8 0.1 concatenate.46
  5.9 0.0 copy-done.7
  5.9 12.0 %collective-permute-start.1 = (bf16[2,208,256]{2,1,0:T(8,128)(2,1)S(1)}, bf16[2,208,256]{2,1,0:T(8,128)(2,1)S(1)}, u32[]{:S(2)}, u32[]{:S(2)}) collective-permute-start(bf16[2,208,256]{2,1,0:T(8,128)(2,1)S(1)} %pad_maximum_fusion.7), channel_id=1, source_target_pairs={{0,31},{1,0},{2,1},{3,2},{4,3},{5,4},{6,5},{7,6},{8,7},{9,8},{10,9... | collective-permute-start | bytes 638984 | tf_op jit(solution)/shard_map/ppermute | solution.py:19
  18.0 0.1 slice.132
  18.1 1.9 %collective-permute-start = (bf16[2,208,256]{2,1,0:T(8,128)(2,1)S(1)}, bf16[2,208,256]{2,1,0:T(8,128)(2,1)S(1)}, u32[]{:S(2)}, u32[]{:S(2)}) collective-permute-start(bf16[2,208,256]{2,1,0:T(8,128)(2,1)S(1)} %fusion.5), channel_id=1, source_target_pairs={{0,1},{1,2},{2,3},{3,4},{4,5},{5,6},{6,7},{7,8},{8,9},{9,10},{10,1... | collective-permute-start | bytes 638984 | tf_op jit(solution)/shard_map/ppermute | solution.py:19
  20.0 2.5 %collective-permute-done.1 = bf16[2,208,256]{2,1,0:T(8,128)(2,1)S(1)} collective-permute-done((bf16[2,208,256]{2,1,0:T(8,128)(2,1)S(1)}, bf16[2,208,256]{2,1,0:T(8,128)(2,1)S(1)}, u32[]{:S(2)}, u32[]{:S(2)}) %collective-permute-start.1) | collective-permute-done | bytes 213024 | tf_op jit(solution)/shard_map/ppermute | solution.py:19
  22.5 6.3 %collective-permute-done = bf16[2,208,256]{2,1,0:T(8,128)(2,1)S(1)} collective-permute-done((bf16[2,208,256]{2,1,0:T(8,128)(2,1)S(1)}, bf16[2,208,256]{2,1,0:T(8,128)(2,1)S(1)}, u32[]{:S(2)}, u32[]{:S(2)}) %collective-permute-start) | collective-permute-done | bytes 213024 | tf_op jit(solution)/shard_map/ppermute | solution.py:19
  28.8 0.1 pad_maximum_fusion.9
  29.0 0.0 copy-start.3
  29.1 0.0 copy-start.4
  29.1 0.1 fusion.1
  29.2 0.0 copy-start.6
  29.2 2.1 %collective-permute-start.2 = (bf16[1440,256]{1,0:T(8,128)(2,1)S(1)}, bf16[1440,256]{1,0:T(8,128)(2,1)S(1)}, u32[]{:S(2)}, u32[]{:S(2)}) collective-permute-start(bf16[1440,256]{1,0:T(8,128)(2,1)S(1)} %get-tuple-element.17), channel_id=1, source_target_pairs={{0,32},{32,64},{64,96},{96,128},{128,160},{160,192},{192,224},{224... | collective-permute-start | bytes 2211848 | tf_op jit(solution)/shard_map/ppermute | solution.py:24
  31.3 7.3 %collective-permute-start.3 = (bf16[1440,256]{1,0:T(8,128)(2,1)S(1)}, bf16[1440,256]{1,0:T(8,128)(2,1)S(1)}, u32[]{:S(2)}, u32[]{:S(2)}) collective-permute-start(bf16[1440,256]{1,0:T(8,128)(2,1)S(1)} %get-tuple-element.18), channel_id=1, source_target_pairs={{32,0},{64,32},{96,64},{128,96},{160,128},{192,160},{224,192},{256... | collective-permute-start | bytes 2211848 | tf_op jit(solution)/shard_map/ppermute | solution.py:24
  38.6 0.0 copy-done.3
  38.6 0.0 copy-done.4
  38.6 0.9 shard_map.92.refs_3_
  39.5 0.0 copy-done.6
  39.5 6.2 %collective-permute-done.2 = bf16[1440,256]{1,0:T(8,128)(2,1)S(1)} collective-permute-done((bf16[1440,256]{1,0:T(8,128)(2,1)S(1)}, bf16[1440,256]{1,0:T(8,128)(2,1)S(1)}, u32[]{:S(2)}, u32[]{:S(2)}) %collective-permute-start.2) | collective-permute-done | bytes 737312 | tf_op jit(solution)/shard_map/ppermute | solution.py:24
  45.8 1.7 %collective-permute-done.3 = bf16[1440,256]{1,0:T(8,128)(2,1)S(1)} collective-permute-done((bf16[1440,256]{1,0:T(8,128)(2,1)S(1)}, bf16[1440,256]{1,0:T(8,128)(2,1)S(1)}, u32[]{:S(2)}, u32[]{:S(2)}) %collective-permute-start.3) | collective-permute-done | bytes 737312 | tf_op jit(solution)/shard_map/ppermute | solution.py:24
  47.5 0.1 pad_maximum_fusion.8.mt_ref
  47.7 0.1 pad_maximum_fusion.refs_0_
  47.8 0.0 copy-start.2
  47.9 0.1 pad_maximum_fusion.2.fw_ref
  47.9 6.5 %shard_map.91 = (bf16[4,2,3,256,256]{4,3,2,1,0:T(8,128)(2,1)}, bf16[2,2,3,128,256]{4,3,2,1,0:T(8,128)(2,1)S(1)}, f32[2,4,384,128]{3,2,1,0:T(8,128)S(1)}) custom-call(bf16[4,384,256]{2,1,0:T(8,128)(2,1)S(1)} %pad_maximum_fusion.2.fw_ref, bf16[4,16,384]{2,1,0:T(8,128)(2,1)S(1)} %pad_maximum_fusion.8.mt_ref), custom_call_target="tpu_custom_call" | custom-call | flops 20000000 | bytes 6000000 | tf_op jit(solution)/shard_map/pallas_call | solution.py:160
  54.4 0.0 copy-start
  54.4 1.2 %copy-done = f32[2,4,384,128]{3,2,1,0:T(8,128)} copy-done((f32[2,4,384,128]{3,2,1,0:T(8,128)}, f32[2,4,384,128]{3,2,1,0:T(8,128)S(1)}, u32[]{:S(2)}) %copy-start) | copy-done | bytes 1572888
  55.6 0.0 copy-done.2
  55.6 3.8 %langevin_first.1 = (f32[2,256,256]{2,1,0:T(8,128)S(1)}, bf16[2,256,256]{2,1,0:T(8,128)(2,1)S(1)}) custom-call(bf16[6,512,256]{2,1,0:T(8,128)(2,1)S(1)} %pad_maximum_fusion.refs_0_, bf16[4,2,3,256,256]{4,3,2,1,0:T(8,128)(2,1)} %get-tuple-element.10.refs_1_, bf16[2,2,3,128,256]{4,3,2,1,0:T(8,128)(2,1)S(1)} %get-tuple-element.11.refs_2_, ...), custom_call_target="tpu_custom_call" | custom-call | flops 1200000000 | bytes 9000000 | tf_op jit(solution)/shard_map/langevin_first/pallas_call | solution.py:178
  59.4 1.9 %collective-permute-start.4 = (bf16[2,128,256]{2,1,0:T(8,128)(2,1)S(1)}, bf16[2,128,256]{2,1,0:T(8,128)(2,1)S(1)}, u32[]{:S(2)}, u32[]{:S(2)}) collective-permute-start(bf16[2,128,256]{2,1,0:T(8,128)(2,1)S(1)} %get-tuple-element.22), channel_id=1, source_target_pairs={{0,1},{1,2},{2,3},{3,4},{4,5},{5,6},{6,7},{7,8},{8,9},{9,10},{10,1... | collective-permute-start | bytes 393224 | tf_op jit(solution)/shard_map/ppermute | solution.py:19
  61.3 6.0 %collective-permute-start.5 = (bf16[2,128,256]{2,1,0:T(8,128)(2,1)S(1)}, bf16[2,128,256]{2,1,0:T(8,128)(2,1)S(1)}, u32[]{:S(2)}, u32[]{:S(2)}) collective-permute-start(bf16[2,128,256]{2,1,0:T(8,128)(2,1)S(1)} %get-tuple-element.21), channel_id=1, source_target_pairs={{0,31},{1,0},{2,1},{3,2},{4,3},{5,4},{6,5},{7,6},{8,7},{9,8},{10,9... | collective-permute-start | bytes 393224 | tf_op jit(solution)/shard_map/ppermute | solution.py:19
  67.4 1.1 %collective-permute-done.4 = bf16[2,128,256]{2,1,0:T(8,128)(2,1)S(1)} collective-permute-done((bf16[2,128,256]{2,1,0:T(8,128)(2,1)S(1)}, bf16[2,128,256]{2,1,0:T(8,128)(2,1)S(1)}, u32[]{:S(2)}, u32[]{:S(2)}) %collective-permute-start.4) | collective-permute-done | bytes 131104 | tf_op jit(solution)/shard_map/ppermute | solution.py:19
  68.5 1.4 %collective-permute-done.5 = bf16[2,128,256]{2,1,0:T(8,128)(2,1)S(1)} collective-permute-done((bf16[2,128,256]{2,1,0:T(8,128)(2,1)S(1)}, bf16[2,128,256]{2,1,0:T(8,128)(2,1)S(1)}, u32[]{:S(2)}, u32[]{:S(2)}) %collective-permute-start.5) | collective-permute-done | bytes 131104 | tf_op jit(solution)/shard_map/ppermute | solution.py:19
  69.9 0.0 copy-start.1
  69.9 6.4 %collective-permute-start.7 = (bf16[2,512,256]{2,1,0:T(8,128)(2,1)S(1)}, bf16[2,512,256]{2,1,0:T(8,128)(2,1)S(1)}, u32[]{:S(2)}, u32[]{:S(2)}) collective-permute-start(bf16[2,512,256]{2,1,0:T(8,128)(2,1)S(1)} %constant_dynamic-update-slice_fusion), channel_id=1, source_target_pairs={{32,0},{64,32},{96,64},{128,96},{160,128},{192,160},{224,192},{256... | collective-permute-start | bytes 1572872 | tf_op jit(solution)/shard_map/ppermute | solution.py:24
  76.3 1.9 %collective-permute-start.6 = (bf16[2,512,256]{2,1,0:T(8,128)(2,1)S(1)}, bf16[2,512,256]{2,1,0:T(8,128)(2,1)S(1)}, u32[]{:S(2)}, u32[]{:S(2)}) collective-permute-start(bf16[2,512,256]{2,1,0:T(8,128)(2,1)S(1)} %constant_dynamic-update-slice_fusion), channel_id=1, source_target_pairs={{0,32},{32,64},{64,96},{96,128},{128,160},{160,192},{192,224},{224... | collective-permute-start | bytes 1572872 | tf_op jit(solution)/shard_map/ppermute | solution.py:24
  78.3 4.7 %collective-permute-done.7 = bf16[2,512,256]{2,1,0:T(8,128)(2,1)S(1)} collective-permute-done((bf16[2,512,256]{2,1,0:T(8,128)(2,1)S(1)}, bf16[2,512,256]{2,1,0:T(8,128)(2,1)S(1)}, u32[]{:S(2)}, u32[]{:S(2)}) %collective-permute-start.7) | collective-permute-done | bytes 524320 | tf_op jit(solution)/shard_map/ppermute | solution.py:24
  83.0 7.4 %collective-permute-done.6 = bf16[2,512,256]{2,1,0:T(8,128)(2,1)S(1)} collective-permute-done((bf16[2,512,256]{2,1,0:T(8,128)(2,1)S(1)}, bf16[2,512,256]{2,1,0:T(8,128)(2,1)S(1)}, u32[]{:S(2)}, u32[]{:S(2)}) %collective-permute-start.6) | collective-permute-done | bytes 524320 | tf_op jit(solution)/shard_map/ppermute | solution.py:24
  90.4 0.2 pad_maximum_fusion.1.refs_0_
  90.6 0.0 copy-done.1
  90.6 4.1 %langevin_last.1 = f32[2,256,256]{2,1,0:T(8,128)} custom-call(bf16[6,512,256]{2,1,0:T(8,128)(2,1)S(1)} %pad_maximum_fusion.1.refs_0_, bf16[4,2,3,256,256]{4,3,2,1,0:T(8,128)(2,1)} %get-tuple-element.10.refs_1_, bf16[2,2,3,128,256]{4,3,2,1,0:T(8,128)(2,1)S(1)} %get-tuple-element.11.refs_2_, bf16[2,2,3,128,256]{4,3,2,1,0:T(8,128)(2,1)S(1)} %shard_map.92.refs_3_, ...), custom_call_target="tpu_custom_call" | custom-call | flops 1200000000 | bytes 9000000 | tf_op jit(solution)/shard_map/langevin_last/pallas_call | solution.py:178
  (33 shorter events, 0.4 us)
Async XLA Ops:
  0.0 4.7 %copy-start.5 = (bf16[2,4,64,4,64]{4,3,2,1,0:T(4,128)(2,1)S(1)}, bf16[2,4,64,4,64]{4,3,2,1,0:T(4,128)(2,1)}, u32[]{:S(2)}) copy-start(bf16[2,4,64,4,64]{4,3,2,1,0:T(4,128)(2,1)} %param.13) | copy-start | bytes 786436
  3.6 2.3 %copy-start.7 = (pred[256]{0:T(512)(128)(4,1)S(1)}, pred[256]{0:T(512)(128)(4,1)}, u32[]{:S(2)}) copy-start(pred[256]{0:T(512)(128)(4,1)} %constant.7.clone.1) | copy-start | bytes 772
  5.9 16.6 %collective-permute-start.1 = (bf16[2,208,256]{2,1,0:T(8,128)(2,1)S(1)}, bf16[2,208,256]{2,1,0:T(8,128)(2,1)S(1)}, u32[]{:S(2)}, u32[]{:S(2)}) collective-permute-start(bf16[2,208,256]{2,1,0:T(8,128)(2,1)S(1)} %pad_maximum_fusion.7), channel_id=1, source_target_pairs={{0,31},{1,0},{2,1},{3,2},{4,3},{5,4},{6,5},{7,6},{8,7},{9,8},{10,9... | collective-permute-start | bytes 638984 | tf_op jit(solution)/shard_map/ppermute | solution.py:19
  18.1 10.7 %collective-permute-start = (bf16[2,208,256]{2,1,0:T(8,128)(2,1)S(1)}, bf16[2,208,256]{2,1,0:T(8,128)(2,1)S(1)}, u32[]{:S(2)}, u32[]{:S(2)}) collective-permute-start(bf16[2,208,256]{2,1,0:T(8,128)(2,1)S(1)} %fusion.5), channel_id=1, source_target_pairs={{0,1},{1,2},{2,3},{3,4},{4,5},{5,6},{6,7},{7,8},{8,9},{9,10},{10,1... | collective-permute-start | bytes 638984 | tf_op jit(solution)/shard_map/ppermute | solution.py:19
  29.0 9.5 %copy-start.3 = (bf16[2,4,9,64,64]{4,3,2,1,0:T(8,128)(2,1)S(1)}, bf16[2,4,9,64,64]{4,3,2,1,0:T(8,128)(2,1)}, u32[]{:S(2)}) copy-start(bf16[2,4,9,64,64]{4,3,2,1,0:T(8,128)(2,1)} %precision_ref.1) | copy-start | bytes 1769476
  29.1 9.5 %copy-start.4 = (s32[2,4,9]{2,1,0:T(4,128)S(1)}, s32[2,4,9]{2,1,0:T(4,128)}, u32[]{:S(2)}) copy-start(s32[2,4,9]{2,1,0:T(4,128)} %pattern_ref.1) | copy-start | bytes 868
  29.2 10.3 %copy-start.6 = (bf16[2,2,4,64,256]{4,3,2,1,0:T(8,128)(2,1)S(1)}, bf16[2,2,4,64,256]{4,3,2,1,0:T(8,128)(2,1)}, u32[]{:S(2)}) copy-start(bf16[2,2,4,64,256]{4,3,2,1,0:T(8,128)(2,1)} %param.10) | copy-start | bytes 1572868
  29.2 16.5 %collective-permute-start.2 = (bf16[1440,256]{1,0:T(8,128)(2,1)S(1)}, bf16[1440,256]{1,0:T(8,128)(2,1)S(1)}, u32[]{:S(2)}, u32[]{:S(2)}) collective-permute-start(bf16[1440,256]{1,0:T(8,128)(2,1)S(1)} %get-tuple-element.17), channel_id=1, source_target_pairs={{0,32},{32,64},{64,96},{96,128},{128,160},{160,192},{192,224},{224... | collective-permute-start | bytes 2211848 | tf_op jit(solution)/shard_map/ppermute | solution.py:24
  31.3 16.2 %collective-permute-start.3 = (bf16[1440,256]{1,0:T(8,128)(2,1)S(1)}, bf16[1440,256]{1,0:T(8,128)(2,1)S(1)}, u32[]{:S(2)}, u32[]{:S(2)}) collective-permute-start(bf16[1440,256]{1,0:T(8,128)(2,1)S(1)} %get-tuple-element.18), channel_id=1, source_target_pairs={{32,0},{64,32},{96,64},{128,96},{160,128},{192,160},{224,192},{256... | collective-permute-start | bytes 2211848 | tf_op jit(solution)/shard_map/ppermute | solution.py:24
  47.8 7.8 %copy-start.2 = (f32[2,4,64,256]{3,2,1,0:T(8,128)S(1)}, f32[2,4,64,256]{3,2,1,0:T(8,128)}, u32[]{:S(2)}) copy-start(f32[2,4,64,256]{3,2,1,0:T(8,128)} %param.9) | copy-start | bytes 1572868
  54.4 1.2 %copy-start = (f32[2,4,384,128]{3,2,1,0:T(8,128)}, f32[2,4,384,128]{3,2,1,0:T(8,128)S(1)}, u32[]{:S(2)}) copy-start(f32[2,4,384,128]{3,2,1,0:T(8,128)S(1)} %get-tuple-element.12.refs_4_) | copy-start | bytes 4718596
  59.4 9.1 %collective-permute-start.4 = (bf16[2,128,256]{2,1,0:T(8,128)(2,1)S(1)}, bf16[2,128,256]{2,1,0:T(8,128)(2,1)S(1)}, u32[]{:S(2)}, u32[]{:S(2)}) collective-permute-start(bf16[2,128,256]{2,1,0:T(8,128)(2,1)S(1)} %get-tuple-element.22), channel_id=1, source_target_pairs={{0,1},{1,2},{2,3},{3,4},{4,5},{5,6},{6,7},{7,8},{8,9},{9,10},{10,1... | collective-permute-start | bytes 393224 | tf_op jit(solution)/shard_map/ppermute | solution.py:19
  61.3 8.5 %collective-permute-start.5 = (bf16[2,128,256]{2,1,0:T(8,128)(2,1)S(1)}, bf16[2,128,256]{2,1,0:T(8,128)(2,1)S(1)}, u32[]{:S(2)}, u32[]{:S(2)}) collective-permute-start(bf16[2,128,256]{2,1,0:T(8,128)(2,1)S(1)} %get-tuple-element.21), channel_id=1, source_target_pairs={{0,31},{1,0},{2,1},{3,2},{4,3},{5,4},{6,5},{7,6},{8,7},{9,8},{10,9... | collective-permute-start | bytes 393224 | tf_op jit(solution)/shard_map/ppermute | solution.py:19
  69.9 20.7 %copy-start.1 = (f32[2,4,384,128]{3,2,1,0:T(8,128)S(1)}, f32[2,4,384,128]{3,2,1,0:T(8,128)}, u32[]{:S(2)}) copy-start(f32[2,4,384,128]{3,2,1,0:T(8,128)} %copy-done) | copy-start | bytes 4718596
  69.9 13.1 %collective-permute-start.7 = (bf16[2,512,256]{2,1,0:T(8,128)(2,1)S(1)}, bf16[2,512,256]{2,1,0:T(8,128)(2,1)S(1)}, u32[]{:S(2)}, u32[]{:S(2)}) collective-permute-start(bf16[2,512,256]{2,1,0:T(8,128)(2,1)S(1)} %constant_dynamic-update-slice_fusion), channel_id=1, source_target_pairs={{32,0},{64,32},{96,64},{128,96},{160,128},{192,160},{224,192},{256... | collective-permute-start | bytes 1572872 | tf_op jit(solution)/shard_map/ppermute | solution.py:24
  76.3 14.1 %collective-permute-start.6 = (bf16[2,512,256]{2,1,0:T(8,128)(2,1)S(1)}, bf16[2,512,256]{2,1,0:T(8,128)(2,1)S(1)}, u32[]{:S(2)}, u32[]{:S(2)}) collective-permute-start(bf16[2,512,256]{2,1,0:T(8,128)(2,1)S(1)} %constant_dynamic-update-slice_fusion), channel_id=1, source_target_pairs={{0,32},{32,64},{64,96},{96,128},{128,160},{160,192},{192,224},{224... | collective-permute-start | bytes 1572872 | tf_op jit(solution)/shard_map/ppermute | solution.py:24

commit v2 on v0

v2 whole, which is shorter than its diff:
```python
import math

import jax
import jax.numpy as jnp
from jax import lax
from jax.experimental import pallas as pl
from jax.experimental.pallas import tpu as pltpu
from jax.sharding import PartitionSpec as P

STEPS = 2
step_size = 0.2
BF = jnp.bfloat16
F32 = jnp.float32
VM = pltpu.VMEM


def shift_lon(block, by):
    count = lax.axis_size("lon")
    return lax.ppermute(block, "lon", [(i, (i + by) % count) for i in range(count)])


def swap_lat(block, first):
    count = lax.axis_size("lat")
    pairs = [(i, i + 1) for i in range(first, count - 1, 2)]
    return lax.ppermute(block, "lat", pairs + [(b, a) for a, b in pairs])


def dot(a, b):
    return jnp.dot(a, b, preferred_element_type=F32)


def split(x):
    high = x.astype(BF)
    rest = x - high.astype(F32)
    middle = rest.astype(BF)
    return [high.astype(F32), middle.astype(F32), rest - middle.astype(F32)]


def prepare_kernel(sample_ref, columns_ref, count_ref, obs_ref, ivar_ref, compact_ref, mt_ref):
    compact_ref[...] = sample_ref[...].astype(BF)
    eye = (
        lax.broadcasted_iota(jnp.int32, (256, 256), 0)
        == lax.broadcasted_iota(jnp.int32, (256, 256), 1)
    ).astype(F32).astype(BF)
    slot = lax.broadcasted_iota(jnp.int32, (4, 256), 0)
    for b in range(2):
        codes = lax.dot_general(
            columns_ref[b].astype(F32).astype(BF), eye, (((0,), (0,)), ((), ())),
            preferred_element_type=F32,
        )

        def row(ref):
            return jnp.concatenate([ref[b, c : c + 1, :] for c in range(4)], axis=1)

        codes = jnp.where(slot < row(count_ref), codes, 99.0)
        rows = [codes] + split(row(obs_ref)) + split(row(ivar_ref)) + [jnp.zeros((6, 256), F32)]
        mt_ref[b] = jnp.concatenate(rows, axis=0).astype(BF)


def prior_matrix_kernel(pattern_ref, precision_ref, lp_ref, slot_ref):
    for b in range(2):
        for j in range(4):
            for k in range(9):
                slot_ref[(b * 4 + j) * 9 + pattern_ref[b, j, k]] = k
    blank = jnp.zeros((64, 64), BF)
    for b in range(2):
        for p in range(2):
            for dr in range(3):
                for t in range(2):
                    j = 2 * p + t
                    parts = [
                        precision_ref[b, j, slot_ref[(b * 4 + j) * 9 + dr * 3 + o]]
                        for o in range(3)
                    ]
                    parts = [blank] * t + parts + [blank] * (1 - t)
                    lp_ref[b, p, dr, t * 64 : (t + 1) * 64, :] = jnp.concatenate(parts, axis=1)


def lanes_iota(n):
    return lax.broadcasted_iota(jnp.int32, (1, n), 1) // 64


def build_forward(weights, columns, store):
    for oc in range(6):
        rows = slice(oc * 64, (oc + 1) * 64)
        pair, code = [], []
        for j in range(4):
            one = weights[rows, j * 64 : (j + 1) * 64]
            pair.append(jnp.concatenate([one, one], axis=1))
            code.append(jnp.broadcast_to(columns[rows, j : j + 1], (64, 128)))
        for q in range(2):
            local_oc = oc - 2 * q
            if not 0 <= local_oc < 4:
                continue
            for h in range(2):
                col = lanes_iota(128) + 2 * h - local_oc + 2 * q
                some = any(0 <= 2 * h + x - local_oc + 2 * q <= 2 for x in range(2))
                for dr in range(3):
                    total = jnp.zeros((64, 128), F32)
                    if some:
                        need = jnp.where((col >= 0) & (col <= 2), col + 3 * dr, 77).astype(F32)
                        for j in range(4):
                            total = jnp.where(code[j] == need, pair[j], total)
                    store(q, dr, slice(local_oc * 64, local_oc * 64 + 64), slice(h * 128, h * 128 + 128), total.astype(BF))


def build_adjoint(turned, meta, b, i, store):
    for p in range(2):
        lanes = slice(p * 128, p * 128 + 256)
        for t in range(2):
            col = t - lanes_iota(256) + 2
            need = jnp.where((col >= 0) & (col <= 2), col + 3 * (b - i + 2), 77).astype(F32)
            total = jnp.zeros((64, 256), F32)
            for j in range(4):
                hit = meta[j : j + 1, lanes] == need
                total = jnp.where(hit, turned[j * 64 : (j + 1) * 64, lanes], total)
            store(p, slice(t * 64, t * 64 + 64), total.astype(BF))


def scales(columns):
    obs = columns[:, 4:5] + columns[:, 5:6] + columns[:, 6:7]
    ivar = columns[:, 7:8] + columns[:, 8:9] + columns[:, 9:10]
    return obs, ivar


def forward_into(acc_ref, i, lf, x, fresh):
    for q in range(2):
        term = dot(lf(q), x[q * 256 : (q + 1) * 256, :])
        lo = slice(q * 128, q * 128 + 128)
        hi = slice(q * 128 + 128, q * 128 + 256)
        if fresh and q == 0:
            acc_ref[i, 0:256, :] = term
        elif fresh:
            acc_ref[i, lo, :] += term[:128]
            acc_ref[i, hi, :] = term[128:]
        else:
            acc_ref[i, q * 128 : q * 128 + 256, :] += term


def prior_into(grad_ref, b, dr, lp_ref, x, fresh):
    for p in range(2):
        term = dot(lp_ref[b, p, dr], x[(1 + 2 * p) * 64 : (5 + 2 * p) * 64, :])
        rows = slice(p * 128, p * 128 + 128)
        if fresh:
            grad_ref[b, rows, :] = term
        else:
            grad_ref[b, rows, :] += term


def middle_terms(first, x_ref, lp_ref, lfm_ref, lfo_ref, acc_ref, grad_ref):
    for i, dr, r in ((1, 1, 0), (1, 2, 1), (2, 0, 0), (2, 1, 1)):
        forward_into(
            acc_ref, i, lambda q: lfm_ref[i - 1, q, dr], x_ref[r], (i, dr) in ((1, 1), (2, 0))
        )
    if not first:
        forward_into(acc_ref, 0, lambda q: lfo_ref[0, q, 2], x_ref[0], True)
        forward_into(acc_ref, 3, lambda q: lfo_ref[1, q, 0], x_ref[1], True)
    for b, dr, r in ((0, 1, 0), (0, 2, 1), (1, 0, 0), (1, 1, 1)):
        prior_into(grad_ref, b, dr, lp_ref, x_ref[r], (b, dr) in ((0, 1), (1, 0)))


def middle_first_kernel(x_ref, fw_ref, mt_ref, lp_ref, lfm_ref, lam_ref, acc_ref, grad_ref):
    for k in range(2):
        i = k + 1
        meta = mt_ref[k].astype(F32)
        columns = jnp.transpose(meta, (1, 0))
        weights = fw_ref[k].astype(F32)

        def put(q, dr, rows, lanes, value):
            lfm_ref[k, q, dr, rows, lanes] = value

        build_forward(weights, columns, put)
        turned = jnp.transpose(weights, (1, 0))
        for b in range(2):

            def put_adjoint(p, rows, value):
                lam_ref[k, b, p, rows, :] = value

            build_adjoint(turned, meta, b, i, put_adjoint)
    middle_terms(True, x_ref, lp_ref, lfm_ref, None, acc_ref, grad_ref)


def middle_last_kernel(x_ref, lp_ref, lfm_ref, lfo_ref, acc_ref, grad_ref):
    middle_terms(False, x_ref, lp_ref, lfm_ref, lfo_ref, acc_ref, grad_ref)


def finish_kernel(first, *refs):
    (side_ref, x_ref, far_ref, pair_ref, halo_ref, mtm_ref, lp_ref, lfm_ref, lam_ref) = refs[:9]
    if first:
        acc_in, grad_in, sample_ref, noise_ref = refs[9:13]
        out_ref, compact_ref, lfo_ref, lao_ref, mto_ref = refs[13:18]
        lines_ref, res_ref, acc_ref, grad_ref = refs[18:]
    else:
        lfo_ref, lao_ref, mto_ref, acc_in, grad_in, sample_ref, noise_ref = refs[9:16]
        out_ref = refs[16]
        lines_ref, res_ref, acc_ref, grad_ref = refs[17:]
    side = side_ref[0]
    for r in range(2):
        lines_ref[0, r] = far_ref[r * 512 : (r + 1) * 512, :]
        lines_ref[1, r, 0:128, :] = halo_ref[r * 256 : r * 256 + 128, :]
        lines_ref[1, r, 128:384, :] = pair_ref[1 - side, r]
        lines_ref[1, r, 384:512, :] = halo_ref[r * 256 + 128 : r * 256 + 256, :]

    acc_ref[1:3] = acc_in[1:3]
    if not first:
        acc_ref[0] = acc_in[0]
        acc_ref[3] = acc_in[3]
    grad_ref[...] = grad_in[...]

    def line(w):
        if w < 2:
            return lines_ref.at[side, w]
        if w < 4:
            return x_ref.at[w - 2]
        return lines_ref.at[1 - side, w - 4]

    if first:
        for k in range(2):
            i = 3 * k
            near = (side == 0) if k == 0 else (side == 1)

            foot = jnp.where(near, far_ref[1024:1440, :], halo_ref[512:928, :])
            weights = foot[0:384].astype(F32)
            meta = jnp.concatenate([foot[384:400], foot[400:416, :128]], axis=1).astype(F32)
            mto_ref[k] = meta.astype(BF)

            def put(q, dr, rows, lanes, value):
                lfo_ref[k, q, dr, rows, lanes] = value

            build_forward(weights, jnp.transpose(meta, (1, 0)), put)

            def put_adjoint(p, rows, value):
                lao_ref[k, p, rows, :] = value

            build_adjoint(jnp.transpose(weights, (1, 0)), meta, k, i, put_adjoint)

    for i in range(4):
        edge = i in (0, 3)
        for dr in range(3):
            w = i + dr
            if w in (2, 3) and not (first and edge):
                continue
            source = (lambda q: lfo_ref[i // 3, q, dr]) if edge else (lambda q: lfm_ref[i - 1, q, dr])
            forward_into(acc_ref, i, source, line(w), first and edge and dr == 0)
        meta = (mto_ref[i // 3] if edge else mtm_ref[i - 1]).astype(F32)
        obs, ivar = scales(jnp.transpose(meta, (1, 0)))
        res_ref[i] = (ivar * (acc_ref[i] - obs)).astype(BF)
    for b in range(2):
        dr = 0 if b == 0 else 2
        prior_into(grad_ref, b, dr, lp_ref, line(b + 1 + dr), False)
        for p in range(2):
            rows = slice(p * 128, (p + 1) * 128)
            acc = grad_ref[b, rows, :]
            for i in range(b, b + 3):
                left = lao_ref[i // 3, p] if i in (0, 3) else lam_ref[i - 1, b, p]
                acc = acc + dot(left, res_ref[i, p * 128 : p * 128 + 256, :])
            value = (
                sample_ref[b, rows, :]
                - step_size * acc
                + math.sqrt(2.0 * step_size) * noise_ref[b, rows, :].astype(F32)
            )
            out_ref[b, rows, :] = value
            if first:
                compact_ref[b, rows, :] = value.astype(BF)


def shape(dims, dtype=BF):
    return jax.ShapeDtypeStruct(dims, dtype)


def call(kernel, name, outs, args, scratch=(), scalars=0, flops=0, moved=0):
    spec = pl.BlockSpec(memory_space=VM)
    return pl.pallas_call(
        kernel,
        name=name,
        out_shape=tuple(outs),
        in_specs=[pl.BlockSpec(memory_space=pltpu.SMEM)] * scalars + [spec] * (len(args) - scalars),
        out_specs=tuple([spec] * len(outs)),
        scratch_shapes=list(scratch),
        compiler_params=pltpu.CompilerParams(vmem_limit_bytes=16 * 1024 * 1024),
        cost_estimate=pl.CostEstimate(flops=flops, bytes_accessed=moved, transcendentals=0),
    )(*args)


def finish(first, args):
    outs = [shape((2, 256, 256), F32)]
    if first:
        outs += [
            shape((2, 256, 256)),
            shape((2, 2, 3, 256, 256)),
            shape((2, 2, 128, 256)),
            shape((2, 16, 384)),
        ]
    return call(
        lambda *refs: finish_kernel(first, *refs),
        "finish_first" if first else "finish_last",
        outs,
        args,
        scratch=[
            pltpu.VMEM((2, 2, 512, 256), BF),
            pltpu.VMEM((4, 384, 256), BF),
            pltpu.VMEM((4, 384, 256), F32),
            pltpu.VMEM((2, 256, 256), F32),
        ],
        scalars=1,
        flops=800000000,
        moved=5000000,
    )


def local(
    sample_field,
    langevin_noise,
    precision,
    pattern,
    foot_weight,
    foot_columns,
    foot_count,
    observed,
    inverse_var,
):
    side = lax.axis_index("lat") % 2
    sides = jnp.full((1,), side, jnp.int32)
    sample = sample_field.reshape(2, 256, 256)
    noise = langevin_noise.reshape(STEPS, 2, 256, 256)
    fw = foot_weight.reshape(2, 256, 256)
    compact, mt = call(
        prepare_kernel,
        "prepare",
        [shape((2, 256, 256)), shape((2, 16, 256))],
        (sample, foot_columns.reshape(2, 256, 4), foot_count, observed, inverse_var),
        flops=1000000,
        moved=1000000,
    )

    def edge(cells, col):
        meta = jnp.pad(mt[:, :, col * 64 : (col + 1) * 64], ((0, 0), (0, 0), (0, 192)))
        return jnp.concatenate([compact[:, cells], fw[:, col * 64 : (col + 1) * 64], meta], axis=1)

    west = shift_lon(edge(slice(128, 256), 3), 1)
    (lp,) = call(
        prior_matrix_kernel,
        "prior_matrix",
        [shape((2, 2, 3, 128, 256))],
        (pattern, precision),
        scratch=[pltpu.SMEM((72,), jnp.int32)],
        scalars=1,
        flops=2000000,
        moved=3000000,
    )
    leaving, lp = lax.optimization_barrier((edge(slice(0, 128), 0), lp))
    east = shift_lon(leaving, -1)
    middle = jnp.concatenate([west[:, :128], compact, east[:, :128]], axis=1)
    fw = jnp.concatenate([west[:, 128:192], fw, east[:, 128:192]], axis=1)
    mt = jnp.concatenate([west[:, 192:, :64], mt, east[:, 192:, :64]], axis=2)

    def foot_row(row):
        meta = jnp.pad(mt[row], ((0, 0), (0, 128)))
        return jnp.concatenate([fw[row], meta[:, :256], meta[:, 256:]], axis=0)

    foot = jnp.stack([foot_row(0), foot_row(1)])
    far_foot = jnp.where(side == 0, foot[0], foot[1])
    mate_foot = jnp.where(side == 0, foot[1], foot[0])

    def lat_exchange(compact, middle, west, east, far_extra, mate_extra):
        far = swap_lat(jnp.concatenate([middle.reshape(1024, 256)] + far_extra, axis=0), 1)
        halo = jnp.concatenate([west, east], axis=1).reshape(512, 256)
        halo = swap_lat(jnp.concatenate([halo] + mate_extra, axis=0), 0)
        count = lax.axis_size("lat")
        pair = lax.all_gather(
            compact, "lat", axis_index_groups=[[i, i + 1] for i in range(0, count, 2)]
        )
        return far, pair, halo

    far, pair, halo = lat_exchange(
        compact, middle, west[:, :128], east[:, :128], [far_foot], [mate_foot]
    )
    lfm, lam, acc, grad = call(
        middle_first_kernel,
        "middle_first",
        [
            shape((2, 2, 3, 256, 256)),
            shape((2, 2, 2, 128, 256)),
            shape((4, 384, 256), F32),
            shape((2, 256, 256), F32),
        ],
        (middle, fw, mt, lp),
        flops=600000000,
        moved=20000000,
    )
    sample, compact, lfo, lao, mto = finish(
        True,
        (sides, middle, far, pair, halo, mt, lp, lfm, lam, acc, grad, sample, noise[0]),
    )

    west = shift_lon(compact[:, 128:], 1)
    east = shift_lon(compact[:, :128], -1)
    middle = jnp.concatenate([west, compact, east], axis=1)
    far, pair, halo = lat_exchange(compact, middle, west, east, [], [])
    acc, grad = call(
        middle_last_kernel,
        "middle_last",
        [shape((4, 384, 256), F32), shape((2, 256, 256), F32)],
        (middle, lp, lfm, lfo),
        flops=600000000,
        moved=20000000,
    )
    (sample,) = finish(
        False,
        (sides, middle, far, pair, halo, mt, lp, lfm, lam, lfo, lao, mto, acc, grad, sample, noise[1]),
    )
    return sample.reshape(sample_field.shape)


def solution(mesh):
    placed = (
        P("lat", "lon", None, None),
        P(None, "lat", "lon", None, None),
        P("lat", "lon", None, None, None),
        P("lat", "lon", None),
        P("lat", "lon", None, None, None),
        P("lat", "lon", None, None),
        P("lat", "lon", None),
        P("lat", "lon", None),
        P("lat", "lon", None),
    )
    return jax.shard_map(
        local, mesh=mesh, in_specs=placed, out_specs=P("lat", "lon", None, None), check_vma=False
    )
```

time: 167 us -> 72.2 us (0.43)
  waiting for transfers between devices: 53.6 us -> 19.5 us
  matrix products: 21.3 us -> 0 us
  starting transfers between devices: 53.8 us -> 33.1 us
  local copies, waits for them, and re-layouts: 21.5 us -> 4.8 us
  other arithmetic: 15.1 us -> 0.39 us
  Pallas kernels: 0 us -> 8.87 us
  blocking collectives: 0 us -> 4.61 us
    ppermute x16 -> x8, waiting for transfers between devices: 53.6 us -> 19.5 us  [the longest x4 12.5 us: swap_lat(): return lax.ppermute(block, 'lat', pairs + [(b, a) for a, b in pairs])]
    ppermute x16 -> x8, starting transfers between devices: 53.8 us -> 33.1 us  [the longest x4 22.4 us: shift_lon(): lax.ppermute(block, 'lon', [(i, (i + by) % count) for i in range(count)])]
    dot_general x4 -> x0, matrix products: 11.2 us -> none  [the longest x2 5.62 us: local(): jnp.einsum('abocd,oabds->abcs', ordered, shifted, preferred_element_type=...]
    unnamed x2 -> x0, matrix products: 10.1 us -> none
    pallas_call x0 -> x6, Pallas kernels: none -> 8.87 us  [call(): pl.pallas_call(kernel, name=name, out_shape=tuple(outs), in_specs=[pl.Blo...]
    scatter-add x24 -> x0, other arithmetic: 8.33 us -> none  [the longest x16 7.97 us: local(): partial_grid = partial_grid.at[offset // 3:offset // 3 + band_height, off...]
    unnamed x33 -> x19, local copies, waits for them, and re-layouts: 9.01 us -> 2.97 us
    dot_general x2 -> x0, local copies, waits for them, and re-layouts: 5.81 us -> none  [local(): jnp.einsum('abfoc,abfs->oabcs', foot_matrix, residual, preferred_element_...]
  transfers between devices with their start and end apart: 16 -> 8, of which waited for: 12 -> 6; matrix products, arithmetic and copies ran while one was open for 8% -> 0% of each run, Pallas kernels for 0% -> 5%
where the time goes in v2:
time: 72.2 us; the launch traced here: 71.6 us
  starting transfers between devices  33.1 us (46%)
  waiting for transfers between devices  19.5 us (27%)
  Pallas kernels  8.87 us (12%)
  local copies, waits for them, and re-layouts  4.8 us (7%)
  blocking collectives  4.61 us (6%)
    ppermute x4, starting transfers between devices, shift_lon(): lax.ppermute(block, 'lon', [(i, (i + by) % count) for i in range(count)])  22.4 us
    ppermute x4, waiting for transfers between devices, swap_lat(): return lax.ppermute(block, 'lat', pairs + [(b, a) for a, b in pairs])  12.5 us
    ppermute x4, starting transfers between devices, swap_lat(): return lax.ppermute(block, 'lat', pairs + [(b, a) for a, b in pairs])  10.7 us
    pallas_call x6, Pallas kernels, call(): pl.pallas_call(kernel, name=name, out_shape=tuple(outs), in_specs=[pl.Blo...  8.87 us
    ppermute x4, waiting for transfers between devices, shift_lon(): lax.ppermute(block, 'lon', [(i, (i + by) % count) for i in range(count)])  6.93 us
    all_gather x2, blocking collectives, lat_exchange(): lax.all_gather(compact, 'lat', axis_index_groups=[[i, i + 1] for i in ran...  4.61 us
    unnamed x19, local copies, waits for them, and re-layouts  2.97 us
    reshape x1, local copies, waits for them, and re-layouts, local(): fw = foot_weight.reshape(2, 256, 256)  1.58 us
  transfers between devices with their start and end apart: 8, of which 6 were waited for; matrix products, arithmetic and copies ran while one was open for 0% of the time, Pallas kernels for 5%

profile of v2, /device:TPU:4, one launch (start us, length us, event | category | flops | bytes accessed | tf_op | source)
XLA Modules:
  0.0 71.6 jit_solution(12425981124469865727)
XLA Ops:
  0.0 0.0 copy-start.7
  0.0 0.0 copy-start
  0.0 0.0 copy-start.1
  0.0 1.6 %reshape.31 = bf16[2,256,256]{2,1,0:T(8,128)(2,1)S(1)} reshape(bf16[2,4,64,4,64]{4,3,2,1,0:T(4,128)(2,1)} %param.13) | data formatting | bytes 524288 | tf_op jit(solution)/shard_map/reshape | solution.py:326
  1.6 0.9 %copy.11 = s32[2,4,64,4]{3,2,1,0:T(8,128)S(1)} copy(s32[2,4,64,4]{2,3,1,0:T(4,128)} %param.14) | data formatting | bytes 16384 | tf_op args[5]
  2.5 0.0 copy-done
  2.5 0.0 copy-start.2
  2.5 0.7 copy-done.2
  3.2 0.0 copy-start.3
  3.2 0.7 copy-done.3
  3.9 0.0 copy-start.4
  3.9 0.7 copy-done.4
  4.6 0.0 copy-start.5
  4.6 0.2 prepare.1
  4.8 0.1 slice.79
  4.9 3.1 %collective-permute-start = (bf16[2,208,256]{2,1,0:T(8,128)(2,1)S(1)}, bf16[2,208,256]{2,1,0:T(8,128)(2,1)S(1)}, u32[]{:S(2)}, u32[]{:S(2)}) collective-permute-start(bf16[2,208,256]{2,1,0:T(8,128)(2,1)S(1)} %fusion.1), channel_id=1, source_target_pairs={{0,1},{1,2},{2,3},{3,4},{4,5},{5,6},{6,7},{7,8},{8,9},{9,10},{10,1... | collective-permute-start | bytes 638984 | tf_op jit(solution)/shard_map/ppermute | solution.py:19
  8.0 0.0 copy-done.7
  8.0 0.0 copy-done.1
  8.0 0.0 copy-done.5
  8.0 0.9 %prior_matrix.1.lp_ref.refs_6_ = bf16[2,2,3,128,256]{4,3,2,1,0:T(8,128)(2,1)S(1)} custom-call(s32[2,4,9]{2,1,0:T(4,128)S(1)} %copy-done.5, bf16[2,4,9,64,64]{4,3,2,1,0:T(8,128)(2,1)S(1)} %copy-done.1), custom_call_target="tpu_custom_call" | custom-call | flops 2000000 | bytes 3000000 | tf_op jit(solution)/shard_map/prior_matrix/pallas_call | solution.py:273
  9.0 10.9 %collective-permute-start.1 = (bf16[2,208,256]{2,1,0:T(8,128)(2,1)S(1)}, bf16[2,208,256]{2,1,0:T(8,128)(2,1)S(1)}, u32[]{:S(2)}, u32[]{:S(2)}) collective-permute-start(bf16[2,208,256]{2,1,0:T(8,128)(2,1)S(1)} %pad_maximum_fusion.6), channel_id=1, source_target_pairs={{0,31},{1,0},{2,1},{3,2},{4,3},{5,4},{6,5},{7,6},{8,7},{9,8},{10,9... | collective-permute-start | bytes 638984 | tf_op jit(solution)/shard_map/ppermute | solution.py:19
  19.8 2.4 %collective-permute-done = bf16[2,208,256]{2,1,0:T(8,128)(2,1)S(1)} collective-permute-done((bf16[2,208,256]{2,1,0:T(8,128)(2,1)S(1)}, bf16[2,208,256]{2,1,0:T(8,128)(2,1)S(1)}, u32[]{:S(2)}, u32[]{:S(2)}) %collective-permute-start) | collective-permute-done | bytes 213024 | tf_op jit(solution)/shard_map/ppermute | solution.py:19
  22.3 2.0 %collective-permute-done.1 = bf16[2,208,256]{2,1,0:T(8,128)(2,1)S(1)} collective-permute-done((bf16[2,208,256]{2,1,0:T(8,128)(2,1)S(1)}, bf16[2,208,256]{2,1,0:T(8,128)(2,1)S(1)}, u32[]{:S(2)}, u32[]{:S(2)}) %collective-permute-start.1) | collective-permute-done | bytes 213024 | tf_op jit(solution)/shard_map/ppermute | solution.py:19
  24.3 0.1 pad_maximum_fusion.9.mt_ref.refs_5_
  24.6 0.1 broadcast_select_fusion
  24.7 0.0 copy-start.6
  24.7 0.1 pad_maximum_fusion
  24.8 3.9 %collective-permute-start.2 = (bf16[1440,256]{1,0:T(8,128)(2,1)S(1)}, bf16[1440,256]{1,0:T(8,128)(2,1)S(1)}, u32[]{:S(2)}, u32[]{:S(2)}) collective-permute-start(bf16[1440,256]{1,0:T(8,128)(2,1)S(1)} %pad_maximum_fusion), channel_id=1, source_target_pairs={{32,64},{96,128},{160,192},{224,256},{288,320},{352,384},{416,448}... | collective-permute-start | bytes 2211848 | tf_op jit(solution)/shard_map/ppermute | solution.py:25
  28.7 1.9 %collective-permute-start.3 = (bf16[928,256]{1,0:T(8,128)(2,1)S(1)}, bf16[928,256]{1,0:T(8,128)(2,1)S(1)}, u32[]{:S(2)}, u32[]{:S(2)}) collective-permute-start(bf16[928,256]{1,0:T(8,128)(2,1)S(1)} %pad_maximum_fusion.2), channel_id=1, source_target_pairs={{0,32},{64,96},{128,160},{192,224},{256,288},{320,352},{384,416},{... | collective-permute-start | bytes 1425416 | tf_op jit(solution)/shard_map/ppermute | solution.py:25
  30.6 2.3 %all-gather = bf16[4,256,256]{2,1,0:T(8,128)(2,1)S(1)} all-gather(bf16[2,256,256]{2,1,0:T(8,128)(2,1)S(1)} %get-tuple-element.20), channel_id=2, replica_groups={{0,32},{64,96},{128,160},{192,224},{256,288},{320,352},{384,416},{448,4..., dimensions={0}, use_global_device_ids=true | all-gather | bytes 786432 | tf_op jit(solution)/shard_map/all_gather | solution.py:370
  32.9 0.0 copy-done.6
  33.0 1.8 %middle_first.1 = (bf16[2,2,3,256,256]{4,3,2,1,0:T(8,128)(2,1)S(1)}, bf16[2,2,2,128,256]{4,3,2,1,0:T(8,128)(2,1)S(1)}, f32[4,384,256]{2,1,0:T(8,128)S(1)}, f32[2,256,256]{2,1,0:T(8,128)S(1)}) custom-call(bf16[2,512,256]{2,1,0:T(8,128)(2,1)S(1)} %pad_maximum_fusion.1.x_ref.refs_1_, bf16[2,384,256]{2,1,0:T(8,128)(2,1)S(1)} %pad_maximum_fusion.3.fw_ref, ...), custom_call_target="tpu_custom_call" | custom-call | flops 600000000 | bytes 20000000 | tf_op jit(solution)/shard_map/middle_first/pallas_call | solution.py:273
  34.8 0.0 collective-permute-done.3.refs_4_
  34.8 6.5 %collective-permute-done.2.refs_2_ = bf16[1440,256]{1,0:T(8,128)(2,1)S(1)} collective-permute-done((bf16[1440,256]{1,0:T(8,128)(2,1)S(1)}, bf16[1440,256]{1,0:T(8,128)(2,1)S(1)}, u32[]{:S(2)}, u32[]{:S(2)}) %collective-permute-start.2) | collective-permute-done | bytes 737312 | tf_op jit(solution)/shard_map/ppermute | solution.py:25
  41.3 2.9 %finish_first.1 = (f32[2,256,256]{2,1,0:T(8,128)S(1)}, bf16[2,256,256]{2,1,0:T(8,128)(2,1)S(1)}, bf16[2,2,3,256,256]{4,3,2,1,0:T(8,128)(2,1)S(1)}, bf16[2,2,128,...) custom-call(s32[1]{0:T(128)} %bitcast.refs_0_, bf16[2,512,256]{2,1,0:T(8,128)(2,1)S(1)} %pad_maximum_fusion.1.x_ref.refs_1_, ...), custom_call_target="tpu_custom_call" | custom-call | flops 800000000 | bytes 5000000 | tf_op jit(solution)/shard_map/finish_first/pallas_call | solution.py:273
  44.2 1.9 %collective-permute-start.4 = (bf16[2,128,256]{2,1,0:T(8,128)(2,1)S(1)}, bf16[2,128,256]{2,1,0:T(8,128)(2,1)S(1)}, u32[]{:S(2)}, u32[]{:S(2)}) collective-permute-start(bf16[2,128,256]{2,1,0:T(8,128)(2,1)S(1)} %get-tuple-element.42), channel_id=1, source_target_pairs={{0,1},{1,2},{2,3},{3,4},{4,5},{5,6},{6,7},{7,8},{8,9},{9,10},{10,1... | collective-permute-start | bytes 393224 | tf_op jit(solution)/shard_map/ppermute | solution.py:19
  46.2 6.5 %collective-permute-start.5 = (bf16[2,128,256]{2,1,0:T(8,128)(2,1)S(1)}, bf16[2,128,256]{2,1,0:T(8,128)(2,1)S(1)}, u32[]{:S(2)}, u32[]{:S(2)}) collective-permute-start(bf16[2,128,256]{2,1,0:T(8,128)(2,1)S(1)} %get-tuple-element.41), channel_id=1, source_target_pairs={{0,31},{1,0},{2,1},{3,2},{4,3},{5,4},{6,5},{7,6},{8,7},{9,8},{10,9... | collective-permute-start | bytes 393224 | tf_op jit(solution)/shard_map/ppermute | solution.py:19
  52.7 1.1 %collective-permute-done.4 = bf16[2,128,256]{2,1,0:T(8,128)(2,1)S(1)} collective-permute-done((bf16[2,128,256]{2,1,0:T(8,128)(2,1)S(1)}, bf16[2,128,256]{2,1,0:T(8,128)(2,1)S(1)}, u32[]{:S(2)}, u32[]{:S(2)}) %collective-permute-start.4) | collective-permute-done | bytes 131104 | tf_op jit(solution)/shard_map/ppermute | solution.py:19
  53.8 1.3 %collective-permute-done.5 = bf16[2,128,256]{2,1,0:T(8,128)(2,1)S(1)} collective-permute-done((bf16[2,128,256]{2,1,0:T(8,128)(2,1)S(1)}, bf16[2,128,256]{2,1,0:T(8,128)(2,1)S(1)}, u32[]{:S(2)}, u32[]{:S(2)}) %collective-permute-start.5) | collective-permute-done | bytes 131104 | tf_op jit(solution)/shard_map/ppermute | solution.py:19
  55.2 3.0 %collective-permute-start.6 = (bf16[1024,256]{1,0:T(8,128)(2,1)S(1)}, bf16[1024,256]{1,0:T(8,128)(2,1)S(1)}, u32[]{:S(2)}, u32[]{:S(2)}) collective-permute-start(bf16[1024,256]{1,0:T(8,128)(2,1)S(1)} %bitcast.21), channel_id=1, source_target_pairs={{32,64},{96,128},{160,192},{224,256},{288,320},{352,384},{416,448}... | collective-permute-start | bytes 1572872 | tf_op jit(solution)/shard_map/ppermute | solution.py:25
  58.3 1.9 %collective-permute-start.7 = (bf16[512,256]{1,0:T(8,128)(2,1)S(1)}, bf16[512,256]{1,0:T(8,128)(2,1)S(1)}, u32[]{:S(2)}, u32[]{:S(2)}) collective-permute-start(bf16[512,256]{1,0:T(8,128)(2,1)S(1)} %bitcast.30), channel_id=1, source_target_pairs={{0,32},{64,96},{128,160},{192,224},{256,288},{320,352},{384,416},{... | collective-permute-start | bytes 786440 | tf_op jit(solution)/shard_map/ppermute | solution.py:25
  60.2 2.3 %all-gather.1 = bf16[4,256,256]{2,1,0:T(8,128)(2,1)S(1)} all-gather(bf16[2,256,256]{2,1,0:T(8,128)(2,1)S(1)} %get-tuple-element.28), channel_id=3, replica_groups={{0,32},{64,96},{128,160},{192,224},{256,288},{320,352},{384,416},{448,4..., dimensions={0}, use_global_device_ids=true | all-gather | bytes 786432 | tf_op jit(solution)/shard_map/all_gather | solution.py:370
  62.5 0.7 middle_last.1
  63.2 0.0 collective-permute-done.7.refs_4_
  63.2 6.1 %collective-permute-done.6.refs_2_ = bf16[1024,256]{1,0:T(8,128)(2,1)S(1)} collective-permute-done((bf16[1024,256]{1,0:T(8,128)(2,1)S(1)}, bf16[1024,256]{1,0:T(8,128)(2,1)S(1)}, u32[]{:S(2)}, u32[]{:S(2)}) %collective-permute-start.6) | collective-permute-done | bytes 524320 | tf_op jit(solution)/shard_map/ppermute | solution.py:25
  69.3 2.4 %finish_last.1 = f32[2,256,256]{2,1,0:T(8,128)} custom-call(s32[1]{0:T(128)} %bitcast.refs_0_, bf16[2,512,256]{2,1,0:T(8,128)(2,1)S(1)} %constant_dynamic-update-slice_fusion.x_ref.refs_1_, bf16[1024,256]{1,0:T(8,128)(2,1)S(1)} %collective-permute-done.6.refs_2_, bf16[2,2,256,256]{3,2,1,0:T(8,128)(2,1)S(1)} %bitcast.25, ...), custom_call_target="tpu_custom_call" | custom-call | flops 800000000 | bytes 5000000 | tf_op jit(solution)/shard_map/finish_last/pallas_call | solution.py:273
  (24 shorter events, 0.4 us)
Async XLA Ops:
  0.0 8.0 %copy-start.7 = (pred[256]{0:T(512)(128)(4,1)S(1)}, pred[256]{0:T(512)(128)(4,1)}, u32[]{:S(2)}) copy-start(pred[256]{0:T(512)(128)(4,1)} %constant.23.clone.1) | copy-start | bytes 772
  0.0 2.5 %copy-start = (f32[2,4,64,256]{3,2,1,0:T(8,128)S(1)}, f32[2,4,64,256]{3,2,1,0:T(8,128)}, u32[]{:S(2)}) copy-start(f32[2,4,64,256]{3,2,1,0:T(8,128)} %param.9) | copy-start | bytes 1572868
  0.0 8.0 %copy-start.1 = (bf16[2,4,9,64,64]{4,3,2,1,0:T(8,128)(2,1)S(1)}, bf16[2,4,9,64,64]{4,3,2,1,0:T(8,128)(2,1)}, u32[]{:S(2)}) copy-start(bf16[2,4,9,64,64]{4,3,2,1,0:T(8,128)(2,1)} %precision_ref.1) | copy-start | bytes 1769476
  2.5 0.7 copy-start.2
  3.2 0.7 copy-start.3
  3.9 0.7 copy-start.4
  4.6 3.5 %copy-start.5 = (s32[2,4,9]{2,1,0:T(4,128)S(1)}, s32[2,4,9]{2,1,0:T(4,128)}, u32[]{:S(2)}) copy-start(s32[2,4,9]{2,1,0:T(4,128)} %pattern_ref.1) | copy-start | bytes 868
  4.9 17.4 %collective-permute-start = (bf16[2,208,256]{2,1,0:T(8,128)(2,1)S(1)}, bf16[2,208,256]{2,1,0:T(8,128)(2,1)S(1)}, u32[]{:S(2)}, u32[]{:S(2)}) collective-permute-start(bf16[2,208,256]{2,1,0:T(8,128)(2,1)S(1)} %fusion.1), channel_id=1, source_target_pairs={{0,1},{1,2},{2,3},{3,4},{4,5},{5,6},{6,7},{7,8},{8,9},{9,10},{10,1... | collective-permute-start | bytes 638984 | tf_op jit(solution)/shard_map/ppermute | solution.py:19
  9.0 15.3 %collective-permute-start.1 = (bf16[2,208,256]{2,1,0:T(8,128)(2,1)S(1)}, bf16[2,208,256]{2,1,0:T(8,128)(2,1)S(1)}, u32[]{:S(2)}, u32[]{:S(2)}) collective-permute-start(bf16[2,208,256]{2,1,0:T(8,128)(2,1)S(1)} %pad_maximum_fusion.6), channel_id=1, source_target_pairs={{0,31},{1,0},{2,1},{3,2},{4,3},{5,4},{6,5},{7,6},{8,7},{9,8},{10,9... | collective-permute-start | bytes 638984 | tf_op jit(solution)/shard_map/ppermute | solution.py:19
  24.7 8.2 %copy-start.6 = (bf16[2,2,4,64,256]{4,3,2,1,0:T(8,128)(2,1)S(1)}, bf16[2,2,4,64,256]{4,3,2,1,0:T(8,128)(2,1)}, u32[]{:S(2)}) copy-start(bf16[2,2,4,64,256]{4,3,2,1,0:T(8,128)(2,1)} %param.10) | copy-start | bytes 1572868
  24.8 16.5 %collective-permute-start.2 = (bf16[1440,256]{1,0:T(8,128)(2,1)S(1)}, bf16[1440,256]{1,0:T(8,128)(2,1)S(1)}, u32[]{:S(2)}, u32[]{:S(2)}) collective-permute-start(bf16[1440,256]{1,0:T(8,128)(2,1)S(1)} %pad_maximum_fusion), channel_id=1, source_target_pairs={{32,64},{96,128},{160,192},{224,256},{288,320},{352,384},{416,448}... | collective-permute-start | bytes 2211848 | tf_op jit(solution)/shard_map/ppermute | solution.py:25
  28.7 6.1 %collective-permute-start.3 = (bf16[928,256]{1,0:T(8,128)(2,1)S(1)}, bf16[928,256]{1,0:T(8,128)(2,1)S(1)}, u32[]{:S(2)}, u32[]{:S(2)}) collective-permute-start(bf16[928,256]{1,0:T(8,128)(2,1)S(1)} %pad_maximum_fusion.2), channel_id=1, source_target_pairs={{0,32},{64,96},{128,160},{192,224},{256,288},{320,352},{384,416},{... | collective-permute-start | bytes 1425416 | tf_op jit(solution)/shard_map/ppermute | solution.py:25
  44.2 9.5 %collective-permute-start.4 = (bf16[2,128,256]{2,1,0:T(8,128)(2,1)S(1)}, bf16[2,128,256]{2,1,0:T(8,128)(2,1)S(1)}, u32[]{:S(2)}, u32[]{:S(2)}) collective-permute-start(bf16[2,128,256]{2,1,0:T(8,128)(2,1)S(1)} %get-tuple-element.42), channel_id=1, source_target_pairs={{0,1},{1,2},{2,3},{3,4},{4,5},{5,6},{6,7},{7,8},{8,9},{9,10},{10,1... | collective-permute-start | bytes 393224 | tf_op jit(solution)/shard_map/ppermute | solution.py:19
  46.2 9.0 %collective-permute-start.5 = (bf16[2,128,256]{2,1,0:T(8,128)(2,1)S(1)}, bf16[2,128,256]{2,1,0:T(8,128)(2,1)S(1)}, u32[]{:S(2)}, u32[]{:S(2)}) collective-permute-start(bf16[2,128,256]{2,1,0:T(8,128)(2,1)S(1)} %get-tuple-element.41), channel_id=1, source_target_pairs={{0,31},{1,0},{2,1},{3,2},{4,3},{5,4},{6,5},{7,6},{8,7},{9,8},{10,9... | collective-permute-start | bytes 393224 | tf_op jit(solution)/shard_map/ppermute | solution.py:19
  55.2 14.1 %collective-permute-start.6 = (bf16[1024,256]{1,0:T(8,128)(2,1)S(1)}, bf16[1024,256]{1,0:T(8,128)(2,1)S(1)}, u32[]{:S(2)}, u32[]{:S(2)}) collective-permute-start(bf16[1024,256]{1,0:T(8,128)(2,1)S(1)} %bitcast.21), channel_id=1, source_target_pairs={{32,64},{96,128},{160,192},{224,256},{288,320},{352,384},{416,448}... | collective-permute-start | bytes 1572872 | tf_op jit(solution)/shard_map/ppermute | solution.py:25
  58.3 5.0 %collective-permute-start.7 = (bf16[512,256]{1,0:T(8,128)(2,1)S(1)}, bf16[512,256]{1,0:T(8,128)(2,1)S(1)}, u32[]{:S(2)}, u32[]{:S(2)}) collective-permute-start(bf16[512,256]{1,0:T(8,128)(2,1)S(1)} %bitcast.30), channel_id=1, source_target_pairs={{0,32},{64,96},{128,160},{192,224},{256,288},{320,352},{384,416},{... | collective-permute-start | bytes 786440 | tf_op jit(solution)/shard_map/ppermute | solution.py:25

commit v3 on v2

v3 whole, which is shorter than its diff:
```python
import math

import jax
import jax.numpy as jnp
from jax import lax
from jax.experimental import pallas as pl
from jax.experimental.pallas import tpu as pltpu
from jax.sharding import PartitionSpec as P

STEPS = 2
step_size = 0.2
BF = jnp.bfloat16
F32 = jnp.float32
VM = pltpu.VMEM


def shift_lon(block, by):
    count = lax.axis_size("lon")
    return lax.ppermute(block, "lon", [(i, (i + by) % count) for i in range(count)])


def swap_lat(block, first):
    count = lax.axis_size("lat")
    pairs = [(i, i + 1) for i in range(first, count - 1, 2)]
    return lax.ppermute(block, "lat", pairs + [(b, a) for a, b in pairs])


def dot(a, b):
    return jnp.dot(a, b, preferred_element_type=F32)


def split(x):
    high = x.astype(BF)
    rest = x - high.astype(F32)
    middle = rest.astype(BF)
    return [high.astype(F32), middle.astype(F32), rest - middle.astype(F32)]


def prepare_kernel(sample_ref, stats_ref, fw_ref, compact_ref, mt_ref, west_ref, east_ref):
    slot = lax.broadcasted_iota(jnp.int32, (4, 256), 0).astype(F32)
    for b in range(2):
        stats = jnp.concatenate([stats_ref[b, c] for c in range(4)], axis=1)
        codes = jnp.where(slot < stats[4:5], stats[0:4], 99.0)
        rows = [codes] + split(stats[5:6]) + split(stats[6:7]) + [jnp.zeros((6, 256), F32)]
        meta = jnp.concatenate(rows, axis=0).astype(BF)
        mt_ref[b] = meta
        compact = sample_ref[b].astype(BF)
        compact_ref[b] = compact
        west_ref[b, 0:128, :] = compact[128:256]
        east_ref[b, 0:128, :] = compact[0:128]
        west_ref[b, 128:192, :] = fw_ref[b, 192:256, :]
        east_ref[b, 128:192, :] = fw_ref[b, 0:64, :]
        west_ref[b, 192:208, :] = jnp.concatenate([meta[:, 192:256]] * 4, axis=1)
        east_ref[b, 192:208, :] = meta


def prior_matrix_kernel(pattern_ref, precision_ref, lp_ref, slot_ref):
    for b in range(2):
        for j in range(4):
            for k in range(9):
                slot_ref[(b * 4 + j) * 9 + pattern_ref[b, j, k]] = k
    blank = jnp.zeros((64, 64), BF)
    for b in range(2):
        for p in range(2):
            for dr in range(3):
                for t in range(2):
                    j = 2 * p + t
                    parts = [
                        precision_ref[b, j, slot_ref[(b * 4 + j) * 9 + dr * 3 + o]]
                        for o in range(3)
                    ]
                    parts = [blank] * t + parts + [blank] * (1 - t)
                    lp_ref[b, p, dr, t * 64 : (t + 1) * 64, :] = jnp.concatenate(parts, axis=1)


def lanes_iota(n):
    return lax.broadcasted_iota(jnp.int32, (1, n), 1) // 64


def build_forward(weights, meta, store):
    codes = jnp.transpose(meta, (1, 0))
    for oc in range(6):
        rows = slice(oc * 64, (oc + 1) * 64)
        pair, code = [], []
        for j in range(4):
            one = weights[rows, j * 64 : (j + 1) * 64]
            pair.append(jnp.concatenate([one, one], axis=1).astype(KIND))
            code.append(jnp.broadcast_to(codes[rows, j : j + 1], (64, 128)).astype(KIND))
        for q in range(2):
            at = oc - 2 * q
            if not 0 <= at < 4:
                continue
            for h in range(2):
                shift = 2 * h - at + 2 * q
                col = lanes_iota(128) + shift
                some = any(0 <= shift + x <= 2 for x in range(2))
                for dr in range(3):
                    total = jnp.zeros((64, 128), KIND)
                    if some:
                        need = jnp.where((col >= 0) & (col <= 2), col + 3 * dr, 77)
                        need = jnp.broadcast_to(need.astype(F32), (64, 128)).astype(KIND)
                        for j in range(4):
                            total = jnp.where(code[j] == need, pair[j], total)
                    store(
                        q,
                        dr,
                        slice(at * 64, at * 64 + 64),
                        slice(h * 128, h * 128 + 128),
                        total.astype(BF),
                    )


def build_adjoint(turned, meta, code_row, store):
    for p in range(2):
        lanes = slice(p * 128, p * 128 + 256)
        for t in range(2):
            col = t - lanes_iota(256) + 2
            need = jnp.where((col >= 0) & (col <= 2), col + 3 * code_row, 77).astype(F32)
            total = jnp.zeros((64, 256), F32)
            for j in range(4):
                hit = meta[j : j + 1, lanes] == need
                total = jnp.where(hit, turned[j * 64 : (j + 1) * 64, lanes], total)
            store(p, slice(t * 64, t * 64 + 64), total.astype(BF))


def unpack_foot(foot_ref, at):
    weights = foot_ref[at : at + 384, :].astype(F32)
    meta = [foot_ref[at + 384 : at + 400, :], foot_ref[at + 400 : at + 416, :128]]
    return weights, jnp.concatenate(meta, axis=1).astype(F32)


def forward(terms):
    halves = []
    for q in range(2):
        total = None
        for operand, field in terms:
            term = dot(operand(q), field[q * 256 : (q + 1) * 256, :])
            total = term if total is None else total + term
        halves.append(total)
    low, high = halves
    return [low[:128], low[128:] + high[:128], high[128:]]


def residual(parts, meta, res_ref, slot):
    columns = jnp.transpose(meta, (1, 0))
    obs = columns[:, 4:5] + columns[:, 5:6] + columns[:, 6:7]
    ivar = columns[:, 7:8] + columns[:, 8:9] + columns[:, 9:10]
    for n in range(3):
        rows = slice(n * 128, (n + 1) * 128)
        res_ref[slot, rows, :] = (ivar[rows] * (parts[n] - obs[rows])).astype(BF)


def field_of(x, p):
    return x[(1 + 2 * p) * 64 : (5 + 2 * p) * 64, :]


def from_residual(res_ref, slot, p):
    return res_ref[slot, p * 128 : p * 128 + 256, :]


def middle_kernel(first, *refs):
    if first:
        side_ref, x_ref, fw_ref, mt_ref, pair_ref, halo_ref, lp_ref = refs[:7]
        lfm_ref, lam_ref, lft_ref, lat_ref, mtt_ref, part_ref, grad_ref = refs[7:14]
        mate_ref, res_ref = refs[14:]
    else:
        (side_ref, x_ref, mt_ref, pair_ref, halo_ref, lp_ref) = refs[:6]
        lfm_ref, lam_ref, lft_ref, lat_ref, mtt_ref, lff_ref = refs[6:12]
        part_ref, grad_ref = refs[12:14]
        mate_ref, res_ref = refs[14:]
    side = side_ref[0]
    for m in range(2):
        mate_ref[m, 0:128, :] = halo_ref[m * 256 : m * 256 + 128, :]
        mate_ref[m, 128:384, :] = pair_ref[1 - side, m]
        mate_ref[m, 384:512, :] = halo_ref[m * 256 + 128 : m * 256 + 256, :]
    if first:
        for k in range(2):
            meta = mt_ref[k].astype(F32)
            weights = fw_ref[k].astype(F32)

            def put(q, dr, rows, lanes, value):
                lfm_ref[k, q, dr, rows, lanes] = value

            build_forward(weights, meta, put)
            turned = jnp.transpose(weights, (1, 0))
            for b in range(2):

                def put_adjoint(p, rows, value):
                    lam_ref[k, b, p, rows, :] = value

                build_adjoint(turned, meta, b - k + 1, put_adjoint)
        weights, meta = unpack_foot(halo_ref, 512)
        mtt_ref[...] = meta.astype(BF)

        def put_mate(q, dr, rows, lanes, value):
            lft_ref[q, dr, rows, lanes] = value

        def put_mate_adjoint(p, rows, value):
            lat_ref[p, rows, :] = value

        build_forward(weights, meta, put_mate)
        build_adjoint(jnp.transpose(weights, (1, 0)), meta, 2 * side, put_mate_adjoint)

    parts = forward(
        [(lambda q, r=r: lfm_ref[1 - side, q, r + side], x_ref.at[r]) for r in range(2)]
        + [(lambda q: lfm_ref[1 - side, q, 2 - 2 * side], mate_ref.at[side])]
    )
    residual(parts, mt_ref[1 - side].astype(F32), res_ref, 0)
    parts = forward(
        [(lambda q, m=m: lft_ref[q, m + 1 - side], mate_ref.at[m]) for m in range(2)]
        + [(lambda q: lft_ref[q, 2 * side], x_ref.at[1 - side])]
    )
    residual(parts, mtt_ref[...].astype(F32), res_ref, 1)
    parts = forward(
        [(lambda q, r=r: lfm_ref[side, q, r + 1 - side], x_ref.at[r]) for r in range(2)]
    )
    for n in range(3):
        part_ref[0, n * 128 : (n + 1) * 128, :] = parts[n]
    if not first:
        parts = forward([(lambda q: lff_ref[q, 2 - 2 * side], x_ref.at[side])])
        for n in range(3):
            part_ref[1, n * 128 : (n + 1) * 128, :] = parts[n]
    for p in range(2):
        rows = slice(p * 128, p * 128 + 128)
        for near_far in range(2):
            b = side if near_far else 1 - side
            total = dot(lam_ref[1 - side, b, p], from_residual(res_ref, 0, p))
            for r in range(2):
                total = total + dot(lp_ref[b, p, r + 1 - b], field_of(x_ref.at[r], p))
            if not near_far:
                total = total + dot(lat_ref[p], from_residual(res_ref, 1, p))
                total = total + dot(lp_ref[b, p, 2 - 2 * side], field_of(mate_ref.at[side], p))
            grad_ref[b, rows, :] = total


def finish_kernel(first, *refs):
    if first:
        (side_ref, x_ref, far_ref, mt_ref, lp_ref, lfm_ref, lam_ref, part_ref, grad_ref) = refs[:9]
        sample_ref, noise_hbm = refs[9:11]
        out_ref, compact_ref, lff_ref, laf_ref, mtf_ref = refs[11:16]
        res_ref, sample_buf, noise_buf, sems = refs[16:]
    else:
        (side_ref, far_ref, mt_ref, lp_ref, lfm_ref, lam_ref, part_ref, grad_ref) = refs[:8]
        lff_ref, laf_ref, mtf_ref, sample_ref, noise_hbm = refs[8:13]
        out_ref = refs[13]
        res_ref, out_buf, noise_buf, sems = refs[14:]
    side = side_ref[0]
    coming = [pltpu.make_async_copy(noise_hbm.at[0 if first else 1], noise_buf, sems.at[0])]
    if first:
        coming.append(pltpu.make_async_copy(sample_ref, sample_buf, sems.at[1]))
    for copy in coming:
        copy.start()
    far = [far_ref.at[f * 512 : (f + 1) * 512] for f in range(2)]
    if first:
        weights, meta = unpack_foot(far_ref, 1024)
        mtf_ref[...] = meta.astype(BF)

        def put(q, dr, rows, lanes, value):
            lff_ref[q, dr, rows, lanes] = value

        def put_adjoint(p, rows, value):
            laf_ref[p, rows, :] = value

        build_forward(weights, meta, put)
        build_adjoint(jnp.transpose(weights, (1, 0)), meta, 2 - 2 * side, put_adjoint)
    nearest = far_ref.at[pl.ds(pl.multiple_of((1 - side) * 512, 512), 512)]
    parts = forward([(lambda q: lfm_ref[side, q, 2 * side], nearest)])
    for n in range(3):
        parts[n] = parts[n] + part_ref[0, n * 128 : (n + 1) * 128, :]
    residual(parts, mt_ref[side].astype(F32), res_ref, 0)
    terms = [(lambda q, f=f: lff_ref[q, f + side], far[f]) for f in range(2)]
    if first:
        terms.append((lambda q: lff_ref[q, 2 - 2 * side], x_ref.at[side]))
    parts = forward(terms)
    if not first:
        for n in range(3):
            parts[n] = parts[n] + part_ref[1, n * 128 : (n + 1) * 128, :]
    residual(parts, mtf_ref[...].astype(F32), res_ref, 1)
    for copy in coming:
        copy.wait()
    old_ref = sample_buf if first else sample_ref
    leaving = []
    for near_far in range(2):
        b = side if near_far else 1 - side
        for p in range(2):
            rows = slice(p * 128, p * 128 + 128)
            total = grad_ref[b, rows, :] + dot(lam_ref[side, b, p], from_residual(res_ref, 0, p))
            if near_far:
                total = total + dot(laf_ref[p], from_residual(res_ref, 1, p))
                field = nearest[(1 + 2 * p) * 64 : (5 + 2 * p) * 64, :]
                total = total + dot(lp_ref[b, p, 2 * side], field)
            value = (
                old_ref[b, rows, :]
                - step_size * total
                + math.sqrt(2.0 * step_size) * noise_buf[b, rows, :].astype(F32)
            )
            if first:
                out_ref[b, rows, :] = value
                compact_ref[b, rows, :] = value.astype(BF)
            else:
                out_buf[b, rows, :] = value
                copy = pltpu.make_async_copy(
                    out_buf.at[b, rows], out_ref.at[b, rows], sems.at[1 + 2 * near_far + p]
                )
                copy.start()
                leaving.append(copy)
    for copy in leaving:
        copy.wait()


KIND = BF


def shape(dims, dtype=BF):
    return jax.ShapeDtypeStruct(dims, dtype)


def call(kernel, name, outs, args, spaces, scratch=(), out_space="v", flops=0, moved=0, grant=16):
    kinds = {"v": VM, "s": pltpu.SMEM, "h": pltpu.HBM}
    return pl.pallas_call(
        kernel,
        name=name,
        out_shape=tuple(outs),
        in_specs=[pl.BlockSpec(memory_space=kinds[space]) for space in spaces],
        out_specs=tuple(pl.BlockSpec(memory_space=kinds[out_space]) for _ in outs),
        scratch_shapes=list(scratch),
        compiler_params=pltpu.CompilerParams(vmem_limit_bytes=grant * 1024 * 1024),
        cost_estimate=pl.CostEstimate(flops=flops, bytes_accessed=moved, transcendentals=0),
    )(*args)


def middle_call(first, args):
    outs = []
    if first:
        outs = [
            shape((2, 2, 3, 256, 256)),
            shape((2, 2, 2, 128, 256)),
            shape((2, 3, 256, 256)),
            shape((2, 128, 256)),
            shape((16, 384)),
        ]
    outs += [shape((2, 384, 256), F32), shape((2, 256, 256), F32)]
    return call(
        lambda *refs: middle_kernel(first, *refs),
        "middle_first" if first else "middle_last",
        outs,
        args,
        "s" + "v" * (len(args) - 1),
        scratch=[pltpu.VMEM((2, 512, 256), BF), pltpu.VMEM((2, 384, 256), BF)],
        flops=700000000,
        moved=20000000,
    )


def finish_call(first, args):
    outs = [shape((2, 256, 256), F32)]
    if first:
        outs += [
            shape((2, 256, 256)),
            shape((2, 3, 256, 256)),
            shape((2, 128, 256)),
            shape((16, 384)),
        ]
    spaces = "s" + "v" * (len(args) - 3) + ("hh" if first else "vh")
    return call(
        lambda *refs: finish_kernel(first, *refs),
        "finish_first" if first else "finish_last",
        outs,
        args,
        spaces,
        scratch=[
            pltpu.VMEM((2, 384, 256), BF),
            pltpu.VMEM((2, 256, 256), F32),
            pltpu.VMEM((2, 256, 256), BF),
            pltpu.SemaphoreType.DMA((5,)),
        ],
        out_space="v" if first else "h",
        flops=400000000,
        moved=5000000,
    )


def local(
    sample_field,
    langevin_noise,
    precision,
    pattern,
    foot_weight,
    foot_columns,
    foot_count,
    observed,
    inverse_var,
):
    side = lax.axis_index("lat") % 2
    sides = jnp.full((1,), side, jnp.int32)
    sample = sample_field.reshape(2, 256, 256)
    noise = langevin_noise.reshape(STEPS, 2, 256, 256)
    fw = foot_weight.reshape(2, 256, 256)
    row = jnp.arange(8, dtype=jnp.int32)[:, None]
    stats = jnp.pad(foot_columns.transpose(0, 1, 3, 2), ((0, 0), (0, 0), (0, 4), (0, 0))).astype(F32)
    stats = jnp.where(row == 4, foot_count[:, :, None].astype(F32), stats)
    stats = jnp.where(row == 5, observed[:, :, None], stats)
    stats = jnp.where(row == 6, inverse_var[:, :, None], stats)
    compact, mt, leaving_west, leaving_east = call(
        prepare_kernel,
        "prepare",
        [shape((2, 256, 256)), shape((2, 16, 256)), shape((2, 208, 256)), shape((2, 208, 256))],
        (sample, stats, fw),
        "vvv",
        flops=1000000,
        moved=1000000,
    )
    (lp,) = call(
        prior_matrix_kernel,
        "prior_matrix",
        [shape((2, 2, 3, 128, 256))],
        (pattern, precision),
        "sv",
        scratch=[pltpu.SMEM((72,), jnp.int32)],
        flops=2000000,
        moved=3000000,
    )

    west = shift_lon(leaving_west, 1)
    east = shift_lon(leaving_east, -1)
    middle = jnp.concatenate([west[:, :128], compact, east[:, :128]], axis=1)
    fw = jnp.concatenate([west[:, 128:192], fw, east[:, 128:192]], axis=1)
    mt = jnp.concatenate([west[:, 192:, :64], mt, east[:, 192:, :64]], axis=2)

    def foot_row(row):
        meta = jnp.pad(mt[row], ((0, 0), (0, 128)))
        return jnp.concatenate([fw[row], meta[:, :256], meta[:, 256:]], axis=0)

    foot = jnp.stack([foot_row(0), foot_row(1)])
    far_foot = jnp.where(side == 0, foot[0], foot[1])
    mate_foot = jnp.where(side == 0, foot[1], foot[0])

    def lat_exchange(compact, middle, west, east, far_extra, mate_extra):
        far = swap_lat(jnp.concatenate([middle.reshape(1024, 256)] + far_extra, axis=0), 1)
        halo = jnp.concatenate([west, east], axis=1).reshape(512, 256)
        halo = swap_lat(jnp.concatenate([halo] + mate_extra, axis=0), 0)
        count = lax.axis_size("lat")
        pair = lax.all_gather(
            compact, "lat", axis_index_groups=[[i, i + 1] for i in range(0, count, 2)]
        )
        return far, pair, halo

    far, pair, halo = lat_exchange(
        compact, middle, west[:, :128], east[:, :128], [far_foot], [mate_foot]
    )
    lfm, lam, lft, lat, mtt, part, grad = middle_call(
        True, (sides, middle, fw, mt, pair, halo, lp)
    )
    sample, compact, lff, laf, mtf = finish_call(
        True, (sides, middle, far, mt, lp, lfm, lam, part, grad, sample, noise)
    )

    west = shift_lon(compact[:, 128:], 1)
    east = shift_lon(compact[:, :128], -1)
    middle = jnp.concatenate([west, compact, east], axis=1)
    far, pair, halo = lat_exchange(compact, middle, west, east, [], [])
    part, grad = middle_call(
        False, (sides, middle, mt, pair, halo, lp, lfm, lam, lft, lat, mtt, lff)
    )
    (sample,) = finish_call(
        False, (sides, far, mt, lp, lfm, lam, part, grad, lff, laf, mtf, sample, noise)
    )
    return sample.reshape(sample_field.shape)


def solution(mesh):
    placed = (
        P("lat", "lon", None, None),
        P(None, "lat", "lon", None, None),
        P("lat", "lon", None, None, None),
        P("lat", "lon", None),
        P("lat", "lon", None, None, None),
        P("lat", "lon", None, None),
        P("lat", "lon", None),
        P("lat", "lon", None),
        P("lat", "lon", None),
    )
    return jax.shard_map(
        local, mesh=mesh, in_specs=placed, out_specs=P("lat", "lon", None, None), check_vma=False
    )
```

time: 72.2 us -> 69.3 us (0.960)
  local copies, waits for them, and re-layouts: 4.8 us -> 2.65 us
  waiting for transfers between devices: 19.5 us -> 17.4 us
  other arithmetic: 0.39 us -> 1.87 us
    ppermute x4, waiting for transfers between devices: 12.5 us -> 10.4 us  [swap_lat(): return lax.ppermute(block, 'lat', pairs + [(b, a) for a, b in pairs])]
    unnamed x19 -> x12, local copies, waits for them, and re-layouts: 2.97 us -> 1.09 us
    select_n x0 -> x1, other arithmetic: none -> 0.81 us  [local(): stats = jnp.where(row == 6, inverse_var[:, :, None], stats)]
  transfers between devices with their start and end apart: 8 -> 8, of which waited for: 6 -> 6; matrix products, arithmetic and copies ran while one was open for 0% -> 0% of each run, Pallas kernels for 5% -> 7%
where the time goes in v3:
time: 69.3 us; the launch traced here: 68.8 us
  starting transfers between devices  33.4 us (48%)
  waiting for transfers between devices  17.4 us (25%)
  Pallas kernels  8.58 us (12%)
  blocking collectives  4.61 us (7%)
  local copies, waits for them, and re-layouts  2.65 us (4%)
  other arithmetic  1.87 us (3%)
    ppermute x4, starting transfers between devices, shift_lon(): lax.ppermute(block, 'lon', [(i, (i + by) % count) for i in range(count)])  22.9 us
    ppermute x4, starting transfers between devices, swap_lat(): return lax.ppermute(block, 'lat', pairs + [(b, a) for a, b in pairs])  10.6 us
    ppermute x4, waiting for transfers between devices, swap_lat(): return lax.ppermute(block, 'lat', pairs + [(b, a) for a, b in pairs])  10.4 us
    pallas_call x6, Pallas kernels, call(): pl.pallas_call(kernel, name=name, out_shape=tuple(outs), in_specs=[pl.Blo...  8.58 us
    ppermute x4, waiting for transfers between devices, shift_lon(): lax.ppermute(block, 'lon', [(i, (i + by) % count) for i in range(count)])  6.98 us
    all_gather x2, blocking collectives, lat_exchange(): lax.all_gather(compact, 'lat', axis_index_groups=[[i, i + 1] for i in ran...  4.61 us
    reshape x1, local copies, waits for them, and re-layouts, local(): fw = foot_weight.reshape(2, 256, 256)  1.45 us
  transfers between devices with their start and end apart: 8, of which 6 were waited for; matrix products, arithmetic and copies ran while one was open for 0% of the time, Pallas kernels for 7%

profile of v3, /device:TPU:4, one launch (start us, length us, event | category | flops | bytes accessed | tf_op | source)
XLA Modules:
  0.0 68.8 jit_solution(14604642980822139619)
XLA Ops:
  0.0 0.7 %convert_element_type.10 = f32[2,4,64]{2,1,0:T(4,128)S(1)} convert(s32[2,4,64]{2,1,0:T(4,128)} %param.15) | non-fusion elementwise | flops 512 | bytes 4096 | tf_op jit(solution)/shard_map/convert_element_type | solution.py:401
  0.7 1.5 %reshape.41.fw_ref = bf16[2,256,256]{2,1,0:T(8,128)(2,1)S(1)} reshape(bf16[2,4,64,4,64]{4,3,2,1,0:T(4,128)(2,1)} %param.13) | data formatting | bytes 524288 | tf_op jit(solution)/shard_map/reshape | solution.py:398
  2.2 0.8 %select_select_fusion.stats_ref = f32[2,4,8,64]{3,2,1,0:T(8,128)S(1)} fusion(s32[2,4,4,64]{3,2,1,0:T(4,128)} %bitcast.29, f32[2,4,64]{2,1,0:T(4,128)S(1)} %convert_element_type.10, f32[2,4,64]{2,1,0:T(4,128)} %param.16, f32[2,4,64]{2,1,0:T(4,128)} %param.17, pred[8]{0:T(512)(128)(4,1)S(1)} %get-tuple-element.53, pred[8]{0:T(512)(128)(4,1)S(1)} %get-tuple-element.54, ...), kind=kLoop, calls=%fused_computation.12 | loop fusion | flops 16384 | bytes 30744 | tf_op jit(solution)/shard_map/jit(_where)/select_n | solution.py:403
  3.0 0.0 copy-start.1
  3.0 1.0 %copy-done.1 = f32[2,4,64,256]{3,2,1,0:T(8,128)S(1)} copy-done((f32[2,4,64,256]{3,2,1,0:T(8,128)S(1)}, f32[2,4,64,256]{3,2,1,0:T(8,128)}, u32[]{:S(2)}) %copy-start.1) | copy-done | bytes 524312
  4.0 0.2 prepare.1
  4.2 3.1 %collective-permute-start = (bf16[2,208,256]{2,1,0:T(8,128)(2,1)S(1)}, bf16[2,208,256]{2,1,0:T(8,128)(2,1)S(1)}, u32[]{:S(2)}, u32[]{:S(2)}) collective-permute-start(bf16[2,208,256]{2,1,0:T(8,128)(2,1)S(1)} %get-tuple-element.23), channel_id=1, source_target_pairs={{0,1},{1,2},{2,3},{3,4},{4,5},{5,6},{6,7},{7,8},{8,9},{9,10},{10,1... | collective-permute-start | bytes 638984 | tf_op jit(solution)/shard_map/ppermute | solution.py:19
  7.3 10.9 %collective-permute-start.1 = (bf16[2,208,256]{2,1,0:T(8,128)(2,1)S(1)}, bf16[2,208,256]{2,1,0:T(8,128)(2,1)S(1)}, u32[]{:S(2)}, u32[]{:S(2)}) collective-permute-start(bf16[2,208,256]{2,1,0:T(8,128)(2,1)S(1)} %get-tuple-element.25), channel_id=1, source_target_pairs={{0,31},{1,0},{2,1},{3,2},{4,3},{5,4},{6,5},{7,6},{8,7},{9,8},{10,9... | collective-permute-start | bytes 638984 | tf_op jit(solution)/shard_map/ppermute | solution.py:19
  18.1 3.3 %collective-permute-done = bf16[2,208,256]{2,1,0:T(8,128)(2,1)S(1)} collective-permute-done((bf16[2,208,256]{2,1,0:T(8,128)(2,1)S(1)}, bf16[2,208,256]{2,1,0:T(8,128)(2,1)S(1)}, u32[]{:S(2)}, u32[]{:S(2)}) %collective-permute-start) | collective-permute-done | bytes 213024 | tf_op jit(solution)/shard_map/ppermute | solution.py:19
  21.4 1.2 %collective-permute-done.1 = bf16[2,208,256]{2,1,0:T(8,128)(2,1)S(1)} collective-permute-done((bf16[2,208,256]{2,1,0:T(8,128)(2,1)S(1)}, bf16[2,208,256]{2,1,0:T(8,128)(2,1)S(1)}, u32[]{:S(2)}, u32[]{:S(2)}) %collective-permute-start.1) | collective-permute-done | bytes 213024 | tf_op jit(solution)/shard_map/ppermute | solution.py:19
  22.7 0.1 pad_maximum_fusion.8.refs_3_.refs_2_
  23.0 0.1 broadcast_select_fusion
  23.1 0.0 copy-start.3
  23.1 0.0 copy-start.4
  23.1 0.1 pad_maximum_fusion
  23.1 3.9 %collective-permute-start.2 = (bf16[1440,256]{1,0:T(8,128)(2,1)S(1)}, bf16[1440,256]{1,0:T(8,128)(2,1)S(1)}, u32[]{:S(2)}, u32[]{:S(2)}) collective-permute-start(bf16[1440,256]{1,0:T(8,128)(2,1)S(1)} %pad_maximum_fusion), channel_id=1, source_target_pairs={{32,64},{96,128},{160,192},{224,256},{288,320},{352,384},{416,448}... | collective-permute-start | bytes 2211848 | tf_op jit(solution)/shard_map/ppermute | solution.py:25
  27.1 1.9 %collective-permute-start.3 = (bf16[928,256]{1,0:T(8,128)(2,1)S(1)}, bf16[928,256]{1,0:T(8,128)(2,1)S(1)}, u32[]{:S(2)}, u32[]{:S(2)}) collective-permute-start(bf16[928,256]{1,0:T(8,128)(2,1)S(1)} %pad_maximum_fusion.2), channel_id=1, source_target_pairs={{0,32},{64,96},{128,160},{192,224},{256,288},{320,352},{384,416},{... | collective-permute-start | bytes 1425416 | tf_op jit(solution)/shard_map/ppermute | solution.py:25
  29.0 0.0 copy-done.3
  29.0 0.0 copy-done.4
  29.0 0.9 %prior_matrix.1.refs_6_.refs_4_.refs_5_.refs_3_ = bf16[2,2,3,128,256]{4,3,2,1,0:T(8,128)(2,1)S(1)} custom-call(s32[2,4,9]{2,1,0:T(4,128)S(1)} %copy-done.4, bf16[2,4,9,64,64]{4,3,2,1,0:T(8,128)(2,1)S(1)} %copy-done.3), custom_call_target="tpu_custom_call" | custom-call | flops 2000000 | bytes 3000000 | tf_op jit(solution)/shard_map/prior_matrix/pallas_call | solution.py:320
  29.9 2.3 %all-gather = bf16[4,256,256]{2,1,0:T(8,128)(2,1)S(1)} all-gather(bf16[2,256,256]{2,1,0:T(8,128)(2,1)S(1)} %get-tuple-element.24), channel_id=2, replica_groups={{0,32},{64,96},{128,160},{192,224},{256,288},{320,352},{384,416},{448,4..., dimensions={0}, use_global_device_ids=true | all-gather | bytes 786432 | tf_op jit(solution)/shard_map/all_gather | solution.py:443
  32.2 0.0 copy-start
  32.2 0.0 copy-start.2
  32.2 0.0 collective-permute-done.3.refs_5_
  32.2 2.8 %middle_first.1 = (bf16[2,2,3,256,256]{4,3,2,1,0:T(8,128)(2,1)S(1)}, bf16[2,2,2,128,256]{4,3,2,1,0:T(8,128)(2,1)S(1)}, bf16[2,3,256,256]{3,2,1,0:T(8,128)(2,1)S(...) custom-call(s32[1]{0:T(128)} %bitcast.refs_0_, ...), custom_call_target="tpu_custom_call" | custom-call | flops 700000000 | bytes 20000000 | tf_op jit(solution)/shard_map/middle_first/pallas_call | solution.py:320
  35.1 4.6 %collective-permute-done.2.refs_2_ = bf16[1440,256]{1,0:T(8,128)(2,1)S(1)} collective-permute-done((bf16[1440,256]{1,0:T(8,128)(2,1)S(1)}, bf16[1440,256]{1,0:T(8,128)(2,1)S(1)}, u32[]{:S(2)}, u32[]{:S(2)}) %collective-permute-start.2) | collective-permute-done | bytes 737312 | tf_op jit(solution)/shard_map/ppermute | solution.py:25
  39.7 0.0 copy-done
  39.7 0.0 copy-done.2
  39.7 1.7 %finish_first.1 = (f32[2,256,256]{2,1,0:T(8,128)S(1)}, bf16[2,256,256]{2,1,0:T(8,128)(2,1)S(1)}, bf16[2,3,256,256]{3,2,1,0:T(8,128)(2,1)S(1)}, bf16[2,128,256]{2,1,0:T(8,128)(2,1)S(1)}, bf16[16,384]{1,0:T(8,128)(2,1)S(1)}) custom-call(s32[1]{0:T(128)} %bitcast.refs_0_, bf16[2,512,256]{2,1,0:T(8,128)(2,1)S(1)} %pad_maximum_fusion.1.refs_1_, ...), custom_call_target="tpu_custom_call" | custom-call | flops 400000000 | bytes 5000000 | tf_op jit(solution)/shard_map/finish_first/pallas_call | solution.py:320
  41.4 1.9 %collective-permute-start.4 = (bf16[2,128,256]{2,1,0:T(8,128)(2,1)S(1)}, bf16[2,128,256]{2,1,0:T(8,128)(2,1)S(1)}, u32[]{:S(2)}, u32[]{:S(2)}) collective-permute-start(bf16[2,128,256]{2,1,0:T(8,128)(2,1)S(1)} %get-tuple-element.46), channel_id=1, source_target_pairs={{0,1},{1,2},{2,3},{3,4},{4,5},{5,6},{6,7},{7,8},{8,9},{9,10},{10,1... | collective-permute-start | bytes 393224 | tf_op jit(solution)/shard_map/ppermute | solution.py:19
  43.4 7.0 %collective-permute-start.5 = (bf16[2,128,256]{2,1,0:T(8,128)(2,1)S(1)}, bf16[2,128,256]{2,1,0:T(8,128)(2,1)S(1)}, u32[]{:S(2)}, u32[]{:S(2)}) collective-permute-start(bf16[2,128,256]{2,1,0:T(8,128)(2,1)S(1)} %get-tuple-element.45), channel_id=1, source_target_pairs={{0,31},{1,0},{2,1},{3,2},{4,3},{5,4},{6,5},{7,6},{8,7},{9,8},{10,9... | collective-permute-start | bytes 393224 | tf_op jit(solution)/shard_map/ppermute | solution.py:19
  50.4 1.1 %collective-permute-done.4 = bf16[2,128,256]{2,1,0:T(8,128)(2,1)S(1)} collective-permute-done((bf16[2,128,256]{2,1,0:T(8,128)(2,1)S(1)}, bf16[2,128,256]{2,1,0:T(8,128)(2,1)S(1)}, u32[]{:S(2)}, u32[]{:S(2)}) %collective-permute-start.4) | collective-permute-done | bytes 131104 | tf_op jit(solution)/shard_map/ppermute | solution.py:19
  51.5 1.3 %collective-permute-done.5 = bf16[2,128,256]{2,1,0:T(8,128)(2,1)S(1)} collective-permute-done((bf16[2,128,256]{2,1,0:T(8,128)(2,1)S(1)}, bf16[2,128,256]{2,1,0:T(8,128)(2,1)S(1)}, u32[]{:S(2)}, u32[]{:S(2)}) %collective-permute-start.5) | collective-permute-done | bytes 131104 | tf_op jit(solution)/shard_map/ppermute | solution.py:19
  52.9 2.9 %collective-permute-start.6 = (bf16[1024,256]{1,0:T(8,128)(2,1)S(1)}, bf16[1024,256]{1,0:T(8,128)(2,1)S(1)}, u32[]{:S(2)}, u32[]{:S(2)}) collective-permute-start(bf16[1024,256]{1,0:T(8,128)(2,1)S(1)} %bitcast.26), channel_id=1, source_target_pairs={{32,64},{96,128},{160,192},{224,256},{288,320},{352,384},{416,448}... | collective-permute-start | bytes 1572872 | tf_op jit(solution)/shard_map/ppermute | solution.py:25
  55.8 1.9 %collective-permute-start.7 = (bf16[512,256]{1,0:T(8,128)(2,1)S(1)}, bf16[512,256]{1,0:T(8,128)(2,1)S(1)}, u32[]{:S(2)}, u32[]{:S(2)}) collective-permute-start(bf16[512,256]{1,0:T(8,128)(2,1)S(1)} %bitcast.28), channel_id=1, source_target_pairs={{0,32},{64,96},{128,160},{192,224},{256,288},{320,352},{384,416},{... | collective-permute-start | bytes 786440 | tf_op jit(solution)/shard_map/ppermute | solution.py:25
  57.7 2.3 %all-gather.1 = bf16[4,256,256]{2,1,0:T(8,128)(2,1)S(1)} all-gather(bf16[2,256,256]{2,1,0:T(8,128)(2,1)S(1)} %get-tuple-element.31), channel_id=3, replica_groups={{0,32},{64,96},{128,160},{192,224},{256,288},{320,352},{384,416},{448,4..., dimensions={0}, use_global_device_ids=true | all-gather | bytes 786432 | tf_op jit(solution)/shard_map/all_gather | solution.py:443
  60.0 0.0 collective-permute-done.7.refs_4_
  60.0 1.2 %middle_last.1 = (f32[2,384,256]{2,1,0:T(8,128)S(1)}, f32[2,256,256]{2,1,0:T(8,128)S(1)}) custom-call(s32[1]{0:T(128)} %bitcast.refs_0_, bf16[2,512,256]{2,1,0:T(8,128)(2,1)S(1)} %constant_dynamic-update-slice_fusion.refs_1_, bf16[2,16,384]{2,1,0:T(8,128)(2,1)S(1)} %pad_maximum_fusion.8.refs_3_.refs_2_, bf16[2,2,256,256]{3,2,1,0:T(8,128)(2,1)S(1)} %bitcast.25, ...), custom_call_target="tpu_custom_call" | custom-call | flops 700000000 | bytes 20000000 | tf_op jit(solution)/shard_map/middle_last/pallas_call | solution.py:320
  61.2 5.8 %collective-permute-done.6.refs_1_ = bf16[1024,256]{1,0:T(8,128)(2,1)S(1)} collective-permute-done((bf16[1024,256]{1,0:T(8,128)(2,1)S(1)}, bf16[1024,256]{1,0:T(8,128)(2,1)S(1)}, u32[]{:S(2)}, u32[]{:S(2)}) %collective-permute-start.6) | collective-permute-done | bytes 524320 | tf_op jit(solution)/shard_map/ppermute | solution.py:25
  67.0 1.8 %finish_last.1 = f32[2,256,256]{2,1,0:T(8,128)} custom-call(s32[1]{0:T(128)} %bitcast.refs_0_, bf16[1024,256]{1,0:T(8,128)(2,1)S(1)} %collective-permute-done.6.refs_1_, bf16[2,16,384]{2,1,0:T(8,128)(2,1)S(1)} %pad_maximum_fusion.8.refs_3_.refs_2_, bf16[2,2,3,128,256]{4,3,2,1,0:T(8,128)(2,1)S(1)} %prior_matrix.1.refs_6_.refs_4_.refs_5_.refs_3_, ...), custom_call_target="tpu_custom_call" | custom-call | flops 400000000 | bytes 5000000 | tf_op jit(solution)/shard_map/finish_last/pallas_call | solution.py:320
  (21 shorter events, 0.3 us)
Async XLA Ops:
  3.0 1.0 %copy-start.1 = (f32[2,4,64,256]{3,2,1,0:T(8,128)S(1)}, f32[2,4,64,256]{3,2,1,0:T(8,128)}, u32[]{:S(2)}) copy-start(f32[2,4,64,256]{3,2,1,0:T(8,128)} %param.9) | copy-start | bytes 1572868
  4.2 17.3 %collective-permute-start = (bf16[2,208,256]{2,1,0:T(8,128)(2,1)S(1)}, bf16[2,208,256]{2,1,0:T(8,128)(2,1)S(1)}, u32[]{:S(2)}, u32[]{:S(2)}) collective-permute-start(bf16[2,208,256]{2,1,0:T(8,128)(2,1)S(1)} %get-tuple-element.23), channel_id=1, source_target_pairs={{0,1},{1,2},{2,3},{3,4},{4,5},{5,6},{6,7},{7,8},{8,9},{9,10},{10,1... | collective-permute-start | bytes 638984 | tf_op jit(solution)/shard_map/ppermute | solution.py:19
  7.3 15.4 %collective-permute-start.1 = (bf16[2,208,256]{2,1,0:T(8,128)(2,1)S(1)}, bf16[2,208,256]{2,1,0:T(8,128)(2,1)S(1)}, u32[]{:S(2)}, u32[]{:S(2)}) collective-permute-start(bf16[2,208,256]{2,1,0:T(8,128)(2,1)S(1)} %get-tuple-element.25), channel_id=1, source_target_pairs={{0,31},{1,0},{2,1},{3,2},{4,3},{5,4},{6,5},{7,6},{8,7},{9,8},{10,9... | collective-permute-start | bytes 638984 | tf_op jit(solution)/shard_map/ppermute | solution.py:19
  23.1 5.9 %copy-start.3 = (bf16[2,4,9,64,64]{4,3,2,1,0:T(8,128)(2,1)S(1)}, bf16[2,4,9,64,64]{4,3,2,1,0:T(8,128)(2,1)}, u32[]{:S(2)}) copy-start(bf16[2,4,9,64,64]{4,3,2,1,0:T(8,128)(2,1)} %precision_ref.1) | copy-start | bytes 1769476
  23.1 5.9 %copy-start.4 = (s32[2,4,9]{2,1,0:T(4,128)S(1)}, s32[2,4,9]{2,1,0:T(4,128)}, u32[]{:S(2)}) copy-start(s32[2,4,9]{2,1,0:T(4,128)} %pattern_ref.1) | copy-start | bytes 868
  23.1 16.5 %collective-permute-start.2 = (bf16[1440,256]{1,0:T(8,128)(2,1)S(1)}, bf16[1440,256]{1,0:T(8,128)(2,1)S(1)}, u32[]{:S(2)}, u32[]{:S(2)}) collective-permute-start(bf16[1440,256]{1,0:T(8,128)(2,1)S(1)} %pad_maximum_fusion), channel_id=1, source_target_pairs={{32,64},{96,128},{160,192},{224,256},{288,320},{352,384},{416,448}... | collective-permute-start | bytes 2211848 | tf_op jit(solution)/shard_map/ppermute | solution.py:25
  27.1 5.2 %collective-permute-start.3 = (bf16[928,256]{1,0:T(8,128)(2,1)S(1)}, bf16[928,256]{1,0:T(8,128)(2,1)S(1)}, u32[]{:S(2)}, u32[]{:S(2)}) collective-permute-start(bf16[928,256]{1,0:T(8,128)(2,1)S(1)} %pad_maximum_fusion.2), channel_id=1, source_target_pairs={{0,32},{64,96},{128,160},{192,224},{256,288},{320,352},{384,416},{... | collective-permute-start | bytes 1425416 | tf_op jit(solution)/shard_map/ppermute | solution.py:25
  32.2 7.4 %copy-start = (bf16[2,2,4,64,256]{4,3,2,1,0:T(8,128)(2,1)S(1)}, bf16[2,2,4,64,256]{4,3,2,1,0:T(8,128)(2,1)}, u32[]{:S(2)}) copy-start(bf16[2,2,4,64,256]{4,3,2,1,0:T(8,128)(2,1)} %param.10) | copy-start | bytes 1572868
  32.2 7.4 %copy-start.2 = (f32[2,4,64,256]{3,2,1,0:T(8,128)S(1)}, f32[2,4,64,256]{3,2,1,0:T(8,128)}, u32[]{:S(2)}) copy-start(f32[2,4,64,256]{3,2,1,0:T(8,128)} %param.9) | copy-start | bytes 1572868
  41.4 10.0 %collective-permute-start.4 = (bf16[2,128,256]{2,1,0:T(8,128)(2,1)S(1)}, bf16[2,128,256]{2,1,0:T(8,128)(2,1)S(1)}, u32[]{:S(2)}, u32[]{:S(2)}) collective-permute-start(bf16[2,128,256]{2,1,0:T(8,128)(2,1)S(1)} %get-tuple-element.46), channel_id=1, source_target_pairs={{0,1},{1,2},{2,3},{3,4},{4,5},{5,6},{6,7},{7,8},{8,9},{9,10},{10,1... | collective-permute-start | bytes 393224 | tf_op jit(solution)/shard_map/ppermute | solution.py:19
  43.4 9.5 %collective-permute-start.5 = (bf16[2,128,256]{2,1,0:T(8,128)(2,1)S(1)}, bf16[2,128,256]{2,1,0:T(8,128)(2,1)S(1)}, u32[]{:S(2)}, u32[]{:S(2)}) collective-permute-start(bf16[2,128,256]{2,1,0:T(8,128)(2,1)S(1)} %get-tuple-element.45), channel_id=1, source_target_pairs={{0,31},{1,0},{2,1},{3,2},{4,3},{5,4},{6,5},{7,6},{8,7},{9,8},{10,9... | collective-permute-start | bytes 393224 | tf_op jit(solution)/shard_map/ppermute | solution.py:19
  52.9 14.1 %collective-permute-start.6 = (bf16[1024,256]{1,0:T(8,128)(2,1)S(1)}, bf16[1024,256]{1,0:T(8,128)(2,1)S(1)}, u32[]{:S(2)}, u32[]{:S(2)}) collective-permute-start(bf16[1024,256]{1,0:T(8,128)(2,1)S(1)} %bitcast.26), channel_id=1, source_target_pairs={{32,64},{96,128},{160,192},{224,256},{288,320},{352,384},{416,448}... | collective-permute-start | bytes 1572872 | tf_op jit(solution)/shard_map/ppermute | solution.py:25
  55.8 4.2 %collective-permute-start.7 = (bf16[512,256]{1,0:T(8,128)(2,1)S(1)}, bf16[512,256]{1,0:T(8,128)(2,1)S(1)}, u32[]{:S(2)}, u32[]{:S(2)}) collective-permute-start(bf16[512,256]{1,0:T(8,128)(2,1)S(1)} %bitcast.28), channel_id=1, source_target_pairs={{0,32},{64,96},{128,160},{192,224},{256,288},{320,352},{384,416},{... | collective-permute-start | bytes 786440 | tf_op jit(solution)/shard_map/ppermute | solution.py:25

commit v4 on v3

--- a/solution.py
+++ b/solution.py
@@ -37,11 +37,9 @@
 
 
 def prepare_kernel(sample_ref, stats_ref, fw_ref, compact_ref, mt_ref, west_ref, east_ref):
-    slot = lax.broadcasted_iota(jnp.int32, (4, 256), 0).astype(F32)
     for b in range(2):
         stats = jnp.concatenate([stats_ref[b, c] for c in range(4)], axis=1)
-        codes = jnp.where(slot < stats[4:5], stats[0:4], 99.0)
-        rows = [codes] + split(stats[5:6]) + split(stats[6:7]) + [jnp.zeros((6, 256), F32)]
+        rows = [stats[0:4]] + split(stats[5:6]) + split(stats[6:7]) + [jnp.zeros((6, 256), F32)]
         meta = jnp.concatenate(rows, axis=0).astype(BF)
         mt_ref[b] = meta
         compact = sample_ref[b].astype(BF)
@@ -170,9 +168,9 @@
         mate_ref, res_ref = refs[14:]
     side = side_ref[0]
     for m in range(2):
-        mate_ref[m, 0:128, :] = halo_ref[m * 256 : m * 256 + 128, :]
+        mate_ref[m, 0:128, :] = halo_ref[1 - side, m * 256 : m * 256 + 128, :]
         mate_ref[m, 128:384, :] = pair_ref[1 - side, m]
-        mate_ref[m, 384:512, :] = halo_ref[m * 256 + 128 : m * 256 + 256, :]
+        mate_ref[m, 384:512, :] = halo_ref[1 - side, m * 256 + 128 : m * 256 + 256, :]
     if first:
         for k in range(2):
             meta = mt_ref[k].astype(F32)
@@ -189,7 +187,7 @@
                     lam_ref[k, b, p, rows, :] = value
 
                 build_adjoint(turned, meta, b - k + 1, put_adjoint)
-        weights, meta = unpack_foot(halo_ref, 512)
+        weights, meta = unpack_foot(halo_ref.at[1 - side], 512)
         mtt_ref[...] = meta.astype(BF)
 
         def put_mate(q, dr, rows, lanes, value):
@@ -235,24 +233,31 @@
 
 def finish_kernel(first, *refs):
     if first:
-        (side_ref, x_ref, far_ref, mt_ref, lp_ref, lfm_ref, lam_ref, part_ref, grad_ref) = refs[:9]
-        sample_ref, noise_hbm = refs[9:11]
-        out_ref, compact_ref, lff_ref, laf_ref, mtf_ref = refs[11:16]
-        res_ref, sample_buf, noise_buf, sems = refs[16:]
+        (side_ref, x_ref, own_ref, halo_ref, mt_ref, lp_ref, lfm_ref, lam_ref) = refs[:8]
+        part_ref, grad_ref, sample_ref, noise_hbm = refs[8:12]
+        out_ref, compact_ref, lff_ref, laf_ref, mtf_ref = refs[12:17]
+        res_ref, far_ref, sample_buf, noise_buf, sems = refs[17:]
     else:
-        (side_ref, far_ref, mt_ref, lp_ref, lfm_ref, lam_ref, part_ref, grad_ref) = refs[:8]
-        lff_ref, laf_ref, mtf_ref, sample_ref, noise_hbm = refs[8:13]
-        out_ref = refs[13]
-        res_ref, out_buf, noise_buf, sems = refs[14:]
+        (side_ref, own_ref, halo_ref, mt_ref, lp_ref, lfm_ref, lam_ref, part_ref) = refs[:8]
+        grad_ref, lff_ref, laf_ref, mtf_ref, sample_ref, noise_hbm = refs[8:14]
+        out_ref = refs[14]
+        res_ref, far_ref, out_buf, noise_buf, sems = refs[15:]
     side = side_ref[0]
     coming = [pltpu.make_async_copy(noise_hbm.at[0 if first else 1], noise_buf, sems.at[0])]
     if first:
         coming.append(pltpu.make_async_copy(sample_ref, sample_buf, sems.at[1]))
     for copy in coming:
         copy.start()
-    far = [far_ref.at[f * 512 : (f + 1) * 512] for f in range(2)]
-    if first:
-        weights, meta = unpack_foot(far_ref, 1024)
+    for f in range(2):
+        far_ref[f, 0:128, :] = halo_ref[f * 256 : f * 256 + 128, :]
+        far_ref[f, 128:384, :] = own_ref[f * 256 : f * 256 + 256, :]
+        far_ref[f, 384:512, :] = halo_ref[f * 256 + 128 : f * 256 + 256, :]
+    far = [far_ref.at[f] for f in range(2)]
+    if first:
+        weights = [halo_ref[512:576, :], own_ref[512:768, :], halo_ref[576:640, :]]
+        weights = jnp.concatenate(weights, axis=0).astype(F32)
+        meta = [halo_ref[640:656, :64], own_ref[768:784, :], halo_ref[640:656, 64:128]]
+        meta = jnp.concatenate(meta, axis=1).astype(F32)
         mtf_ref[...] = meta.astype(BF)
 
         def put(q, dr, rows, lanes, value):
@@ -263,7 +268,7 @@
 
         build_forward(weights, meta, put)
         build_adjoint(jnp.transpose(weights, (1, 0)), meta, 2 - 2 * side, put_adjoint)
-    nearest = far_ref.at[pl.ds(pl.multiple_of((1 - side) * 512, 512), 512)]
+    nearest = far_ref.at[1 - side]
     parts = forward([(lambda q: lfm_ref[side, q, 2 * side], nearest)])
     for n in range(3):
         parts[n] = parts[n] + part_ref[0, n * 128 : (n + 1) * 128, :]
@@ -347,8 +352,8 @@
         args,
         "s" + "v" * (len(args) - 1),
         scratch=[pltpu.VMEM((2, 512, 256), BF), pltpu.VMEM((2, 384, 256), BF)],
-        flops=700000000,
-        moved=20000000,
+        flops=1000000,
+        moved=100000,
     )
 
 
@@ -370,6 +375,7 @@
         spaces,
         scratch=[
             pltpu.VMEM((2, 384, 256), BF),
+            pltpu.VMEM((2, 512, 256), BF),
             pltpu.VMEM((2, 256, 256), F32),
             pltpu.VMEM((2, 256, 256), BF),
             pltpu.SemaphoreType.DMA((5,)),
@@ -397,10 +403,10 @@
     noise = langevin_noise.reshape(STEPS, 2, 256, 256)
     fw = foot_weight.reshape(2, 256, 256)
     row = jnp.arange(8, dtype=jnp.int32)[:, None]
-    stats = jnp.pad(foot_columns.transpose(0, 1, 3, 2), ((0, 0), (0, 0), (0, 4), (0, 0))).astype(F32)
-    stats = jnp.where(row == 4, foot_count[:, :, None].astype(F32), stats)
-    stats = jnp.where(row == 5, observed[:, :, None], stats)
-    stats = jnp.where(row == 6, inverse_var[:, :, None], stats)
+    codes = jnp.pad(foot_columns.transpose(0, 1, 3, 2), ((0, 0), (0, 0), (0, 4), (0, 0)))
+    codes = jnp.where(row < foot_count[:, :, None], codes, 99).astype(F32)
+    stats = jnp.where(row == 6, inverse_var[:, :, None], observed[:, :, None])
+    stats = jnp.where(row < 4, codes, stats)
     compact, mt, leaving_west, leaving_east = call(
         prepare_kernel,
         "prepare",
@@ -423,47 +429,52 @@
 
     west = shift_lon(leaving_west, 1)
     east = shift_lon(leaving_east, -1)
+    fw_own, mt_own = fw, mt
+
+    def near_row(rows):
+        return jnp.where(side == 0, rows[0], rows[1])
+
+    own_far = swap_lat(
+        jnp.concatenate([compact.reshape(512, 256), near_row(fw_own), near_row(mt_own)], axis=0), 1
+    )
     middle = jnp.concatenate([west[:, :128], compact, east[:, :128]], axis=1)
     fw = jnp.concatenate([west[:, 128:192], fw, east[:, 128:192]], axis=1)
     mt = jnp.concatenate([west[:, 192:, :64], mt, east[:, 192:, :64]], axis=2)
 
-    def foot_row(row):
-        meta = jnp.pad(mt[row], ((0, 0), (0, 128)))
-        return jnp.concatenate([fw[row], meta[:, :256], meta[:, 256:]], axis=0)
-
-    foot = jnp.stack([foot_row(0), foot_row(1)])
-    far_foot = jnp.where(side == 0, foot[0], foot[1])
-    mate_foot = jnp.where(side == 0, foot[1], foot[0])
-
-    def lat_exchange(compact, middle, west, east, far_extra, mate_extra):
-        far = swap_lat(jnp.concatenate([middle.reshape(1024, 256)] + far_extra, axis=0), 1)
-        halo = jnp.concatenate([west, east], axis=1).reshape(512, 256)
-        halo = swap_lat(jnp.concatenate([halo] + mate_extra, axis=0), 0)
+    def mates(compact, halo, extra):
         count = lax.axis_size("lat")
-        pair = lax.all_gather(
-            compact, "lat", axis_index_groups=[[i, i + 1] for i in range(0, count, 2)]
-        )
-        return far, pair, halo
-
-    far, pair, halo = lat_exchange(
-        compact, middle, west[:, :128], east[:, :128], [far_foot], [mate_foot]
-    )
+        groups = [[i, i + 1] for i in range(0, count, 2)]
+        pair = lax.all_gather(compact, "lat", axis_index_groups=groups)
+        halo = jnp.concatenate([halo] + extra, axis=0)
+        return pair, lax.all_gather(halo, "lat", axis_index_groups=groups)
+
+    halo = jnp.concatenate([west[:, :128], east[:, :128]], axis=1).reshape(512, 256)
+    meta = jnp.concatenate([west[:, 192:, :64], east[:, 192:, :64]], axis=2)
+    meta = jnp.pad(near_row(meta), ((0, 0), (0, 128)))
+    foot = [near_row(west[:, 128:192]), near_row(east[:, 128:192]), meta]
+    halo_far = swap_lat(jnp.concatenate([halo] + foot, axis=0), 1)
+    mate_meta = jnp.pad(jnp.where(side == 0, mt[1], mt[0]), ((0, 0), (0, 128)))
+    mate_foot = [jnp.where(side == 0, fw[1], fw[0]), mate_meta[:, :256], mate_meta[:, 256:]]
+    pair, halo = mates(compact, halo, mate_foot)
     lfm, lam, lft, lat, mtt, part, grad = middle_call(
         True, (sides, middle, fw, mt, pair, halo, lp)
     )
     sample, compact, lff, laf, mtf = finish_call(
-        True, (sides, middle, far, mt, lp, lfm, lam, part, grad, sample, noise)
+        True, (sides, middle, own_far, halo_far, mt, lp, lfm, lam, part, grad, sample, noise)
     )
 
     west = shift_lon(compact[:, 128:], 1)
     east = shift_lon(compact[:, :128], -1)
+    own_far = swap_lat(compact.reshape(512, 256), 1)
     middle = jnp.concatenate([west, compact, east], axis=1)
-    far, pair, halo = lat_exchange(compact, middle, west, east, [], [])
+    halo = jnp.concatenate([west, east], axis=1).reshape(512, 256)
+    halo_far = swap_lat(halo, 1)
+    pair, halo = mates(compact, halo, [])
     part, grad = middle_call(
         False, (sides, middle, mt, pair, halo, lp, lfm, lam, lft, lat, mtt, lff)
     )
     (sample,) = finish_call(
-        False, (sides, far, mt, lp, lfm, lam, part, grad, lff, laf, mtf, sample, noise)
+        False, (sides, own_far, halo_far, mt, lp, lfm, lam, part, grad, lff, laf, mtf, sample, noise)
     )
     return sample.reshape(sample_field.shape)
 

time: 69.3 us -> 66.4 us (0.958)
  the two profiles are of different devices: /device:TPU:4 before, /device:TPU:25 now
where the time goes in v4:
time: 66.4 us; the launch traced here: 66 us
  starting transfers between devices  39.8 us (60%)
  blocking collectives  9.03 us (14%)
  Pallas kernels  8.63 us (13%)
  waiting for transfers between devices  3.83 us (6%)
  local copies, waits for them, and re-layouts  2.88 us (4%)
  other arithmetic  1.39 us (2%)
    ppermute x4, starting transfers between devices, shift_lon(): lax.ppermute(block, 'lon', [(i, (i + by) % count) for i in range(count)])  21.5 us
    ppermute x4, starting transfers between devices, swap_lat(): return lax.ppermute(block, 'lat', pairs + [(b, a) for a, b in pairs])  18.4 us
    pallas_call x6, Pallas kernels, call(): pl.pallas_call(kernel, name=name, out_shape=tuple(outs), in_specs=[pl.Blo...  8.63 us
    all_gather x2, blocking collectives, mates(): return (pair, lax.all_gather(halo, 'lat', axis_index_groups=groups))  4.67 us
    all_gather x2, blocking collectives, mates(): pair = lax.all_gather(compact, 'lat', axis_index_groups=groups)  4.36 us
    ppermute x4, waiting for transfers between devices, swap_lat(): return lax.ppermute(block, 'lat', pairs + [(b, a) for a, b in pairs])  3.82 us
    reshape x1, local copies, waits for them, and re-layouts, local(): fw = foot_weight.reshape(2, 256, 256)  1.52 us
  transfers between devices with their start and end apart: 8, of which 2 were waited for; matrix products, arithmetic and copies ran while one was open for 1% of the time, Pallas kernels for 7%

profile of v4, /device:TPU:25, one launch (start us, length us, event | category | flops | bytes accessed | tf_op | source)
XLA Modules:
  0.0 66.0 jit_solution(4108885129353155212)
XLA Ops:
  0.0 0.0 copy-start.5
  0.0 1.5 %reshape.54.fw_ref = bf16[2,256,256]{2,1,0:T(8,128)(2,1)S(1)} reshape(bf16[2,4,64,4,64]{4,3,2,1,0:T(4,128)(2,1)} %param.13) | data formatting | bytes 524288 | tf_op jit(solution)/shard_map/reshape | solution.py:404
  1.5 0.0 copy-start.4
  1.5 0.8 %select_select_fusion.stats_ref = f32[2,4,8,64]{3,2,1,0:T(8,128)S(1)} fusion(s32[2,4,4,64]{3,2,1,0:T(4,128)} %bitcast.38, f32[2,4,64]{2,1,0:T(4,128)} %param.16, f32[2,4,64]{2,1,0:T(4,128)} %param.17, s32[2,4,64]{2,1,0:T(4,128)} %param.15, pred[8]{0:T(512)(128)(4,1)S(1)} %get-tuple-element.45, pred[8]{0:T(512)(128)(4,1)S(1)} %get-tuple-element.46), kind=kLoop, calls=%fused_computation.16 | loop fusion | flops 20480 | bytes 30736 | tf_op jit(solution)/shard_map/jit(_where)/select_n | solution.py:409
  2.4 0.0 copy-start.1
  2.4 1.0 %copy-done.1 = f32[2,4,64,256]{3,2,1,0:T(8,128)S(1)} copy-done((f32[2,4,64,256]{3,2,1,0:T(8,128)S(1)}, f32[2,4,64,256]{3,2,1,0:T(8,128)}, u32[]{:S(2)}) %copy-start.1) | copy-done | bytes 524312
  3.4 0.0 copy-start.3
  3.4 0.2 prepare.1
  3.6 3.2 %collective-permute-start = (bf16[2,208,256]{2,1,0:T(8,128)(2,1)S(1)}, bf16[2,208,256]{2,1,0:T(8,128)(2,1)S(1)}, u32[]{:S(2)}, u32[]{:S(2)}) collective-permute-start(bf16[2,208,256]{2,1,0:T(8,128)(2,1)S(1)} %get-tuple-element.23), channel_id=1, source_target_pairs={{0,1},{1,2},{2,3},{3,4},{4,5},{5,6},{6,7},{7,8},{8,9},{9,10},{10,1... | collective-permute-start | bytes 638984 | tf_op jit(solution)/shard_map/ppermute | solution.py:19
  6.8 10.9 %collective-permute-start.1 = (bf16[2,208,256]{2,1,0:T(8,128)(2,1)S(1)}, bf16[2,208,256]{2,1,0:T(8,128)(2,1)S(1)}, u32[]{:S(2)}, u32[]{:S(2)}) collective-permute-start(bf16[2,208,256]{2,1,0:T(8,128)(2,1)S(1)} %get-tuple-element.25), channel_id=1, source_target_pairs={{0,31},{1,0},{2,1},{3,2},{4,3},{5,4},{6,5},{7,6},{8,7},{9,8},{10,9... | collective-permute-start | bytes 638984 | tf_op jit(solution)/shard_map/ppermute | solution.py:19
  17.7 0.0 copy-done.5
  17.7 0.1 slice_select_fusion
  17.8 0.2 select_n.98
  18.1 4.9 %collective-permute-start.2 = (bf16[784,256]{1,0:T(8,128)(2,1)S(1)}, bf16[784,256]{1,0:T(8,128)(2,1)S(1)}, u32[]{:S(2)}, u32[]{:S(2)}) collective-permute-start(bf16[784,256]{1,0:T(8,128)(2,1)S(1)} %pad_maximum_fusion.3), channel_id=1, source_target_pairs={{32,64},{96,128},{160,192},{224,256},{288,320},{352,384},{416,448}... | collective-permute-start | bytes 1204232 | tf_op jit(solution)/shard_map/ppermute | solution.py:25
  23.0 0.0 copy-done.4
  23.0 0.0 copy-done.3
  23.0 0.9 %prior_matrix.1.refs_6_.refs_5_.refs_4_ = bf16[2,2,3,128,256]{4,3,2,1,0:T(8,128)(2,1)S(1)} custom-call(s32[2,4,9]{2,1,0:T(4,128)S(1)} %copy-done.4, bf16[2,4,9,64,64]{4,3,2,1,0:T(8,128)(2,1)S(1)} %copy-done.3), custom_call_target="tpu_custom_call" | custom-call | flops 2000000 | bytes 3000000 | tf_op jit(solution)/shard_map/prior_matrix/pallas_call | solution.py:325
  23.9 2.2 %all-gather = bf16[4,256,256]{2,1,0:T(8,128)(2,1)S(1)} all-gather(bf16[2,256,256]{2,1,0:T(8,128)(2,1)S(1)} %get-tuple-element.24), channel_id=2, replica_groups={{0,32},{64,96},{128,160},{192,224},{256,288},{320,352},{384,416},{448,4..., dimensions={0}, use_global_device_ids=true | all-gather | bytes 786432 | tf_op jit(solution)/shard_map/all_gather | solution.py:447
  26.1 0.0 collective-permute-done
  26.1 0.0 collective-permute-done.1
  26.1 0.1 fusion.8
  26.2 0.1 pad_maximum_fusion.6.refs_3_.refs_4_.refs_2_
  26.6 4.3 %collective-permute-start.3 = (bf16[656,256]{1,0:T(8,128)(2,1)S(1)}, bf16[656,256]{1,0:T(8,128)(2,1)S(1)}, u32[]{:S(2)}, u32[]{:S(2)}) collective-permute-start(bf16[656,256]{1,0:T(8,128)(2,1)S(1)} %fusion.1), channel_id=1, source_target_pairs={{32,64},{96,128},{160,192},{224,256},{288,320},{352,384},{416,448}... | collective-permute-start | bytes 1007624 | tf_op jit(solution)/shard_map/ppermute | solution.py:25
  30.9 2.5 %all-gather.1 = bf16[1856,256]{1,0:T(8,128)(2,1)S(1)} all-gather(bf16[928,256]{1,0:T(8,128)(2,1)S(1)} %pad_maximum_fusion.2), channel_id=3, replica_groups={{0,32},{64,96},{128,160},{192,224},{256,288},{320,352},{384,416},{448,4..., dimensions={0}, use_global_device_ids=true | all-gather | bytes 1425408 | tf_op jit(solution)/shard_map/all_gather | solution.py:449
  33.4 0.0 copy-start
  33.4 0.0 copy-start.2
  33.4 2.8 %middle_first.1 = (bf16[2,2,3,256,256]{4,3,2,1,0:T(8,128)(2,1)S(1)}, bf16[2,2,2,128,256]{4,3,2,1,0:T(8,128)(2,1)S(1)}, bf16[2,3,256,256]{3,2,1,0:T(8,128)(2,1)S(...) custom-call(s32[1]{0:T(128)} %bitcast.refs_0_, ...), custom_call_target="tpu_custom_call" | custom-call | flops 1000000 | bytes 100000 | tf_op jit(solution)/shard_map/middle_first/pallas_call | solution.py:325
  36.2 0.0 collective-permute-done.2.refs_2_
  36.2 2.4 %collective-permute-done.3.refs_3_ = bf16[656,256]{1,0:T(8,128)(2,1)S(1)} collective-permute-done((bf16[656,256]{1,0:T(8,128)(2,1)S(1)}, bf16[656,256]{1,0:T(8,128)(2,1)S(1)}, u32[]{:S(2)}, u32[]{:S(2)}) %collective-permute-start.3) | collective-permute-done | bytes 335904 | tf_op jit(solution)/shard_map/ppermute | solution.py:25
  38.7 0.0 copy-done
  38.7 0.0 copy-done.2
  38.7 1.8 %finish_first.1 = (f32[2,256,256]{2,1,0:T(8,128)S(1)}, bf16[2,256,256]{2,1,0:T(8,128)(2,1)S(1)}, bf16[2,3,256,256]{3,2,1,0:T(8,128)(2,1)S(1)}, bf16[2,128,256]{2,1,0:T(8,128)(2,1)S(1)}, bf16[16,384]{1,0:T(8,128)(2,1)S(1)}) custom-call(s32[1]{0:T(128)} %bitcast.refs_0_, bf16[2,512,256]{2,1,0:T(8,128)(2,1)S(1)} %pad_maximum_fusion.refs_1_, ...), custom_call_target="tpu_custom_call" | custom-call | flops 400000000 | bytes 5000000 | tf_op jit(solution)/shard_map/finish_first/pallas_call | solution.py:325
  40.5 1.9 %collective-permute-start.5 = (bf16[2,128,256]{2,1,0:T(8,128)(2,1)S(1)}, bf16[2,128,256]{2,1,0:T(8,128)(2,1)S(1)}, u32[]{:S(2)}, u32[]{:S(2)}) collective-permute-start(bf16[2,128,256]{2,1,0:T(8,128)(2,1)S(1)} %get-tuple-element.42), channel_id=1, source_target_pairs={{0,1},{1,2},{2,3},{3,4},{4,5},{5,6},{6,7},{7,8},{8,9},{9,10},{10,1... | collective-permute-start | bytes 393224 | tf_op jit(solution)/shard_map/ppermute | solution.py:19
  42.4 5.5 %collective-permute-start.6 = (bf16[2,128,256]{2,1,0:T(8,128)(2,1)S(1)}, bf16[2,128,256]{2,1,0:T(8,128)(2,1)S(1)}, u32[]{:S(2)}, u32[]{:S(2)}) collective-permute-start(bf16[2,128,256]{2,1,0:T(8,128)(2,1)S(1)} %get-tuple-element.41), channel_id=1, source_target_pairs={{0,31},{1,0},{2,1},{3,2},{4,3},{5,4},{6,5},{7,6},{8,7},{9,8},{10,9... | collective-permute-start | bytes 393224 | tf_op jit(solution)/shard_map/ppermute | solution.py:19
  47.9 4.9 %collective-permute-start.4 = (bf16[512,256]{1,0:T(8,128)(2,1)S(1)}, bf16[512,256]{1,0:T(8,128)(2,1)S(1)}, u32[]{:S(2)}, u32[]{:S(2)}) collective-permute-start(bf16[512,256]{1,0:T(8,128)(2,1)S(1)} %bitcast.27), channel_id=1, source_target_pairs={{32,64},{96,128},{160,192},{224,256},{288,320},{352,384},{416,448}... | collective-permute-start | bytes 786440 | tf_op jit(solution)/shard_map/ppermute | solution.py:25
  52.8 0.0 collective-permute-done.5
  52.8 0.0 collective-permute-done.6
  52.8 4.3 %collective-permute-start.7 = (bf16[512,256]{1,0:T(8,128)(2,1)S(1)}, bf16[512,256]{1,0:T(8,128)(2,1)S(1)}, u32[]{:S(2)}, u32[]{:S(2)}) collective-permute-start(bf16[512,256]{1,0:T(8,128)(2,1)S(1)} %bitcast.36), channel_id=1, source_target_pairs={{32,64},{96,128},{160,192},{224,256},{288,320},{352,384},{416,448}... | collective-permute-start | bytes 786440 | tf_op jit(solution)/shard_map/ppermute | solution.py:25
  57.1 2.2 %all-gather.2 = bf16[4,256,256]{2,1,0:T(8,128)(2,1)S(1)} all-gather(bf16[2,256,256]{2,1,0:T(8,128)(2,1)S(1)} %get-tuple-element.31), channel_id=4, replica_groups={{0,32},{64,96},{128,160},{192,224},{256,288},{320,352},{384,416},{448,4..., dimensions={0}, use_global_device_ids=true | all-gather | bytes 786432 | tf_op jit(solution)/shard_map/all_gather | solution.py:447
  59.4 2.2 %all_gather.27.refs_4_ = bf16[2,512,256]{2,1,0:T(8,128)(2,1)S(1)} all-gather(bf16[1,512,256]{2,1,0:T(8,128)(2,1)S(1)} %bitcast.37), channel_id=1, replica_groups={{0,32},{64,96},{128,160},{192,224},{256,288},{320,352},{384,416},{448,4..., dimensions={0}, use_global_device_ids=true | all-gather | bytes 786432 | tf_op jit(solution)/shard_map/all_gather | solution.py:449
  61.5 1.2 %middle_last.1 = (f32[2,384,256]{2,1,0:T(8,128)S(1)}, f32[2,256,256]{2,1,0:T(8,128)S(1)}) custom-call(s32[1]{0:T(128)} %bitcast.refs_0_, bf16[2,512,256]{2,1,0:T(8,128)(2,1)S(1)} %pad_maximum_fusion.1.refs_1_, bf16[2,16,384]{2,1,0:T(8,128)(2,1)S(1)} %pad_maximum_fusion.6.refs_3_.refs_4_.refs_2_, bf16[2,2,256,256]{3,2,1,0:T(8,128)(2,1)S(1)} %bitcast.33, ...), custom_call_target="tpu_custom_call" | custom-call | flops 1000000 | bytes 100000 | tf_op jit(solution)/shard_map/middle_last/pallas_call | solution.py:325
  62.7 0.0 collective-permute-done.4.refs_1_
  62.7 1.4 %collective-permute-done.7.refs_2_ = bf16[512,256]{1,0:T(8,128)(2,1)S(1)} collective-permute-done((bf16[512,256]{1,0:T(8,128)(2,1)S(1)}, bf16[512,256]{1,0:T(8,128)(2,1)S(1)}, u32[]{:S(2)}, u32[]{:S(2)}) %collective-permute-start.7) | collective-permute-done | bytes 262176 | tf_op jit(solution)/shard_map/ppermute | solution.py:25
  64.1 1.8 %finish_last.1 = f32[2,256,256]{2,1,0:T(8,128)} custom-call(s32[1]{0:T(128)} %bitcast.refs_0_, bf16[512,256]{1,0:T(8,128)(2,1)S(1)} %collective-permute-done.4.refs_1_, bf16[512,256]{1,0:T(8,128)(2,1)S(1)} %collective-permute-done.7.refs_2_, bf16[2,16,384]{2,1,0:T(8,128)(2,1)S(1)} %pad_maximum_fusion.6.refs_3_.refs_4_.refs_2_, ...), custom_call_target="tpu_custom_call" | custom-call | flops 400000000 | bytes 5000000 | tf_op jit(solution)/shard_map/finish_last/pallas_call | solution.py:325
  (23 shorter events, 0.4 us)
Async XLA Ops:
  0.0 17.7 %copy-start.5 = (bf16[2,4,64,4,64]{4,3,2,1,0:T(4,128)(2,1)S(1)}, bf16[2,4,64,4,64]{4,3,2,1,0:T(4,128)(2,1)}, u32[]{:S(2)}) copy-start(bf16[2,4,64,4,64]{4,3,2,1,0:T(4,128)(2,1)} %param.13) | copy-start | bytes 786436
  1.5 21.4 %copy-start.4 = (s32[2,4,9]{2,1,0:T(4,128)S(1)}, s32[2,4,9]{2,1,0:T(4,128)}, u32[]{:S(2)}) copy-start(s32[2,4,9]{2,1,0:T(4,128)} %pattern_ref.1) | copy-start | bytes 868
  2.4 1.0 %copy-start.1 = (f32[2,4,64,256]{3,2,1,0:T(8,128)S(1)}, f32[2,4,64,256]{3,2,1,0:T(8,128)}, u32[]{:S(2)}) copy-start(f32[2,4,64,256]{3,2,1,0:T(8,128)} %param.9) | copy-start | bytes 1572868
  3.4 19.6 %copy-start.3 = (bf16[2,4,9,64,64]{4,3,2,1,0:T(8,128)(2,1)S(1)}, bf16[2,4,9,64,64]{4,3,2,1,0:T(8,128)(2,1)}, u32[]{:S(2)}) copy-start(bf16[2,4,9,64,64]{4,3,2,1,0:T(8,128)(2,1)} %precision_ref.1) | copy-start | bytes 1769476
  3.6 22.5 %collective-permute-start = (bf16[2,208,256]{2,1,0:T(8,128)(2,1)S(1)}, bf16[2,208,256]{2,1,0:T(8,128)(2,1)S(1)}, u32[]{:S(2)}, u32[]{:S(2)}) collective-permute-start(bf16[2,208,256]{2,1,0:T(8,128)(2,1)S(1)} %get-tuple-element.23), channel_id=1, source_target_pairs={{0,1},{1,2},{2,3},{3,4},{4,5},{5,6},{6,7},{7,8},{8,9},{9,10},{10,1... | collective-permute-start | bytes 638984 | tf_op jit(solution)/shard_map/ppermute | solution.py:19
  6.8 19.3 %collective-permute-start.1 = (bf16[2,208,256]{2,1,0:T(8,128)(2,1)S(1)}, bf16[2,208,256]{2,1,0:T(8,128)(2,1)S(1)}, u32[]{:S(2)}, u32[]{:S(2)}) collective-permute-start(bf16[2,208,256]{2,1,0:T(8,128)(2,1)S(1)} %get-tuple-element.25), channel_id=1, source_target_pairs={{0,31},{1,0},{2,1},{3,2},{4,3},{5,4},{6,5},{7,6},{8,7},{9,8},{10,9... | collective-permute-start | bytes 638984 | tf_op jit(solution)/shard_map/ppermute | solution.py:19
  18.1 18.1 %collective-permute-start.2 = (bf16[784,256]{1,0:T(8,128)(2,1)S(1)}, bf16[784,256]{1,0:T(8,128)(2,1)S(1)}, u32[]{:S(2)}, u32[]{:S(2)}) collective-permute-start(bf16[784,256]{1,0:T(8,128)(2,1)S(1)} %pad_maximum_fusion.3), channel_id=1, source_target_pairs={{32,64},{96,128},{160,192},{224,256},{288,320},{352,384},{416,448}... | collective-permute-start | bytes 1204232 | tf_op jit(solution)/shard_map/ppermute | solution.py:25
  26.6 12.1 %collective-permute-start.3 = (bf16[656,256]{1,0:T(8,128)(2,1)S(1)}, bf16[656,256]{1,0:T(8,128)(2,1)S(1)}, u32[]{:S(2)}, u32[]{:S(2)}) collective-permute-start(bf16[656,256]{1,0:T(8,128)(2,1)S(1)} %fusion.1), channel_id=1, source_target_pairs={{32,64},{96,128},{160,192},{224,256},{288,320},{352,384},{416,448}... | collective-permute-start | bytes 1007624 | tf_op jit(solution)/shard_map/ppermute | solution.py:25
  33.4 5.2 %copy-start = (bf16[2,2,4,64,256]{4,3,2,1,0:T(8,128)(2,1)S(1)}, bf16[2,2,4,64,256]{4,3,2,1,0:T(8,128)(2,1)}, u32[]{:S(2)}) copy-start(bf16[2,2,4,64,256]{4,3,2,1,0:T(8,128)(2,1)} %param.10) | copy-start | bytes 1572868
  33.4 5.2 %copy-start.2 = (f32[2,4,64,256]{3,2,1,0:T(8,128)S(1)}, f32[2,4,64,256]{3,2,1,0:T(8,128)}, u32[]{:S(2)}) copy-start(f32[2,4,64,256]{3,2,1,0:T(8,128)} %param.9) | copy-start | bytes 1572868
  40.5 12.3 %collective-permute-start.5 = (bf16[2,128,256]{2,1,0:T(8,128)(2,1)S(1)}, bf16[2,128,256]{2,1,0:T(8,128)(2,1)S(1)}, u32[]{:S(2)}, u32[]{:S(2)}) collective-permute-start(bf16[2,128,256]{2,1,0:T(8,128)(2,1)S(1)} %get-tuple-element.42), channel_id=1, source_target_pairs={{0,1},{1,2},{2,3},{3,4},{4,5},{5,6},{6,7},{7,8},{8,9},{9,10},{10,1... | collective-permute-start | bytes 393224 | tf_op jit(solution)/shard_map/ppermute | solution.py:19
  42.4 10.4 %collective-permute-start.6 = (bf16[2,128,256]{2,1,0:T(8,128)(2,1)S(1)}, bf16[2,128,256]{2,1,0:T(8,128)(2,1)S(1)}, u32[]{:S(2)}, u32[]{:S(2)}) collective-permute-start(bf16[2,128,256]{2,1,0:T(8,128)(2,1)S(1)} %get-tuple-element.41), channel_id=1, source_target_pairs={{0,31},{1,0},{2,1},{3,2},{4,3},{5,4},{6,5},{7,6},{8,7},{9,8},{10,9... | collective-permute-start | bytes 393224 | tf_op jit(solution)/shard_map/ppermute | solution.py:19
  47.9 14.8 %collective-permute-start.4 = (bf16[512,256]{1,0:T(8,128)(2,1)S(1)}, bf16[512,256]{1,0:T(8,128)(2,1)S(1)}, u32[]{:S(2)}, u32[]{:S(2)}) collective-permute-start(bf16[512,256]{1,0:T(8,128)(2,1)S(1)} %bitcast.27), channel_id=1, source_target_pairs={{32,64},{96,128},{160,192},{224,256},{288,320},{352,384},{416,448}... | collective-permute-start | bytes 786440 | tf_op jit(solution)/shard_map/ppermute | solution.py:25
  52.8 11.3 %collective-permute-start.7 = (bf16[512,256]{1,0:T(8,128)(2,1)S(1)}, bf16[512,256]{1,0:T(8,128)(2,1)S(1)}, u32[]{:S(2)}, u32[]{:S(2)}) collective-permute-start(bf16[512,256]{1,0:T(8,128)(2,1)S(1)} %bitcast.36), channel_id=1, source_target_pairs={{32,64},{96,128},{160,192},{224,256},{288,320},{352,384},{416,448}... | collective-permute-start | bytes 786440 | tf_op jit(solution)/shard_map/ppermute | solution.py:25

commit v5 on v4

--- a/solution.py
+++ b/solution.py
@@ -416,17 +416,6 @@
         flops=1000000,
         moved=1000000,
     )
-    (lp,) = call(
-        prior_matrix_kernel,
-        "prior_matrix",
-        [shape((2, 2, 3, 128, 256))],
-        (pattern, precision),
-        "sv",
-        scratch=[pltpu.SMEM((72,), jnp.int32)],
-        flops=2000000,
-        moved=3000000,
-    )
-
     west = shift_lon(leaving_west, 1)
     east = shift_lon(leaving_east, -1)
     fw_own, mt_own = fw, mt
@@ -449,13 +438,24 @@
         return pair, lax.all_gather(halo, "lat", axis_index_groups=groups)
 
     halo = jnp.concatenate([west[:, :128], east[:, :128]], axis=1).reshape(512, 256)
+    mate_own, halo, late_pattern = lax.optimization_barrier((compact, halo, pattern))
+    (lp,) = call(
+        prior_matrix_kernel,
+        "prior_matrix",
+        [shape((2, 2, 3, 128, 256))],
+        (late_pattern, precision),
+        "sv",
+        scratch=[pltpu.SMEM((72,), jnp.int32)],
+        flops=2000000,
+        moved=3000000,
+    )
     meta = jnp.concatenate([west[:, 192:, :64], east[:, 192:, :64]], axis=2)
     meta = jnp.pad(near_row(meta), ((0, 0), (0, 128)))
     foot = [near_row(west[:, 128:192]), near_row(east[:, 128:192]), meta]
     halo_far = swap_lat(jnp.concatenate([halo] + foot, axis=0), 1)
     mate_meta = jnp.pad(jnp.where(side == 0, mt[1], mt[0]), ((0, 0), (0, 128)))
     mate_foot = [jnp.where(side == 0, fw[1], fw[0]), mate_meta[:, :256], mate_meta[:, 256:]]
-    pair, halo = mates(compact, halo, mate_foot)
+    pair, halo = mates(mate_own, halo, mate_foot)
     lfm, lam, lft, lat, mtt, part, grad = middle_call(
         True, (sides, middle, fw, mt, pair, halo, lp)
     )

time: 66.4 us -> 64.7 us (0.974)
  waiting for transfers between devices: 3.83 us -> 1.73 us
    ppermute x4, waiting for transfers between devices: 3.82 us -> 1.72 us  [swap_lat(): return lax.ppermute(block, 'lat', pairs + [(b, a) for a, b in pairs])]
  transfers between devices with their start and end apart: 8 -> 8, of which waited for: 2 -> 1; matrix products, arithmetic and copies ran while one was open for 1% -> 1% of each run, Pallas kernels for 7% -> 8%
where the time goes in v5:
time: 64.7 us; the launch traced here: 64.3 us
  starting transfers between devices  40.2 us (62%)
  blocking collectives  9.03 us (14%)
  Pallas kernels  8.63 us (13%)
  local copies, waits for them, and re-layouts  2.88 us (4%)
  waiting for transfers between devices  1.73 us (3%)
  other arithmetic  1.38 us (2%)
    ppermute x4, starting transfers between devices, shift_lon(): lax.ppermute(block, 'lon', [(i, (i + by) % count) for i in range(count)])  21.7 us
    ppermute x4, starting transfers between devices, swap_lat(): return lax.ppermute(block, 'lat', pairs + [(b, a) for a, b in pairs])  18.5 us
    pallas_call x6, Pallas kernels, call(): pl.pallas_call(kernel, name=name, out_shape=tuple(outs), in_specs=[pl.Blo...  8.63 us
    all_gather x2, blocking collectives, mates(): return (pair, lax.all_gather(halo, 'lat', axis_index_groups=groups))  4.67 us
    all_gather x2, blocking collectives, mates(): pair = lax.all_gather(compact, 'lat', axis_index_groups=groups)  4.36 us
    ppermute x4, waiting for transfers between devices, swap_lat(): return lax.ppermute(block, 'lat', pairs + [(b, a) for a, b in pairs])  1.72 us
    reshape x1, local copies, waits for them, and re-layouts, local(): fw = foot_weight.reshape(2, 256, 256)  1.52 us
  transfers between devices with their start and end apart: 8, of which 1 were waited for; matrix products, arithmetic and copies ran while one was open for 1% of the time, Pallas kernels for 8%

profile of v5, /device:TPU:25, one launch (start us, length us, event | category | flops | bytes accessed | tf_op | source)
XLA Modules:
  0.0 64.3 jit_solution(9418756727214049001)
XLA Ops:
  0.0 0.0 copy-start.5
  0.0 1.5 %reshape.54.fw_ref = bf16[2,256,256]{2,1,0:T(8,128)(2,1)S(1)} reshape(bf16[2,4,64,4,64]{4,3,2,1,0:T(4,128)(2,1)} %param.13) | data formatting | bytes 524288 | tf_op jit(solution)/shard_map/reshape | solution.py:404
  1.5 0.8 %select_select_fusion.stats_ref = f32[2,4,8,64]{3,2,1,0:T(8,128)S(1)} fusion(s32[2,4,4,64]{3,2,1,0:T(4,128)} %bitcast.38, f32[2,4,64]{2,1,0:T(4,128)} %param.16, f32[2,4,64]{2,1,0:T(4,128)} %param.17, s32[2,4,64]{2,1,0:T(4,128)} %param.15, pred[8]{0:T(512)(128)(4,1)S(1)} %get-tuple-element.51, pred[8]{0:T(512)(128)(4,1)S(1)} %get-tuple-element.52), kind=kLoop, calls=%fused_computation.16 | loop fusion | flops 20480 | bytes 30736 | tf_op jit(solution)/shard_map/jit(_where)/select_n | solution.py:409
  2.3 0.0 copy-start.1
  2.4 1.0 %copy-done.1 = f32[2,4,64,256]{3,2,1,0:T(8,128)S(1)} copy-done((f32[2,4,64,256]{3,2,1,0:T(8,128)S(1)}, f32[2,4,64,256]{3,2,1,0:T(8,128)}, u32[]{:S(2)}) %copy-start.1) | copy-done | bytes 524312
  3.4 0.2 prepare.1
  3.5 3.1 %collective-permute-start = (bf16[2,208,256]{2,1,0:T(8,128)(2,1)S(1)}, bf16[2,208,256]{2,1,0:T(8,128)(2,1)S(1)}, u32[]{:S(2)}, u32[]{:S(2)}) collective-permute-start(bf16[2,208,256]{2,1,0:T(8,128)(2,1)S(1)} %get-tuple-element.26), channel_id=1, source_target_pairs={{0,1},{1,2},{2,3},{3,4},{4,5},{5,6},{6,7},{7,8},{8,9},{9,10},{10,1... | collective-permute-start | bytes 638984 | tf_op jit(solution)/shard_map/ppermute | solution.py:19
  6.7 10.9 %collective-permute-start.1 = (bf16[2,208,256]{2,1,0:T(8,128)(2,1)S(1)}, bf16[2,208,256]{2,1,0:T(8,128)(2,1)S(1)}, u32[]{:S(2)}, u32[]{:S(2)}) collective-permute-start(bf16[2,208,256]{2,1,0:T(8,128)(2,1)S(1)} %get-tuple-element.28), channel_id=1, source_target_pairs={{0,31},{1,0},{2,1},{3,2},{4,3},{5,4},{6,5},{7,6},{8,7},{9,8},{10,9... | collective-permute-start | bytes 638984 | tf_op jit(solution)/shard_map/ppermute | solution.py:19
  17.5 0.0 copy-done.5
  17.5 0.1 slice_select_fusion
  17.7 0.2 select_n.98
  18.0 4.9 %collective-permute-start.2 = (bf16[784,256]{1,0:T(8,128)(2,1)S(1)}, bf16[784,256]{1,0:T(8,128)(2,1)S(1)}, u32[]{:S(2)}, u32[]{:S(2)}) collective-permute-start(bf16[784,256]{1,0:T(8,128)(2,1)S(1)} %pad_maximum_fusion.3), channel_id=1, source_target_pairs={{32,64},{96,128},{160,192},{224,256},{288,320},{352,384},{416,448}... | collective-permute-start | bytes 1204232 | tf_op jit(solution)/shard_map/ppermute | solution.py:25
  22.8 0.0 collective-permute-done
  22.8 0.0 collective-permute-done.1
  22.9 0.1 fusion.8
  22.9 0.1 pad_maximum_fusion.6.refs_3_.refs_4_.refs_2_
  23.2 0.0 copy-start.3
  23.2 0.0 copy-start.4
  23.4 4.5 %collective-permute-start.3 = (bf16[656,256]{1,0:T(8,128)(2,1)S(1)}, bf16[656,256]{1,0:T(8,128)(2,1)S(1)}, u32[]{:S(2)}, u32[]{:S(2)}) collective-permute-start(bf16[656,256]{1,0:T(8,128)(2,1)S(1)} %fusion.1), channel_id=1, source_target_pairs={{32,64},{96,128},{160,192},{224,256},{288,320},{352,384},{416,448}... | collective-permute-start | bytes 1007624 | tf_op jit(solution)/shard_map/ppermute | solution.py:25
  27.8 2.2 %all-gather = bf16[4,256,256]{2,1,0:T(8,128)(2,1)S(1)} all-gather(bf16[2,256,256]{2,1,0:T(8,128)(2,1)S(1)} %get-tuple-element.32), channel_id=2, replica_groups={{0,32},{64,96},{128,160},{192,224},{256,288},{320,352},{384,416},{448,4..., dimensions={0}, use_global_device_ids=true | all-gather | bytes 786432 | tf_op jit(solution)/shard_map/all_gather | solution.py:436
  30.0 0.0 copy-done.3
  30.0 0.0 copy-done.4
  30.0 0.9 %prior_matrix.1.refs_6_.refs_5_.refs_4_ = bf16[2,2,3,128,256]{4,3,2,1,0:T(8,128)(2,1)S(1)} custom-call(s32[2,4,9]{2,1,0:T(4,128)S(1)} %copy-done.4, bf16[2,4,9,64,64]{4,3,2,1,0:T(8,128)(2,1)S(1)} %copy-done.3), custom_call_target="tpu_custom_call" | custom-call | flops 2000000 | bytes 3000000 | tf_op jit(solution)/shard_map/prior_matrix/pallas_call | solution.py:325
  30.9 2.5 %all-gather.1 = bf16[1856,256]{1,0:T(8,128)(2,1)S(1)} all-gather(bf16[928,256]{1,0:T(8,128)(2,1)S(1)} %pad_maximum_fusion.2), channel_id=3, replica_groups={{0,32},{64,96},{128,160},{192,224},{256,288},{320,352},{384,416},{448,4..., dimensions={0}, use_global_device_ids=true | all-gather | bytes 1425408 | tf_op jit(solution)/shard_map/all_gather | solution.py:438
  33.4 0.0 copy-start
  33.4 0.0 copy-start.2
  33.4 2.8 %middle_first.1 = (bf16[2,2,3,256,256]{4,3,2,1,0:T(8,128)(2,1)S(1)}, bf16[2,2,2,128,256]{4,3,2,1,0:T(8,128)(2,1)S(1)}, bf16[2,3,256,256]{3,2,1,0:T(8,128)(2,1)S(...) custom-call(s32[1]{0:T(128)} %bitcast.refs_0_, ...), custom_call_target="tpu_custom_call" | custom-call | flops 1000000 | bytes 100000 | tf_op jit(solution)/shard_map/middle_first/pallas_call | solution.py:325
  36.3 0.0 collective-permute-done.2.refs_2_
  36.3 0.0 collective-permute-done.3.refs_3_
  36.3 0.0 copy-done
  36.3 0.0 copy-done.2
  36.3 1.8 %finish_first.1 = (f32[2,256,256]{2,1,0:T(8,128)S(1)}, bf16[2,256,256]{2,1,0:T(8,128)(2,1)S(1)}, bf16[2,3,256,256]{3,2,1,0:T(8,128)(2,1)S(1)}, bf16[2,128,256]{2,1,0:T(8,128)(2,1)S(1)}, bf16[16,384]{1,0:T(8,128)(2,1)S(1)}) custom-call(s32[1]{0:T(128)} %bitcast.refs_0_, bf16[2,512,256]{2,1,0:T(8,128)(2,1)S(1)} %pad_maximum_fusion.refs_1_, ...), custom_call_target="tpu_custom_call" | custom-call | flops 400000000 | bytes 5000000 | tf_op jit(solution)/shard_map/finish_first/pallas_call | solution.py:325
  38.1 1.9 %collective-permute-start.5 = (bf16[2,128,256]{2,1,0:T(8,128)(2,1)S(1)}, bf16[2,128,256]{2,1,0:T(8,128)(2,1)S(1)}, u32[]{:S(2)}, u32[]{:S(2)}) collective-permute-start(bf16[2,128,256]{2,1,0:T(8,128)(2,1)S(1)} %get-tuple-element.48), channel_id=1, source_target_pairs={{0,1},{1,2},{2,3},{3,4},{4,5},{5,6},{6,7},{7,8},{8,9},{9,10},{10,1... | collective-permute-start | bytes 393224 | tf_op jit(solution)/shard_map/ppermute | solution.py:19
  40.0 5.8 %collective-permute-start.6 = (bf16[2,128,256]{2,1,0:T(8,128)(2,1)S(1)}, bf16[2,128,256]{2,1,0:T(8,128)(2,1)S(1)}, u32[]{:S(2)}, u32[]{:S(2)}) collective-permute-start(bf16[2,128,256]{2,1,0:T(8,128)(2,1)S(1)} %get-tuple-element.47), channel_id=1, source_target_pairs={{0,31},{1,0},{2,1},{3,2},{4,3},{5,4},{6,5},{7,6},{8,7},{9,8},{10,9... | collective-permute-start | bytes 393224 | tf_op jit(solution)/shard_map/ppermute | solution.py:19
  45.9 5.2 %collective-permute-start.4 = (bf16[512,256]{1,0:T(8,128)(2,1)S(1)}, bf16[512,256]{1,0:T(8,128)(2,1)S(1)}, u32[]{:S(2)}, u32[]{:S(2)}) collective-permute-start(bf16[512,256]{1,0:T(8,128)(2,1)S(1)} %bitcast.27), channel_id=1, source_target_pairs={{32,64},{96,128},{160,192},{224,256},{288,320},{352,384},{416,448}... | collective-permute-start | bytes 786440 | tf_op jit(solution)/shard_map/ppermute | solution.py:25
  51.1 0.0 collective-permute-done.5
  51.1 0.0 collective-permute-done.6
  51.2 4.0 %collective-permute-start.7 = (bf16[512,256]{1,0:T(8,128)(2,1)S(1)}, bf16[512,256]{1,0:T(8,128)(2,1)S(1)}, u32[]{:S(2)}, u32[]{:S(2)}) collective-permute-start(bf16[512,256]{1,0:T(8,128)(2,1)S(1)} %bitcast.36), channel_id=1, source_target_pairs={{32,64},{96,128},{160,192},{224,256},{288,320},{352,384},{416,448}... | collective-permute-start | bytes 786440 | tf_op jit(solution)/shard_map/ppermute | solution.py:25
  55.2 2.2 %all-gather.2 = bf16[4,256,256]{2,1,0:T(8,128)(2,1)S(1)} all-gather(bf16[2,256,256]{2,1,0:T(8,128)(2,1)S(1)} %get-tuple-element.37), channel_id=4, replica_groups={{0,32},{64,96},{128,160},{192,224},{256,288},{320,352},{384,416},{448,4..., dimensions={0}, use_global_device_ids=true | all-gather | bytes 786432 | tf_op jit(solution)/shard_map/all_gather | solution.py:436
  57.4 2.2 %all_gather.27.refs_4_ = bf16[2,512,256]{2,1,0:T(8,128)(2,1)S(1)} all-gather(bf16[1,512,256]{2,1,0:T(8,128)(2,1)S(1)} %bitcast.37), channel_id=1, replica_groups={{0,32},{64,96},{128,160},{192,224},{256,288},{320,352},{384,416},{448,4..., dimensions={0}, use_global_device_ids=true | all-gather | bytes 786432 | tf_op jit(solution)/shard_map/all_gather | solution.py:438
  59.6 1.2 %middle_last.1 = (f32[2,384,256]{2,1,0:T(8,128)S(1)}, f32[2,256,256]{2,1,0:T(8,128)S(1)}) custom-call(s32[1]{0:T(128)} %bitcast.refs_0_, bf16[2,512,256]{2,1,0:T(8,128)(2,1)S(1)} %pad_maximum_fusion.1.refs_1_, bf16[2,16,384]{2,1,0:T(8,128)(2,1)S(1)} %pad_maximum_fusion.6.refs_3_.refs_4_.refs_2_, bf16[2,2,256,256]{3,2,1,0:T(8,128)(2,1)S(1)} %bitcast.33, ...), custom_call_target="tpu_custom_call" | custom-call | flops 1000000 | bytes 100000 | tf_op jit(solution)/shard_map/middle_last/pallas_call | solution.py:325
  60.7 0.0 collective-permute-done.4.refs_1_
  60.8 1.7 %collective-permute-done.7.refs_2_ = bf16[512,256]{1,0:T(8,128)(2,1)S(1)} collective-permute-done((bf16[512,256]{1,0:T(8,128)(2,1)S(1)}, bf16[512,256]{1,0:T(8,128)(2,1)S(1)}, u32[]{:S(2)}, u32[]{:S(2)}) %collective-permute-start.7) | collective-permute-done | bytes 262176 | tf_op jit(solution)/shard_map/ppermute | solution.py:25
  62.5 1.8 %finish_last.1 = f32[2,256,256]{2,1,0:T(8,128)} custom-call(s32[1]{0:T(128)} %bitcast.refs_0_, bf16[512,256]{1,0:T(8,128)(2,1)S(1)} %collective-permute-done.4.refs_1_, bf16[512,256]{1,0:T(8,128)(2,1)S(1)} %collective-permute-done.7.refs_2_, bf16[2,16,384]{2,1,0:T(8,128)(2,1)S(1)} %pad_maximum_fusion.6.refs_3_.refs_4_.refs_2_, ...), custom_call_target="tpu_custom_call" | custom-call | flops 400000000 | bytes 5000000 | tf_op jit(solution)/shard_map/finish_last/pallas_call | solution.py:325
  (23 shorter events, 0.4 us)
Async XLA Ops:
  0.0 17.5 %copy-start.5 = (bf16[2,4,64,4,64]{4,3,2,1,0:T(4,128)(2,1)S(1)}, bf16[2,4,64,4,64]{4,3,2,1,0:T(4,128)(2,1)}, u32[]{:S(2)}) copy-start(bf16[2,4,64,4,64]{4,3,2,1,0:T(4,128)(2,1)} %param.13) | copy-start | bytes 786436
  2.3 1.0 %copy-start.1 = (f32[2,4,64,256]{3,2,1,0:T(8,128)S(1)}, f32[2,4,64,256]{3,2,1,0:T(8,128)}, u32[]{:S(2)}) copy-start(f32[2,4,64,256]{3,2,1,0:T(8,128)} %param.9) | copy-start | bytes 1572868
  3.5 19.3 %collective-permute-start = (bf16[2,208,256]{2,1,0:T(8,128)(2,1)S(1)}, bf16[2,208,256]{2,1,0:T(8,128)(2,1)S(1)}, u32[]{:S(2)}, u32[]{:S(2)}) collective-permute-start(bf16[2,208,256]{2,1,0:T(8,128)(2,1)S(1)} %get-tuple-element.26), channel_id=1, source_target_pairs={{0,1},{1,2},{2,3},{3,4},{4,5},{5,6},{6,7},{7,8},{8,9},{9,10},{10,1... | collective-permute-start | bytes 638984 | tf_op jit(solution)/shard_map/ppermute | solution.py:19
  6.7 16.2 %collective-permute-start.1 = (bf16[2,208,256]{2,1,0:T(8,128)(2,1)S(1)}, bf16[2,208,256]{2,1,0:T(8,128)(2,1)S(1)}, u32[]{:S(2)}, u32[]{:S(2)}) collective-permute-start(bf16[2,208,256]{2,1,0:T(8,128)(2,1)S(1)} %get-tuple-element.28), channel_id=1, source_target_pairs={{0,31},{1,0},{2,1},{3,2},{4,3},{5,4},{6,5},{7,6},{8,7},{9,8},{10,9... | collective-permute-start | bytes 638984 | tf_op jit(solution)/shard_map/ppermute | solution.py:19
  18.0 18.3 %collective-permute-start.2 = (bf16[784,256]{1,0:T(8,128)(2,1)S(1)}, bf16[784,256]{1,0:T(8,128)(2,1)S(1)}, u32[]{:S(2)}, u32[]{:S(2)}) collective-permute-start(bf16[784,256]{1,0:T(8,128)(2,1)S(1)} %pad_maximum_fusion.3), channel_id=1, source_target_pairs={{32,64},{96,128},{160,192},{224,256},{288,320},{352,384},{416,448}... | collective-permute-start | bytes 1204232 | tf_op jit(solution)/shard_map/ppermute | solution.py:25
  23.2 6.8 %copy-start.3 = (bf16[2,4,9,64,64]{4,3,2,1,0:T(8,128)(2,1)S(1)}, bf16[2,4,9,64,64]{4,3,2,1,0:T(8,128)(2,1)}, u32[]{:S(2)}) copy-start(bf16[2,4,9,64,64]{4,3,2,1,0:T(8,128)(2,1)} %precision_ref.1) | copy-start | bytes 1769476
  23.2 6.8 %copy-start.4 = (s32[2,4,9]{2,1,0:T(4,128)S(1)}, s32[2,4,9]{2,1,0:T(4,128)}, u32[]{:S(2)}) copy-start(s32[2,4,9]{2,1,0:T(4,128)} %pattern_ref) | copy-start | bytes 868
  23.4 12.9 %collective-permute-start.3 = (bf16[656,256]{1,0:T(8,128)(2,1)S(1)}, bf16[656,256]{1,0:T(8,128)(2,1)S(1)}, u32[]{:S(2)}, u32[]{:S(2)}) collective-permute-start(bf16[656,256]{1,0:T(8,128)(2,1)S(1)} %fusion.1), channel_id=1, source_target_pairs={{32,64},{96,128},{160,192},{224,256},{288,320},{352,384},{416,448}... | collective-permute-start | bytes 1007624 | tf_op jit(solution)/shard_map/ppermute | solution.py:25
  33.4 2.8 %copy-start = (bf16[2,2,4,64,256]{4,3,2,1,0:T(8,128)(2,1)S(1)}, bf16[2,2,4,64,256]{4,3,2,1,0:T(8,128)(2,1)}, u32[]{:S(2)}) copy-start(bf16[2,2,4,64,256]{4,3,2,1,0:T(8,128)(2,1)} %param.10) | copy-start | bytes 1572868
  33.4 2.9 %copy-start.2 = (f32[2,4,64,256]{3,2,1,0:T(8,128)S(1)}, f32[2,4,64,256]{3,2,1,0:T(8,128)}, u32[]{:S(2)}) copy-start(f32[2,4,64,256]{3,2,1,0:T(8,128)} %param.9) | copy-start | bytes 1572868
  38.1 13.0 %collective-permute-start.5 = (bf16[2,128,256]{2,1,0:T(8,128)(2,1)S(1)}, bf16[2,128,256]{2,1,0:T(8,128)(2,1)S(1)}, u32[]{:S(2)}, u32[]{:S(2)}) collective-permute-start(bf16[2,128,256]{2,1,0:T(8,128)(2,1)S(1)} %get-tuple-element.48), channel_id=1, source_target_pairs={{0,1},{1,2},{2,3},{3,4},{4,5},{5,6},{6,7},{7,8},{8,9},{9,10},{10,1... | collective-permute-start | bytes 393224 | tf_op jit(solution)/shard_map/ppermute | solution.py:19
  40.0 11.1 %collective-permute-start.6 = (bf16[2,128,256]{2,1,0:T(8,128)(2,1)S(1)}, bf16[2,128,256]{2,1,0:T(8,128)(2,1)S(1)}, u32[]{:S(2)}, u32[]{:S(2)}) collective-permute-start(bf16[2,128,256]{2,1,0:T(8,128)(2,1)S(1)} %get-tuple-element.47), channel_id=1, source_target_pairs={{0,31},{1,0},{2,1},{3,2},{4,3},{5,4},{6,5},{7,6},{8,7},{9,8},{10,9... | collective-permute-start | bytes 393224 | tf_op jit(solution)/shard_map/ppermute | solution.py:19
  45.9 14.9 %collective-permute-start.4 = (bf16[512,256]{1,0:T(8,128)(2,1)S(1)}, bf16[512,256]{1,0:T(8,128)(2,1)S(1)}, u32[]{:S(2)}, u32[]{:S(2)}) collective-permute-start(bf16[512,256]{1,0:T(8,128)(2,1)S(1)} %bitcast.27), channel_id=1, source_target_pairs={{32,64},{96,128},{160,192},{224,256},{288,320},{352,384},{416,448}... | collective-permute-start | bytes 786440 | tf_op jit(solution)/shard_map/ppermute | solution.py:25
  51.2 11.3 %collective-permute-start.7 = (bf16[512,256]{1,0:T(8,128)(2,1)S(1)}, bf16[512,256]{1,0:T(8,128)(2,1)S(1)}, u32[]{:S(2)}, u32[]{:S(2)}) collective-permute-start(bf16[512,256]{1,0:T(8,128)(2,1)S(1)} %bitcast.36), channel_id=1, source_target_pairs={{32,64},{96,128},{160,192},{224,256},{288,320},{352,384},{416,448}... | collective-permute-start | bytes 786440 | tf_op jit(solution)/shard_map/ppermute | solution.py:25

commit v6 on v5

--- a/solution.py
+++ b/solution.py
@@ -158,9 +158,10 @@
 
 def middle_kernel(first, *refs):
     if first:
-        side_ref, x_ref, fw_ref, mt_ref, pair_ref, halo_ref, lp_ref = refs[:7]
-        lfm_ref, lam_ref, lft_ref, lat_ref, mtt_ref, part_ref, grad_ref = refs[7:14]
-        mate_ref, res_ref = refs[14:]
+        side_ref, pattern_ref, x_ref, fw_ref, mt_ref, pair_ref, halo_ref, precision_ref = refs[:8]
+        lfm_ref, lam_ref, lft_ref, lat_ref, mtt_ref, part_ref, grad_ref, lp_ref = refs[8:16]
+        mate_ref, res_ref, slot_ref = refs[16:]
+        prior_matrix_kernel(pattern_ref, precision_ref, lp_ref, slot_ref)
     else:
         (side_ref, x_ref, mt_ref, pair_ref, halo_ref, lp_ref) = refs[:6]
         lfm_ref, lam_ref, lft_ref, lat_ref, mtt_ref, lff_ref = refs[6:12]
@@ -345,13 +346,15 @@
             shape((16, 384)),
         ]
     outs += [shape((2, 384, 256), F32), shape((2, 256, 256), F32)]
+    outs += [shape((2, 2, 3, 128, 256))] if first else []
     return call(
         lambda *refs: middle_kernel(first, *refs),
         "middle_first" if first else "middle_last",
         outs,
         args,
-        "s" + "v" * (len(args) - 1),
-        scratch=[pltpu.VMEM((2, 512, 256), BF), pltpu.VMEM((2, 384, 256), BF)],
+        ("ss" if first else "s") + "v" * (len(args) - (2 if first else 1)),
+        scratch=[pltpu.VMEM((2, 512, 256), BF), pltpu.VMEM((2, 384, 256), BF)]
+        + ([pltpu.SMEM((72,), jnp.int32)] if first else []),
         flops=1000000,
         moved=100000,
     )
@@ -438,17 +441,7 @@
         return pair, lax.all_gather(halo, "lat", axis_index_groups=groups)
 
     halo = jnp.concatenate([west[:, :128], east[:, :128]], axis=1).reshape(512, 256)
-    mate_own, halo, late_pattern = lax.optimization_barrier((compact, halo, pattern))
-    (lp,) = call(
-        prior_matrix_kernel,
-        "prior_matrix",
-        [shape((2, 2, 3, 128, 256))],
-        (late_pattern, precision),
-        "sv",
-        scratch=[pltpu.SMEM((72,), jnp.int32)],
-        flops=2000000,
-        moved=3000000,
-    )
+    mate_own, halo = lax.optimization_barrier((compact, halo))
     meta = jnp.concatenate([west[:, 192:, :64], east[:, 192:, :64]], axis=2)
     meta = jnp.pad(near_row(meta), ((0, 0), (0, 128)))
     foot = [near_row(west[:, 128:192]), near_row(east[:, 128:192]), meta]
@@ -456,8 +449,8 @@
     mate_meta = jnp.pad(jnp.where(side == 0, mt[1], mt[0]), ((0, 0), (0, 128)))
     mate_foot = [jnp.where(side == 0, fw[1], fw[0]), mate_meta[:, :256], mate_meta[:, 256:]]
     pair, halo = mates(mate_own, halo, mate_foot)
-    lfm, lam, lft, lat, mtt, part, grad = middle_call(
-        True, (sides, middle, fw, mt, pair, halo, lp)
+    lfm, lam, lft, lat, mtt, part, grad, lp = middle_call(
+        True, (sides, pattern, middle, fw, mt, pair, halo, precision)
     )
     sample, compact, lff, laf, mtf = finish_call(
         True, (sides, middle, own_far, halo_far, mt, lp, lfm, lam, part, grad, sample, noise)

time: 64.7 us -> 64.4 us (level)
    pallas_call x6 -> x5, Pallas kernels: 8.63 us -> 8.32 us  [call(): pl.pallas_call(kernel, name=name, out_shape=tuple(outs), in_specs=[pl.Blo...]
  transfers between devices with their start and end apart: 8 -> 8, of which waited for: 1 -> 1; matrix products, arithmetic and copies ran while one was open for 1% -> 1% of each run, Pallas kernels for 8% -> 7%
where the time goes in v6:
time: 64.4 us; the launch traced here: 64 us
  starting transfers between devices  40.2 us (62%)
  blocking collectives  9.03 us (14%)
  Pallas kernels  8.32 us (13%)
  local copies, waits for them, and re-layouts  2.88 us (4%)
  waiting for transfers between devices  1.76 us (3%)
  other arithmetic  1.38 us (2%)
    ppermute x4, starting transfers between devices, shift_lon(): lax.ppermute(block, 'lon', [(i, (i + by) % count) for i in range(count)])  21.7 us
    ppermute x4, starting transfers between devices, swap_lat(): return lax.ppermute(block, 'lat', pairs + [(b, a) for a, b in pairs])  18.5 us
    pallas_call x5, Pallas kernels, call(): pl.pallas_call(kernel, name=name, out_shape=tuple(outs), in_specs=[pl.Blo...  8.32 us
    all_gather x2, blocking collectives, mates(): return (pair, lax.all_gather(halo, 'lat', axis_index_groups=groups))  4.67 us
    all_gather x2, blocking collectives, mates(): pair = lax.all_gather(compact, 'lat', axis_index_groups=groups)  4.36 us
    ppermute x4, waiting for transfers between devices, swap_lat(): return lax.ppermute(block, 'lat', pairs + [(b, a) for a, b in pairs])  1.75 us
    reshape x1, local copies, waits for them, and re-layouts, local(): fw = foot_weight.reshape(2, 256, 256)  1.52 us
  transfers between devices with their start and end apart: 8, of which 1 were waited for; matrix products, arithmetic and copies ran while one was open for 1% of the time, Pallas kernels for 7%

profile of v6, /device:TPU:25, one launch (start us, length us, event | category | flops | bytes accessed | tf_op | source)
XLA Modules:
  0.0 64.0 jit_solution(6799184751433908779)
XLA Ops:
  0.0 0.0 copy-start.5
  0.0 1.5 %reshape.54.fw_ref = bf16[2,256,256]{2,1,0:T(8,128)(2,1)S(1)} reshape(bf16[2,4,64,4,64]{4,3,2,1,0:T(4,128)(2,1)} %param.13) | data formatting | bytes 524288 | tf_op jit(solution)/shard_map/reshape | solution.py:407
  1.5 0.8 %select_select_fusion.stats_ref = f32[2,4,8,64]{3,2,1,0:T(8,128)S(1)} fusion(s32[2,4,4,64]{3,2,1,0:T(4,128)} %bitcast.38, f32[2,4,64]{2,1,0:T(4,128)} %param.16, f32[2,4,64]{2,1,0:T(4,128)} %param.17, s32[2,4,64]{2,1,0:T(4,128)} %param.15, pred[8]{0:T(512)(128)(4,1)S(1)} %get-tuple-element.51, pred[8]{0:T(512)(128)(4,1)S(1)} %get-tuple-element.52), kind=kLoop, calls=%fused_computation.16 | loop fusion | flops 20480 | bytes 30736 | tf_op jit(solution)/shard_map/jit(_where)/select_n | solution.py:412
  2.3 0.0 copy-start.1
  2.4 1.0 %copy-done.1 = f32[2,4,64,256]{3,2,1,0:T(8,128)S(1)} copy-done((f32[2,4,64,256]{3,2,1,0:T(8,128)S(1)}, f32[2,4,64,256]{3,2,1,0:T(8,128)}, u32[]{:S(2)}) %copy-start.1) | copy-done | bytes 524312
  3.4 0.2 prepare.1
  3.5 3.1 %collective-permute-start = (bf16[2,208,256]{2,1,0:T(8,128)(2,1)S(1)}, bf16[2,208,256]{2,1,0:T(8,128)(2,1)S(1)}, u32[]{:S(2)}, u32[]{:S(2)}) collective-permute-start(bf16[2,208,256]{2,1,0:T(8,128)(2,1)S(1)} %get-tuple-element.26), channel_id=1, source_target_pairs={{0,1},{1,2},{2,3},{3,4},{4,5},{5,6},{6,7},{7,8},{8,9},{9,10},{10,1... | collective-permute-start | bytes 638984 | tf_op jit(solution)/shard_map/ppermute | solution.py:19
  6.7 10.9 %collective-permute-start.1 = (bf16[2,208,256]{2,1,0:T(8,128)(2,1)S(1)}, bf16[2,208,256]{2,1,0:T(8,128)(2,1)S(1)}, u32[]{:S(2)}, u32[]{:S(2)}) collective-permute-start(bf16[2,208,256]{2,1,0:T(8,128)(2,1)S(1)} %get-tuple-element.28), channel_id=1, source_target_pairs={{0,31},{1,0},{2,1},{3,2},{4,3},{5,4},{6,5},{7,6},{8,7},{9,8},{10,9... | collective-permute-start | bytes 638984 | tf_op jit(solution)/shard_map/ppermute | solution.py:19
  17.5 0.0 copy-done.5
  17.5 0.1 slice_select_fusion
  17.7 0.2 select_n.98
  18.0 4.9 %collective-permute-start.2 = (bf16[784,256]{1,0:T(8,128)(2,1)S(1)}, bf16[784,256]{1,0:T(8,128)(2,1)S(1)}, u32[]{:S(2)}, u32[]{:S(2)}) collective-permute-start(bf16[784,256]{1,0:T(8,128)(2,1)S(1)} %pad_maximum_fusion.3), channel_id=1, source_target_pairs={{32,64},{96,128},{160,192},{224,256},{288,320},{352,384},{416,448}... | collective-permute-start | bytes 1204232 | tf_op jit(solution)/shard_map/ppermute | solution.py:25
  22.8 0.0 collective-permute-done
  22.8 0.0 collective-permute-done.1
  22.9 0.1 fusion.8
  22.9 0.1 pad_maximum_fusion.6.refs_4_.refs_2_.refs_3_
  23.3 0.0 copy-start.3
  23.3 0.0 copy-start.4
  23.4 4.5 %collective-permute-start.3 = (bf16[656,256]{1,0:T(8,128)(2,1)S(1)}, bf16[656,256]{1,0:T(8,128)(2,1)S(1)}, u32[]{:S(2)}, u32[]{:S(2)}) collective-permute-start(bf16[656,256]{1,0:T(8,128)(2,1)S(1)} %fusion.1), channel_id=1, source_target_pairs={{32,64},{96,128},{160,192},{224,256},{288,320},{352,384},{416,448}... | collective-permute-start | bytes 1007624 | tf_op jit(solution)/shard_map/ppermute | solution.py:25
  27.8 2.2 %all-gather = bf16[4,256,256]{2,1,0:T(8,128)(2,1)S(1)} all-gather(bf16[2,256,256]{2,1,0:T(8,128)(2,1)S(1)} %get-tuple-element.31), channel_id=2, replica_groups={{0,32},{64,96},{128,160},{192,224},{256,288},{320,352},{384,416},{448,4..., dimensions={0}, use_global_device_ids=true | all-gather | bytes 786432 | tf_op jit(solution)/shard_map/all_gather | solution.py:439
  30.0 2.5 %all-gather.1 = bf16[1856,256]{1,0:T(8,128)(2,1)S(1)} all-gather(bf16[928,256]{1,0:T(8,128)(2,1)S(1)} %pad_maximum_fusion.2), channel_id=3, replica_groups={{0,32},{64,96},{128,160},{192,224},{256,288},{320,352},{384,416},{448,4..., dimensions={0}, use_global_device_ids=true | all-gather | bytes 1425408 | tf_op jit(solution)/shard_map/all_gather | solution.py:441
  32.5 0.0 copy-done.3
  32.5 0.0 copy-done.4
  32.5 0.0 copy-start
  32.5 0.0 copy-start.2
  32.5 3.4 %middle_first.1 = (bf16[2,2,3,256,256]{4,3,2,1,0:T(8,128)(2,1)S(1)}, bf16[2,2,2,128,256]{4,3,2,1,0:T(8,128)(2,1)S(1)}, bf16[2,3,256,256]{3,2,1,0:T(8,128)(2,1)S(...) custom-call(s32[1]{0:T(128)} %bitcast.refs_0_, ...), custom_call_target="tpu_custom_call" | custom-call | flops 1000000 | bytes 100000 | tf_op jit(solution)/shard_map/middle_first/pallas_call | solution.py:326
  36.0 0.0 collective-permute-done.2.refs_2_
  36.0 0.0 collective-permute-done.3.refs_3_
  36.0 0.0 copy-done
  36.0 0.0 copy-done.2
  36.0 1.8 %finish_first.1 = (f32[2,256,256]{2,1,0:T(8,128)S(1)}, bf16[2,256,256]{2,1,0:T(8,128)(2,1)S(1)}, bf16[2,3,256,256]{3,2,1,0:T(8,128)(2,1)S(1)}, bf16[2,128,256]{2,1,0:T(8,128)(2,1)S(1)}, bf16[16,384]{1,0:T(8,128)(2,1)S(1)}) custom-call(s32[1]{0:T(128)} %bitcast.refs_0_, bf16[2,512,256]{2,1,0:T(8,128)(2,1)S(1)} %pad_maximum_fusion.refs_2_.refs_1_, ...), custom_call_target="tpu_custom_call" | custom-call | flops 400000000 | bytes 5000000 | tf_op jit(solution)/shard_map/finish_first/pallas_call | solution.py:326
  37.8 1.9 %collective-permute-start.5 = (bf16[2,128,256]{2,1,0:T(8,128)(2,1)S(1)}, bf16[2,128,256]{2,1,0:T(8,128)(2,1)S(1)}, u32[]{:S(2)}, u32[]{:S(2)}) collective-permute-start(bf16[2,128,256]{2,1,0:T(8,128)(2,1)S(1)} %get-tuple-element.48), channel_id=1, source_target_pairs={{0,1},{1,2},{2,3},{3,4},{4,5},{5,6},{6,7},{7,8},{8,9},{9,10},{10,1... | collective-permute-start | bytes 393224 | tf_op jit(solution)/shard_map/ppermute | solution.py:19
  39.8 5.8 %collective-permute-start.6 = (bf16[2,128,256]{2,1,0:T(8,128)(2,1)S(1)}, bf16[2,128,256]{2,1,0:T(8,128)(2,1)S(1)}, u32[]{:S(2)}, u32[]{:S(2)}) collective-permute-start(bf16[2,128,256]{2,1,0:T(8,128)(2,1)S(1)} %get-tuple-element.47), channel_id=1, source_target_pairs={{0,31},{1,0},{2,1},{3,2},{4,3},{5,4},{6,5},{7,6},{8,7},{9,8},{10,9... | collective-permute-start | bytes 393224 | tf_op jit(solution)/shard_map/ppermute | solution.py:19
  45.6 5.2 %collective-permute-start.4 = (bf16[512,256]{1,0:T(8,128)(2,1)S(1)}, bf16[512,256]{1,0:T(8,128)(2,1)S(1)}, u32[]{:S(2)}, u32[]{:S(2)}) collective-permute-start(bf16[512,256]{1,0:T(8,128)(2,1)S(1)} %bitcast.27), channel_id=1, source_target_pairs={{32,64},{96,128},{160,192},{224,256},{288,320},{352,384},{416,448}... | collective-permute-start | bytes 786440 | tf_op jit(solution)/shard_map/ppermute | solution.py:25
  50.8 0.0 collective-permute-done.5
  50.9 0.0 collective-permute-done.6
  50.9 4.0 %collective-permute-start.7 = (bf16[512,256]{1,0:T(8,128)(2,1)S(1)}, bf16[512,256]{1,0:T(8,128)(2,1)S(1)}, u32[]{:S(2)}, u32[]{:S(2)}) collective-permute-start(bf16[512,256]{1,0:T(8,128)(2,1)S(1)} %bitcast.36), channel_id=1, source_target_pairs={{32,64},{96,128},{160,192},{224,256},{288,320},{352,384},{416,448}... | collective-permute-start | bytes 786440 | tf_op jit(solution)/shard_map/ppermute | solution.py:25
  54.9 2.2 %all-gather.2 = bf16[4,256,256]{2,1,0:T(8,128)(2,1)S(1)} all-gather(bf16[2,256,256]{2,1,0:T(8,128)(2,1)S(1)} %get-tuple-element.37), channel_id=4, replica_groups={{0,32},{64,96},{128,160},{192,224},{256,288},{320,352},{384,416},{448,4..., dimensions={0}, use_global_device_ids=true | all-gather | bytes 786432 | tf_op jit(solution)/shard_map/all_gather | solution.py:439
  57.1 2.2 %all_gather.27.refs_4_ = bf16[2,512,256]{2,1,0:T(8,128)(2,1)S(1)} all-gather(bf16[1,512,256]{2,1,0:T(8,128)(2,1)S(1)} %bitcast.37), channel_id=1, replica_groups={{0,32},{64,96},{128,160},{192,224},{256,288},{320,352},{384,416},{448,4..., dimensions={0}, use_global_device_ids=true | all-gather | bytes 786432 | tf_op jit(solution)/shard_map/all_gather | solution.py:441
  59.3 1.1 %middle_last.1 = (f32[2,384,256]{2,1,0:T(8,128)S(1)}, f32[2,256,256]{2,1,0:T(8,128)S(1)}) custom-call(s32[1]{0:T(128)} %bitcast.refs_0_, bf16[2,512,256]{2,1,0:T(8,128)(2,1)S(1)} %pad_maximum_fusion.1.refs_1_, bf16[2,16,384]{2,1,0:T(8,128)(2,1)S(1)} %pad_maximum_fusion.6.refs_4_.refs_2_.refs_3_, bf16[2,2,256,256]{3,2,1,0:T(8,128)(2,1)S(1)} %bitcast.33, ...), custom_call_target="tpu_custom_call" | custom-call | flops 1000000 | bytes 100000 | tf_op jit(solution)/shard_map/middle_last/pallas_call | solution.py:326
  60.4 0.0 collective-permute-done.4.refs_1_
  60.4 1.7 %collective-permute-done.7.refs_2_ = bf16[512,256]{1,0:T(8,128)(2,1)S(1)} collective-permute-done((bf16[512,256]{1,0:T(8,128)(2,1)S(1)}, bf16[512,256]{1,0:T(8,128)(2,1)S(1)}, u32[]{:S(2)}, u32[]{:S(2)}) %collective-permute-start.7) | collective-permute-done | bytes 262176 | tf_op jit(solution)/shard_map/ppermute | solution.py:25
  62.2 1.8 %finish_last.1 = f32[2,256,256]{2,1,0:T(8,128)} custom-call(s32[1]{0:T(128)} %bitcast.refs_0_, bf16[512,256]{1,0:T(8,128)(2,1)S(1)} %collective-permute-done.4.refs_1_, bf16[512,256]{1,0:T(8,128)(2,1)S(1)} %collective-permute-done.7.refs_2_, bf16[2,16,384]{2,1,0:T(8,128)(2,1)S(1)} %pad_maximum_fusion.6.refs_4_.refs_2_.refs_3_, ...), custom_call_target="tpu_custom_call" | custom-call | flops 400000000 | bytes 5000000 | tf_op jit(solution)/shard_map/finish_last/pallas_call | solution.py:326
  (23 shorter events, 0.4 us)
Async XLA Ops:
  0.0 17.5 %copy-start.5 = (bf16[2,4,64,4,64]{4,3,2,1,0:T(4,128)(2,1)S(1)}, bf16[2,4,64,4,64]{4,3,2,1,0:T(4,128)(2,1)}, u32[]{:S(2)}) copy-start(bf16[2,4,64,4,64]{4,3,2,1,0:T(4,128)(2,1)} %param.13) | copy-start | bytes 786436
  2.3 1.0 %copy-start.1 = (f32[2,4,64,256]{3,2,1,0:T(8,128)S(1)}, f32[2,4,64,256]{3,2,1,0:T(8,128)}, u32[]{:S(2)}) copy-start(f32[2,4,64,256]{3,2,1,0:T(8,128)} %param.9) | copy-start | bytes 1572868
  3.5 19.3 %collective-permute-start = (bf16[2,208,256]{2,1,0:T(8,128)(2,1)S(1)}, bf16[2,208,256]{2,1,0:T(8,128)(2,1)S(1)}, u32[]{:S(2)}, u32[]{:S(2)}) collective-permute-start(bf16[2,208,256]{2,1,0:T(8,128)(2,1)S(1)} %get-tuple-element.26), channel_id=1, source_target_pairs={{0,1},{1,2},{2,3},{3,4},{4,5},{5,6},{6,7},{7,8},{8,9},{9,10},{10,1... | collective-permute-start | bytes 638984 | tf_op jit(solution)/shard_map/ppermute | solution.py:19
  6.7 16.2 %collective-permute-start.1 = (bf16[2,208,256]{2,1,0:T(8,128)(2,1)S(1)}, bf16[2,208,256]{2,1,0:T(8,128)(2,1)S(1)}, u32[]{:S(2)}, u32[]{:S(2)}) collective-permute-start(bf16[2,208,256]{2,1,0:T(8,128)(2,1)S(1)} %get-tuple-element.28), channel_id=1, source_target_pairs={{0,31},{1,0},{2,1},{3,2},{4,3},{5,4},{6,5},{7,6},{8,7},{9,8},{10,9... | collective-permute-start | bytes 638984 | tf_op jit(solution)/shard_map/ppermute | solution.py:19
  18.0 18.0 %collective-permute-start.2 = (bf16[784,256]{1,0:T(8,128)(2,1)S(1)}, bf16[784,256]{1,0:T(8,128)(2,1)S(1)}, u32[]{:S(2)}, u32[]{:S(2)}) collective-permute-start(bf16[784,256]{1,0:T(8,128)(2,1)S(1)} %pad_maximum_fusion.3), channel_id=1, source_target_pairs={{32,64},{96,128},{160,192},{224,256},{288,320},{352,384},{416,448}... | collective-permute-start | bytes 1204232 | tf_op jit(solution)/shard_map/ppermute | solution.py:25
  23.3 9.2 %copy-start.3 = (bf16[2,4,9,64,64]{4,3,2,1,0:T(8,128)(2,1)S(1)}, bf16[2,4,9,64,64]{4,3,2,1,0:T(8,128)(2,1)}, u32[]{:S(2)}) copy-start(bf16[2,4,9,64,64]{4,3,2,1,0:T(8,128)(2,1)} %refs_7_.1) | copy-start | bytes 1769476
  23.3 9.2 %copy-start.4 = (s32[2,4,9]{2,1,0:T(4,128)S(1)}, s32[2,4,9]{2,1,0:T(4,128)}, u32[]{:S(2)}) copy-start(s32[2,4,9]{2,1,0:T(4,128)} %refs_1_.1) | copy-start | bytes 868
  23.4 12.6 %collective-permute-start.3 = (bf16[656,256]{1,0:T(8,128)(2,1)S(1)}, bf16[656,256]{1,0:T(8,128)(2,1)S(1)}, u32[]{:S(2)}, u32[]{:S(2)}) collective-permute-start(bf16[656,256]{1,0:T(8,128)(2,1)S(1)} %fusion.1), channel_id=1, source_target_pairs={{32,64},{96,128},{160,192},{224,256},{288,320},{352,384},{416,448}... | collective-permute-start | bytes 1007624 | tf_op jit(solution)/shard_map/ppermute | solution.py:25
  32.5 3.5 %copy-start = (bf16[2,2,4,64,256]{4,3,2,1,0:T(8,128)(2,1)S(1)}, bf16[2,2,4,64,256]{4,3,2,1,0:T(8,128)(2,1)}, u32[]{:S(2)}) copy-start(bf16[2,2,4,64,256]{4,3,2,1,0:T(8,128)(2,1)} %param.10) | copy-start | bytes 1572868
  32.5 3.5 %copy-start.2 = (f32[2,4,64,256]{3,2,1,0:T(8,128)S(1)}, f32[2,4,64,256]{3,2,1,0:T(8,128)}, u32[]{:S(2)}) copy-start(f32[2,4,64,256]{3,2,1,0:T(8,128)} %param.9) | copy-start | bytes 1572868
  37.8 13.0 %collective-permute-start.5 = (bf16[2,128,256]{2,1,0:T(8,128)(2,1)S(1)}, bf16[2,128,256]{2,1,0:T(8,128)(2,1)S(1)}, u32[]{:S(2)}, u32[]{:S(2)}) collective-permute-start(bf16[2,128,256]{2,1,0:T(8,128)(2,1)S(1)} %get-tuple-element.48), channel_id=1, source_target_pairs={{0,1},{1,2},{2,3},{3,4},{4,5},{5,6},{6,7},{7,8},{8,9},{9,10},{10,1... | collective-permute-start | bytes 393224 | tf_op jit(solution)/shard_map/ppermute | solution.py:19
  39.8 11.1 %collective-permute-start.6 = (bf16[2,128,256]{2,1,0:T(8,128)(2,1)S(1)}, bf16[2,128,256]{2,1,0:T(8,128)(2,1)S(1)}, u32[]{:S(2)}, u32[]{:S(2)}) collective-permute-start(bf16[2,128,256]{2,1,0:T(8,128)(2,1)S(1)} %get-tuple-element.47), channel_id=1, source_target_pairs={{0,31},{1,0},{2,1},{3,2},{4,3},{5,4},{6,5},{7,6},{8,7},{9,8},{10,9... | collective-permute-start | bytes 393224 | tf_op jit(solution)/shard_map/ppermute | solution.py:19
  45.6 14.8 %collective-permute-start.4 = (bf16[512,256]{1,0:T(8,128)(2,1)S(1)}, bf16[512,256]{1,0:T(8,128)(2,1)S(1)}, u32[]{:S(2)}, u32[]{:S(2)}) collective-permute-start(bf16[512,256]{1,0:T(8,128)(2,1)S(1)} %bitcast.27), channel_id=1, source_target_pairs={{32,64},{96,128},{160,192},{224,256},{288,320},{352,384},{416,448}... | collective-permute-start | bytes 786440 | tf_op jit(solution)/shard_map/ppermute | solution.py:25
  50.9 11.3 %collective-permute-start.7 = (bf16[512,256]{1,0:T(8,128)(2,1)S(1)}, bf16[512,256]{1,0:T(8,128)(2,1)S(1)}, u32[]{:S(2)}, u32[]{:S(2)}) collective-permute-start(bf16[512,256]{1,0:T(8,128)(2,1)S(1)} %bitcast.36), channel_id=1, source_target_pairs={{32,64},{96,128},{160,192},{224,256},{288,320},{352,384},{416,448}... | collective-permute-start | bytes 786440 | tf_op jit(solution)/shard_map/ppermute | solution.py:25

commit v7 on v6

--- a/solution.py
+++ b/solution.py
@@ -75,9 +75,9 @@
     return lax.broadcasted_iota(jnp.int32, (1, n), 1) // 64
 
 
-def build_forward(weights, meta, store):
+def build_forward(weights, meta, store, owners=range(6)):
     codes = jnp.transpose(meta, (1, 0))
-    for oc in range(6):
+    for oc in owners:
         rows = slice(oc * 64, (oc + 1) * 64)
         pair, code = [], []
         for j in range(4):
@@ -159,8 +159,10 @@
 def middle_kernel(first, *refs):
     if first:
         side_ref, pattern_ref, x_ref, fw_ref, mt_ref, pair_ref, halo_ref, precision_ref = refs[:8]
-        lfm_ref, lam_ref, lft_ref, lat_ref, mtt_ref, part_ref, grad_ref, lp_ref = refs[8:16]
-        mate_ref, res_ref, slot_ref = refs[16:]
+        far_ref = refs[8]
+        lfm_ref, lam_ref, lft_ref, lat_ref, mtt_ref, part_ref, grad_ref, lp_ref = refs[9:17]
+        early_ref = refs[17]
+        mate_ref, res_ref, slot_ref = refs[18:]
         prior_matrix_kernel(pattern_ref, precision_ref, lp_ref, slot_ref)
     else:
         (side_ref, x_ref, mt_ref, pair_ref, halo_ref, lp_ref) = refs[:6]
@@ -198,6 +200,19 @@
             lat_ref[p, rows, :] = value
 
         build_forward(weights, meta, put_mate)
+
+        def put_early(q, dr, rows, lanes, value):
+            early_ref[q, dr, rows, lanes] = value
+
+        blank, edge = jnp.zeros((64, 256), F32), jnp.zeros((16, 64), F32)
+        far_weights = [blank, far_ref[512:768, :].astype(F32), blank]
+        far_meta = [edge, far_ref[768:784, :].astype(F32), edge]
+        build_forward(
+            jnp.concatenate(far_weights, axis=0),
+            jnp.concatenate(far_meta, axis=1),
+            put_early,
+            range(1, 5),
+        )
         build_adjoint(jnp.transpose(weights, (1, 0)), meta, 2 * side, put_mate_adjoint)
 
     parts = forward(
@@ -235,9 +250,9 @@
 def finish_kernel(first, *refs):
     if first:
         (side_ref, x_ref, own_ref, halo_ref, mt_ref, lp_ref, lfm_ref, lam_ref) = refs[:8]
-        part_ref, grad_ref, sample_ref, noise_hbm = refs[8:12]
-        out_ref, compact_ref, lff_ref, laf_ref, mtf_ref = refs[12:17]
-        res_ref, far_ref, sample_buf, noise_buf, sems = refs[17:]
+        part_ref, grad_ref, early_ref, sample_ref, noise_hbm = refs[8:13]
+        out_ref, compact_ref, lff_ref, laf_ref, mtf_ref = refs[13:18]
+        res_ref, far_ref, sample_buf, noise_buf, sems = refs[18:]
     else:
         (side_ref, own_ref, halo_ref, mt_ref, lp_ref, lfm_ref, lam_ref, part_ref) = refs[:8]
         grad_ref, lff_ref, laf_ref, mtf_ref, sample_ref, noise_hbm = refs[8:14]
@@ -267,7 +282,9 @@
         def put_adjoint(p, rows, value):
             laf_ref[p, rows, :] = value
 
-        build_forward(weights, meta, put)
+        lff_ref[0, :, 64:256, :] = early_ref[0, :, 64:256, :]
+        lff_ref[1, :, 0:192, :] = early_ref[1, :, 0:192, :]
+        build_forward(weights, meta, put, (0, 5))
         build_adjoint(jnp.transpose(weights, (1, 0)), meta, 2 - 2 * side, put_adjoint)
     nearest = far_ref.at[1 - side]
     parts = forward([(lambda q: lfm_ref[side, q, 2 * side], nearest)])
@@ -346,7 +363,7 @@
             shape((16, 384)),
         ]
     outs += [shape((2, 384, 256), F32), shape((2, 256, 256), F32)]
-    outs += [shape((2, 2, 3, 128, 256))] if first else []
+    outs += [shape((2, 2, 3, 128, 256)), shape((2, 3, 256, 256))] if first else []
     return call(
         lambda *refs: middle_kernel(first, *refs),
         "middle_first" if first else "middle_last",
@@ -449,11 +466,11 @@
     mate_meta = jnp.pad(jnp.where(side == 0, mt[1], mt[0]), ((0, 0), (0, 128)))
     mate_foot = [jnp.where(side == 0, fw[1], fw[0]), mate_meta[:, :256], mate_meta[:, 256:]]
     pair, halo = mates(mate_own, halo, mate_foot)
-    lfm, lam, lft, lat, mtt, part, grad, lp = middle_call(
-        True, (sides, pattern, middle, fw, mt, pair, halo, precision)
+    lfm, lam, lft, lat, mtt, part, grad, lp, early = middle_call(
+        True, (sides, pattern, middle, fw, mt, pair, halo, precision, own_far)
     )
     sample, compact, lff, laf, mtf = finish_call(
-        True, (sides, middle, own_far, halo_far, mt, lp, lfm, lam, part, grad, sample, noise)
+        True, (sides, middle, own_far, halo_far, mt, lp, lfm, lam, part, grad, early, sample, noise)
     )
 
     west = shift_lon(compact[:, 128:], 1)

time: 64.4 us -> 64.7 us (level)
  transfers between devices with their start and end apart: 8 -> 8, of which waited for: 1 -> 1; matrix products, arithmetic and copies ran while one was open for 1% -> 1% of each run, Pallas kernels for 7% -> 8%
where the time goes in v7:
time: 64.7 us; the launch traced here: 64.2 us
  starting transfers between devices  40.2 us (62%)
  blocking collectives  9.03 us (14%)
  Pallas kernels  8.58 us (13%)
  local copies, waits for them, and re-layouts  2.89 us (4%)
  waiting for transfers between devices  1.72 us (3%)
  other arithmetic  1.38 us (2%)
    ppermute x4, starting transfers between devices, shift_lon(): lax.ppermute(block, 'lon', [(i, (i + by) % count) for i in range(count)])  21.7 us
    ppermute x4, starting transfers between devices, swap_lat(): return lax.ppermute(block, 'lat', pairs + [(b, a) for a, b in pairs])  18.5 us
    pallas_call x5, Pallas kernels, call(): pl.pallas_call(kernel, name=name, out_shape=tuple(outs), in_specs=[pl.Blo...  8.58 us
    all_gather x2, blocking collectives, mates(): return (pair, lax.all_gather(halo, 'lat', axis_index_groups=groups))  4.67 us
    all_gather x2, blocking collectives, mates(): pair = lax.all_gather(compact, 'lat', axis_index_groups=groups)  4.36 us
    ppermute x4, waiting for transfers between devices, swap_lat(): return lax.ppermute(block, 'lat', pairs + [(b, a) for a, b in pairs])  1.71 us
    reshape x1, local copies, waits for them, and re-layouts, local(): fw = foot_weight.reshape(2, 256, 256)  1.52 us
  transfers between devices with their start and end apart: 8, of which 1 were waited for; matrix products, arithmetic and copies ran while one was open for 1% of the time, Pallas kernels for 8%

profile of v7, /device:TPU:25, one launch (start us, length us, event | category | flops | bytes accessed | tf_op | source)
XLA Modules:
  0.0 64.2 jit_solution(12991662762308864169)
XLA Ops:
  0.0 0.0 copy-start.5
  0.0 1.5 %reshape.54.fw_ref = bf16[2,256,256]{2,1,0:T(8,128)(2,1)S(1)} reshape(bf16[2,4,64,4,64]{4,3,2,1,0:T(4,128)(2,1)} %param.13) | data formatting | bytes 524288 | tf_op jit(solution)/shard_map/reshape | solution.py:424
  1.5 0.8 %select_select_fusion.stats_ref = f32[2,4,8,64]{3,2,1,0:T(8,128)S(1)} fusion(s32[2,4,4,64]{3,2,1,0:T(4,128)} %bitcast.38, f32[2,4,64]{2,1,0:T(4,128)} %param.16, f32[2,4,64]{2,1,0:T(4,128)} %param.17, s32[2,4,64]{2,1,0:T(4,128)} %param.15, pred[8]{0:T(512)(128)(4,1)S(1)} %get-tuple-element.53, pred[8]{0:T(512)(128)(4,1)S(1)} %get-tuple-element.54), kind=kLoop, calls=%fused_computation.16 | loop fusion | flops 20480 | bytes 30736 | tf_op jit(solution)/shard_map/jit(_where)/select_n | solution.py:429
  2.3 0.0 copy-start.1
  2.4 1.0 %copy-done.1 = f32[2,4,64,256]{3,2,1,0:T(8,128)S(1)} copy-done((f32[2,4,64,256]{3,2,1,0:T(8,128)S(1)}, f32[2,4,64,256]{3,2,1,0:T(8,128)}, u32[]{:S(2)}) %copy-start.1) | copy-done | bytes 524312
  3.4 0.2 prepare.1
  3.5 3.1 %collective-permute-start = (bf16[2,208,256]{2,1,0:T(8,128)(2,1)S(1)}, bf16[2,208,256]{2,1,0:T(8,128)(2,1)S(1)}, u32[]{:S(2)}, u32[]{:S(2)}) collective-permute-start(bf16[2,208,256]{2,1,0:T(8,128)(2,1)S(1)} %get-tuple-element.27), channel_id=1, source_target_pairs={{0,1},{1,2},{2,3},{3,4},{4,5},{5,6},{6,7},{7,8},{8,9},{9,10},{10,1... | collective-permute-start | bytes 638984 | tf_op jit(solution)/shard_map/ppermute | solution.py:19
  6.7 10.9 %collective-permute-start.1 = (bf16[2,208,256]{2,1,0:T(8,128)(2,1)S(1)}, bf16[2,208,256]{2,1,0:T(8,128)(2,1)S(1)}, u32[]{:S(2)}, u32[]{:S(2)}) collective-permute-start(bf16[2,208,256]{2,1,0:T(8,128)(2,1)S(1)} %get-tuple-element.29), channel_id=1, source_target_pairs={{0,31},{1,0},{2,1},{3,2},{4,3},{5,4},{6,5},{7,6},{8,7},{9,8},{10,9... | collective-permute-start | bytes 638984 | tf_op jit(solution)/shard_map/ppermute | solution.py:19
  17.5 0.0 copy-done.5
  17.5 0.1 slice_select_fusion
  17.7 0.2 select_n.98
  18.0 4.9 %collective-permute-start.2 = (bf16[784,256]{1,0:T(8,128)(2,1)S(1)}, bf16[784,256]{1,0:T(8,128)(2,1)S(1)}, u32[]{:S(2)}, u32[]{:S(2)}) collective-permute-start(bf16[784,256]{1,0:T(8,128)(2,1)S(1)} %pad_maximum_fusion.3), channel_id=1, source_target_pairs={{32,64},{96,128},{160,192},{224,256},{288,320},{352,384},{416,448}... | collective-permute-start | bytes 1204232 | tf_op jit(solution)/shard_map/ppermute | solution.py:25
  22.8 0.0 collective-permute-done
  22.8 0.0 collective-permute-done.1
  22.9 0.1 fusion.8
  22.9 0.1 pad_maximum_fusion.6.refs_4_.refs_2_.refs_3_
  23.3 0.0 copy-start.3
  23.3 0.0 copy-start.4
  23.4 4.5 %collective-permute-start.3 = (bf16[656,256]{1,0:T(8,128)(2,1)S(1)}, bf16[656,256]{1,0:T(8,128)(2,1)S(1)}, u32[]{:S(2)}, u32[]{:S(2)}) collective-permute-start(bf16[656,256]{1,0:T(8,128)(2,1)S(1)} %fusion.1), channel_id=1, source_target_pairs={{32,64},{96,128},{160,192},{224,256},{288,320},{352,384},{416,448}... | collective-permute-start | bytes 1007624 | tf_op jit(solution)/shard_map/ppermute | solution.py:25
  27.8 2.2 %all-gather = bf16[4,256,256]{2,1,0:T(8,128)(2,1)S(1)} all-gather(bf16[2,256,256]{2,1,0:T(8,128)(2,1)S(1)} %get-tuple-element.32), channel_id=2, replica_groups={{0,32},{64,96},{128,160},{192,224},{256,288},{320,352},{384,416},{448,4..., dimensions={0}, use_global_device_ids=true | all-gather | bytes 786432 | tf_op jit(solution)/shard_map/all_gather | solution.py:456
  30.0 2.5 %all-gather.1 = bf16[1856,256]{1,0:T(8,128)(2,1)S(1)} all-gather(bf16[928,256]{1,0:T(8,128)(2,1)S(1)} %pad_maximum_fusion.2), channel_id=3, replica_groups={{0,32},{64,96},{128,160},{192,224},{256,288},{320,352},{384,416},{448,4..., dimensions={0}, use_global_device_ids=true | all-gather | bytes 1425408 | tf_op jit(solution)/shard_map/all_gather | solution.py:458
  32.5 0.0 collective-permute-done.2.refs_8_.refs_2_
  32.5 0.0 copy-done.3
  32.5 0.0 copy-done.4
  32.5 0.0 copy-start
  32.5 0.0 copy-start.2
  32.5 3.9 %middle_first.1 = (bf16[2,2,3,256,256]{4,3,2,1,0:T(8,128)(2,1)S(1)}, bf16[2,2,2,128,256]{4,3,2,1,0:T(8,128)(2,1)S(1)}, bf16[2,3,256,256]{3,2,1,0:T(8,128)(2,1)S(...) custom-call(s32[1]{0:T(128)} %bitcast.refs_0_, ...), custom_call_target="tpu_custom_call" | custom-call | flops 1000000 | bytes 100000 | tf_op jit(solution)/shard_map/middle_first/pallas_call | solution.py:343
  36.4 0.0 collective-permute-done.3.refs_3_
  36.4 0.0 copy-done
  36.5 0.0 copy-done.2
  36.5 1.6 %finish_first.1 = (f32[2,256,256]{2,1,0:T(8,128)S(1)}, bf16[2,256,256]{2,1,0:T(8,128)(2,1)S(1)}, bf16[2,3,256,256]{3,2,1,0:T(8,128)(2,1)S(1)}, bf16[2,128,256]{2,1,0:T(8,128)(2,1)S(1)}, bf16[16,384]{1,0:T(8,128)(2,1)S(1)}) custom-call(s32[1]{0:T(128)} %bitcast.refs_0_, bf16[2,512,256]{2,1,0:T(8,128)(2,1)S(1)} %pad_maximum_fusion.refs_2_.refs_1_, ...), custom_call_target="tpu_custom_call" | custom-call | flops 400000000 | bytes 5000000 | tf_op jit(solution)/shard_map/finish_first/pallas_call | solution.py:343
  38.1 1.9 %collective-permute-start.5 = (bf16[2,128,256]{2,1,0:T(8,128)(2,1)S(1)}, bf16[2,128,256]{2,1,0:T(8,128)(2,1)S(1)}, u32[]{:S(2)}, u32[]{:S(2)}) collective-permute-start(bf16[2,128,256]{2,1,0:T(8,128)(2,1)S(1)} %get-tuple-element.50), channel_id=1, source_target_pairs={{0,1},{1,2},{2,3},{3,4},{4,5},{5,6},{6,7},{7,8},{8,9},{9,10},{10,1... | collective-permute-start | bytes 393224 | tf_op jit(solution)/shard_map/ppermute | solution.py:19
  40.0 5.8 %collective-permute-start.6 = (bf16[2,128,256]{2,1,0:T(8,128)(2,1)S(1)}, bf16[2,128,256]{2,1,0:T(8,128)(2,1)S(1)}, u32[]{:S(2)}, u32[]{:S(2)}) collective-permute-start(bf16[2,128,256]{2,1,0:T(8,128)(2,1)S(1)} %get-tuple-element.49), channel_id=1, source_target_pairs={{0,31},{1,0},{2,1},{3,2},{4,3},{5,4},{6,5},{7,6},{8,7},{9,8},{10,9... | collective-permute-start | bytes 393224 | tf_op jit(solution)/shard_map/ppermute | solution.py:19
  45.8 5.2 %collective-permute-start.4 = (bf16[512,256]{1,0:T(8,128)(2,1)S(1)}, bf16[512,256]{1,0:T(8,128)(2,1)S(1)}, u32[]{:S(2)}, u32[]{:S(2)}) collective-permute-start(bf16[512,256]{1,0:T(8,128)(2,1)S(1)} %bitcast.27), channel_id=1, source_target_pairs={{32,64},{96,128},{160,192},{224,256},{288,320},{352,384},{416,448}... | collective-permute-start | bytes 786440 | tf_op jit(solution)/shard_map/ppermute | solution.py:25
  51.0 0.0 collective-permute-done.5
  51.1 0.0 collective-permute-done.6
  51.1 4.0 %collective-permute-start.7 = (bf16[512,256]{1,0:T(8,128)(2,1)S(1)}, bf16[512,256]{1,0:T(8,128)(2,1)S(1)}, u32[]{:S(2)}, u32[]{:S(2)}) collective-permute-start(bf16[512,256]{1,0:T(8,128)(2,1)S(1)} %bitcast.36), channel_id=1, source_target_pairs={{32,64},{96,128},{160,192},{224,256},{288,320},{352,384},{416,448}... | collective-permute-start | bytes 786440 | tf_op jit(solution)/shard_map/ppermute | solution.py:25
  55.1 2.2 %all-gather.2 = bf16[4,256,256]{2,1,0:T(8,128)(2,1)S(1)} all-gather(bf16[2,256,256]{2,1,0:T(8,128)(2,1)S(1)} %get-tuple-element.39), channel_id=4, replica_groups={{0,32},{64,96},{128,160},{192,224},{256,288},{320,352},{384,416},{448,4..., dimensions={0}, use_global_device_ids=true | all-gather | bytes 786432 | tf_op jit(solution)/shard_map/all_gather | solution.py:456
  57.3 2.2 %all_gather.27.refs_4_ = bf16[2,512,256]{2,1,0:T(8,128)(2,1)S(1)} all-gather(bf16[1,512,256]{2,1,0:T(8,128)(2,1)S(1)} %bitcast.37), channel_id=1, replica_groups={{0,32},{64,96},{128,160},{192,224},{256,288},{320,352},{384,416},{448,4..., dimensions={0}, use_global_device_ids=true | all-gather | bytes 786432 | tf_op jit(solution)/shard_map/all_gather | solution.py:458
  59.5 1.2 %middle_last.1 = (f32[2,384,256]{2,1,0:T(8,128)S(1)}, f32[2,256,256]{2,1,0:T(8,128)S(1)}) custom-call(s32[1]{0:T(128)} %bitcast.refs_0_, bf16[2,512,256]{2,1,0:T(8,128)(2,1)S(1)} %pad_maximum_fusion.1.refs_1_, bf16[2,16,384]{2,1,0:T(8,128)(2,1)S(1)} %pad_maximum_fusion.6.refs_4_.refs_2_.refs_3_, bf16[2,2,256,256]{3,2,1,0:T(8,128)(2,1)S(1)} %bitcast.33, ...), custom_call_target="tpu_custom_call" | custom-call | flops 1000000 | bytes 100000 | tf_op jit(solution)/shard_map/middle_last/pallas_call | solution.py:343
  60.7 0.0 collective-permute-done.4.refs_1_
  60.7 1.7 %collective-permute-done.7.refs_2_ = bf16[512,256]{1,0:T(8,128)(2,1)S(1)} collective-permute-done((bf16[512,256]{1,0:T(8,128)(2,1)S(1)}, bf16[512,256]{1,0:T(8,128)(2,1)S(1)}, u32[]{:S(2)}, u32[]{:S(2)}) %collective-permute-start.7) | collective-permute-done | bytes 262176 | tf_op jit(solution)/shard_map/ppermute | solution.py:25
  62.4 1.8 %finish_last.1 = f32[2,256,256]{2,1,0:T(8,128)} custom-call(s32[1]{0:T(128)} %bitcast.refs_0_, bf16[512,256]{1,0:T(8,128)(2,1)S(1)} %collective-permute-done.4.refs_1_, bf16[512,256]{1,0:T(8,128)(2,1)S(1)} %collective-permute-done.7.refs_2_, bf16[2,16,384]{2,1,0:T(8,128)(2,1)S(1)} %pad_maximum_fusion.6.refs_4_.refs_2_.refs_3_, ...), custom_call_target="tpu_custom_call" | custom-call | flops 400000000 | bytes 5000000 | tf_op jit(solution)/shard_map/finish_last/pallas_call | solution.py:343
  (23 shorter events, 0.4 us)
Async XLA Ops:
  0.0 17.5 %copy-start.5 = (bf16[2,4,64,4,64]{4,3,2,1,0:T(4,128)(2,1)S(1)}, bf16[2,4,64,4,64]{4,3,2,1,0:T(4,128)(2,1)}, u32[]{:S(2)}) copy-start(bf16[2,4,64,4,64]{4,3,2,1,0:T(4,128)(2,1)} %param.13) | copy-start | bytes 786436
  2.3 1.0 %copy-start.1 = (f32[2,4,64,256]{3,2,1,0:T(8,128)S(1)}, f32[2,4,64,256]{3,2,1,0:T(8,128)}, u32[]{:S(2)}) copy-start(f32[2,4,64,256]{3,2,1,0:T(8,128)} %param.9) | copy-start | bytes 1572868
  3.5 19.3 %collective-permute-start = (bf16[2,208,256]{2,1,0:T(8,128)(2,1)S(1)}, bf16[2,208,256]{2,1,0:T(8,128)(2,1)S(1)}, u32[]{:S(2)}, u32[]{:S(2)}) collective-permute-start(bf16[2,208,256]{2,1,0:T(8,128)(2,1)S(1)} %get-tuple-element.27), channel_id=1, source_target_pairs={{0,1},{1,2},{2,3},{3,4},{4,5},{5,6},{6,7},{7,8},{8,9},{9,10},{10,1... | collective-permute-start | bytes 638984 | tf_op jit(solution)/shard_map/ppermute | solution.py:19
  6.7 16.2 %collective-permute-start.1 = (bf16[2,208,256]{2,1,0:T(8,128)(2,1)S(1)}, bf16[2,208,256]{2,1,0:T(8,128)(2,1)S(1)}, u32[]{:S(2)}, u32[]{:S(2)}) collective-permute-start(bf16[2,208,256]{2,1,0:T(8,128)(2,1)S(1)} %get-tuple-element.29), channel_id=1, source_target_pairs={{0,31},{1,0},{2,1},{3,2},{4,3},{5,4},{6,5},{7,6},{8,7},{9,8},{10,9... | collective-permute-start | bytes 638984 | tf_op jit(solution)/shard_map/ppermute | solution.py:19
  18.0 14.6 %collective-permute-start.2 = (bf16[784,256]{1,0:T(8,128)(2,1)S(1)}, bf16[784,256]{1,0:T(8,128)(2,1)S(1)}, u32[]{:S(2)}, u32[]{:S(2)}) collective-permute-start(bf16[784,256]{1,0:T(8,128)(2,1)S(1)} %pad_maximum_fusion.3), channel_id=1, source_target_pairs={{32,64},{96,128},{160,192},{224,256},{288,320},{352,384},{416,448}... | collective-permute-start | bytes 1204232 | tf_op jit(solution)/shard_map/ppermute | solution.py:25
  23.3 9.2 %copy-start.3 = (bf16[2,4,9,64,64]{4,3,2,1,0:T(8,128)(2,1)S(1)}, bf16[2,4,9,64,64]{4,3,2,1,0:T(8,128)(2,1)}, u32[]{:S(2)}) copy-start(bf16[2,4,9,64,64]{4,3,2,1,0:T(8,128)(2,1)} %refs_7_.1) | copy-start | bytes 1769476
  23.3 9.2 %copy-start.4 = (s32[2,4,9]{2,1,0:T(4,128)S(1)}, s32[2,4,9]{2,1,0:T(4,128)}, u32[]{:S(2)}) copy-start(s32[2,4,9]{2,1,0:T(4,128)} %refs_1_.1) | copy-start | bytes 868
  23.4 13.1 %collective-permute-start.3 = (bf16[656,256]{1,0:T(8,128)(2,1)S(1)}, bf16[656,256]{1,0:T(8,128)(2,1)S(1)}, u32[]{:S(2)}, u32[]{:S(2)}) collective-permute-start(bf16[656,256]{1,0:T(8,128)(2,1)S(1)} %fusion.1), channel_id=1, source_target_pairs={{32,64},{96,128},{160,192},{224,256},{288,320},{352,384},{416,448}... | collective-permute-start | bytes 1007624 | tf_op jit(solution)/shard_map/ppermute | solution.py:25
  32.5 3.9 %copy-start = (bf16[2,2,4,64,256]{4,3,2,1,0:T(8,128)(2,1)S(1)}, bf16[2,2,4,64,256]{4,3,2,1,0:T(8,128)(2,1)}, u32[]{:S(2)}) copy-start(bf16[2,2,4,64,256]{4,3,2,1,0:T(8,128)(2,1)} %param.10) | copy-start | bytes 1572868
  32.5 3.9 %copy-start.2 = (f32[2,4,64,256]{3,2,1,0:T(8,128)S(1)}, f32[2,4,64,256]{3,2,1,0:T(8,128)}, u32[]{:S(2)}) copy-start(f32[2,4,64,256]{3,2,1,0:T(8,128)} %param.9) | copy-start | bytes 1572868
  38.1 13.0 %collective-permute-start.5 = (bf16[2,128,256]{2,1,0:T(8,128)(2,1)S(1)}, bf16[2,128,256]{2,1,0:T(8,128)(2,1)S(1)}, u32[]{:S(2)}, u32[]{:S(2)}) collective-permute-start(bf16[2,128,256]{2,1,0:T(8,128)(2,1)S(1)} %get-tuple-element.50), channel_id=1, source_target_pairs={{0,1},{1,2},{2,3},{3,4},{4,5},{5,6},{6,7},{7,8},{8,9},{9,10},{10,1... | collective-permute-start | bytes 393224 | tf_op jit(solution)/shard_map/ppermute | solution.py:19
  40.0 11.1 %collective-permute-start.6 = (bf16[2,128,256]{2,1,0:T(8,128)(2,1)S(1)}, bf16[2,128,256]{2,1,0:T(8,128)(2,1)S(1)}, u32[]{:S(2)}, u32[]{:S(2)}) collective-permute-start(bf16[2,128,256]{2,1,0:T(8,128)(2,1)S(1)} %get-tuple-element.49), channel_id=1, source_target_pairs={{0,31},{1,0},{2,1},{3,2},{4,3},{5,4},{6,5},{7,6},{8,7},{9,8},{10,9... | collective-permute-start | bytes 393224 | tf_op jit(solution)/shard_map/ppermute | solution.py:19
  45.8 14.9 %collective-permute-start.4 = (bf16[512,256]{1,0:T(8,128)(2,1)S(1)}, bf16[512,256]{1,0:T(8,128)(2,1)S(1)}, u32[]{:S(2)}, u32[]{:S(2)}) collective-permute-start(bf16[512,256]{1,0:T(8,128)(2,1)S(1)} %bitcast.27), channel_id=1, source_target_pairs={{32,64},{96,128},{160,192},{224,256},{288,320},{352,384},{416,448}... | collective-permute-start | bytes 786440 | tf_op jit(solution)/shard_map/ppermute | solution.py:25
  51.1 11.3 %collective-permute-start.7 = (bf16[512,256]{1,0:T(8,128)(2,1)S(1)}, bf16[512,256]{1,0:T(8,128)(2,1)S(1)}, u32[]{:S(2)}, u32[]{:S(2)}) collective-permute-start(bf16[512,256]{1,0:T(8,128)(2,1)S(1)} %bitcast.36), channel_id=1, source_target_pairs={{32,64},{96,128},{160,192},{224,256},{288,320},{352,384},{416,448}... | collective-permute-start | bytes 786440 | tf_op jit(solution)/shard_map/ppermute | solution.py:25
